TPU v7x, 512 devices: a whole 4x4x16 slice. The times are simulated.
512 devices in a mesh: freq: 16 (over y, x_hi, core), gx: 32 (over z, x_lo).
Axes of the slice: x: 4 (x_hi: 2, x_lo: 2; x = x_hi * 2 + x_lo), y: 4, z: 16, core: 2. Of those that a mesh axis runs over, the one named last changes fastest.
Arguments:
- sigma_h: float32 [128, 64, 256], P('gx'), may hold values from 0.3 to 3
- sigma_v: float32 [128, 64, 256], P('gx'), may hold values from 0.3 to 3
- wave_scale: float32 [16], P('freq'), may hold values from 0.25 to 4
- field_start: bfloat16 [16, 2, 3, 128, 64, 256], P('freq', None, None, 'gx'), may hold values from -6 to 6
- adjoint_start: bfloat16 [16, 2, 3, 128, 64, 256], P('freq', None, None, 'gx'), may hold values from -6 to 6
- observed: bfloat16 [16, 2, 3, 128, 64, 256], P('freq', None, None, 'gx'), may hold values from -6 to 6
- tx_count: int32 [1], replicated, may hold values from 1 to 64
- tx_cells: int32 [64], replicated, may hold values from 0 to 2097151
Outputs:
- gradient: float32 [2, 128, 64, 256], P(None, 'gx', 'freq')
- final_field: float32 [16, 2, 3, 128, 64, 256], P('freq', None, None, 'gx')
All inputs are finite; a program needn't handle non-finite values.
Results may differ from a plain program's by a relative error of at most 0.0003.
Values sent between devices are 32-bit elements; how exact they have to be, the bound alone decides.
No kernel may reach another device: no remote copies, remote signals or barrier semaphores. Data moves between devices by JAX's collectives and lax.ppermute only.
A program may use at most 64 MiB of HBM per device.

v0:
```python
import jax
import jax.numpy as jnp
from jax import lax
from jax.sharding import PartitionSpec as P

ITERS = 2


THETA = 0.5
SOURCE_GAIN = 8.0


def padded_2(cells, sides, width):
    for axis, dim in sides:
        count = lax.axis_size(axis)
        ends = count - 1
        head = lax.slice_in_dim(cells, 0, width, axis=dim)
        tail = lax.slice_in_dim(cells, cells.shape[dim] - width, cells.shape[dim], axis=dim)
        cells = jnp.concatenate(
            [
                lax.ppermute(tail, axis, [(i, (i + 1) % count) for i in range(ends)]),
                cells,
                lax.ppermute(head, axis, [((i + 1) % count, i) for i in range(ends)]),
            ],
            axis=dim,
        )
    return cells


def ahead_diff(values, along):
    along = values.ndim + along
    widths = [(0, 0)] * values.ndim
    widths[along] = (0, 1)
    padded = jnp.pad(values, widths)
    return lax.slice_in_dim(padded, 1, values.shape[along] + 1, axis=along) - values


def behind_diff(values, along):
    along = values.ndim + along
    widths = [(0, 0)] * values.ndim
    widths[along] = (1, 0)
    padded = jnp.pad(values, widths)
    return values - lax.slice_in_dim(padded, 0, values.shape[along], axis=along)


def curl_masked(efield, inside):
    comp_x = efield[..., 0, :, :, :]
    comp_y = efield[..., 1, :, :, :]
    comp_z = efield[..., 2, :, :, :]
    twist_x = (ahead_diff(comp_z, -2) - ahead_diff(comp_y, -1)) * inside
    twist_y = (ahead_diff(comp_x, -1) - ahead_diff(comp_z, -3)) * inside
    twist_z = (ahead_diff(comp_y, -3) - ahead_diff(comp_x, -2)) * inside
    back_x = behind_diff(twist_z, -2) - behind_diff(twist_y, -1)
    back_y = behind_diff(twist_x, -1) - behind_diff(twist_z, -3)
    back_z = behind_diff(twist_y, -3) - behind_diff(twist_x, -2)
    return jnp.stack([back_x, back_y, back_z], axis=-4)


def relax(efield, curled, source_term, sig_pair, wave_scale):
    sigma_comp = jnp.stack([sig_pair[0], sig_pair[0], sig_pair[1]])
    coupling = wave_scale[:, None, None, None, None] * sigma_comp[None]
    real_part = efield[:, 0]
    imag_part = efield[:, 1]
    resid_real = source_term[:, 0] - (curled[:, 0] - coupling * imag_part)
    resid_imag = source_term[:, 1] - (curled[:, 1] + coupling * real_part)
    modulus = 16.0 + coupling * coupling
    update_real = (4.0 * resid_real + coupling * resid_imag) / modulus
    update_imag = (4.0 * resid_imag - coupling * resid_real) / modulus
    return efield + THETA * jnp.stack([update_real, update_imag], axis=1)


def make_source(tx_cells, tx_count, wave_scale, x_start, slab_width, size_y, size_z):
    plane_size = size_y * size_z
    cell_x = tx_cells // plane_size - x_start
    remainder = tx_cells % plane_size
    cell_y = remainder // size_z
    cell_z = remainder % size_z
    active = (jnp.arange(tx_cells.shape[0]) < tx_count[0]) & (cell_x >= 0) & (cell_x < slab_width)
    weights = jnp.where(active, 1.0, 0.0).astype(jnp.float32)
    counts = jnp.zeros((slab_width, size_y, size_z), jnp.float32)
    counts = counts.at[jnp.clip(cell_x, 0, slab_width - 1), cell_y, cell_z].add(weights)
    imag_x = SOURCE_GAIN * wave_scale[:, None, None, None] * counts[None]
    blank = jnp.zeros_like(imag_x)
    real_block = jnp.stack([blank, blank, blank], axis=1)
    imag_block = jnp.stack([imag_x, blank, blank], axis=1)
    return jnp.stack([real_block, imag_block], axis=1)


def adjoint_source(efield, observed):
    differ = efield - observed.astype(jnp.float32)
    return jnp.stack([differ[:, 0], -differ[:, 1]], axis=1)


def gradient_terms(efield, adjoint, wave_scale):
    product = adjoint[:, 0] * efield[:, 1] + adjoint[:, 1] * efield[:, 0]
    weighted = wave_scale[:, None, None, None, None] * product
    horizontal = jnp.sum(weighted[:, 0] + weighted[:, 1], axis=0)
    vertical = jnp.sum(weighted[:, 2], axis=0)
    return jnp.stack([horizontal, vertical])


def inside_mask(first, width, total_x):
    positions = first + jnp.arange(width)
    return ((positions >= 0) & (positions < total_x)).astype(jnp.float32)[:, None, None]


def local_sweep(efield, source_term, sig_pair, wave_scale, inside_pad):
    padded = padded_2(efield, (("gx", 3),), 1)
    curled = curl_masked(padded, inside_pad)[:, :, :, 1:-1]
    return relax(efield, curled, source_term, sig_pair, wave_scale)


def on_device(
    sigma_h, sigma_v, wave_scale, field_start, adjoint_start, observed, tx_count, tx_cells
):
    slab_width = sigma_h.shape[0]
    size_y = sigma_h.shape[1]
    size_z = sigma_h.shape[2]
    slab_index = lax.axis_index("gx")
    total_x = slab_width * lax.axis_size("gx")
    slab_first = slab_index * slab_width
    sig_pair = jnp.stack([sigma_h, sigma_v])
    efield = field_start.astype(jnp.float32)
    adjoint = adjoint_start.astype(jnp.float32)
    inside_pad = inside_mask(slab_first - 1, slab_width + 2, total_x)
    source_term = make_source(
        tx_cells, tx_count, wave_scale, slab_first, slab_width, size_y, size_z
    )
    for sweep in range(ITERS):
        efield = local_sweep(efield, source_term, sig_pair, wave_scale, inside_pad)
    adjoint_rhs = adjoint_source(efield, observed)
    for sweep in range(ITERS):
        adjoint = local_sweep(adjoint, adjoint_rhs, sig_pair, wave_scale, inside_pad)
    local_grad = gradient_terms(efield, adjoint, wave_scale)
    summed = lax.psum(local_grad, "freq")
    share_rows = size_y // lax.axis_size("freq")
    gradient = lax.dynamic_slice_in_dim(summed, lax.axis_index("freq") * share_rows, share_rows, 2)
    return (gradient, efield)


def solution(mesh):
    placed = (
        P("gx", None, None),
        P("gx", None, None),
        P("freq"),
        P("freq", None, None, "gx", None, None),
        P("freq", None, None, "gx", None, None),
        P("freq", None, None, "gx", None, None),
        P(),
        P(),
    )
    return jax.shard_map(
        on_device,
        mesh=mesh,
        in_specs=placed,
        out_specs=(P(None, "gx", "freq", None), P("freq", None, None, "gx", None, None)),
        check_vma=False,
    )
```

profile of v0, /device:TPU:1, one launch (start us, length us, event | category | flops | bytes accessed | tf_op | source)
XLA Modules:
  0.0 269.4 jit_solution(7268834031824373260)
XLA Ops:
  7.2 1.2 fusion.149
  8.4 0.8 copy.50
  9.2 4.7 %collective-permute-start = (f32[1,2,3,1,64,256]{5,4,3,1,2,0:T(8,128)}, f32[1,2,3,1,64,256]{5,4,3,1,2,0:T(8,128)}, u32[]{:S(2)}, u32[]{:S(2)}) collective-permute-start(f32[1,2,3,1,64,256]{5,4,3,1,2,0:T(8,128)} %copy.50), channel_id=1, source_target_pairs={{0,1},{1,2},{2,3},{3,4},{4,5},{5,6},{6,7},{7,8},{8,9},{9,10},{10,1... | collective-permute-start | bytes 1179656 | tf_op jit(solution)/shard_map/ppermute | solution.py:21
  13.9 0.8 copy.51
  14.7 1.4 collective-permute-start.1
  16.3 1.0 fusion.147
  17.3 4.7 %collective-permute-start.4 = (f32[1,2,3,1,64,256]{5,4,3,1,2,0:T(8,128)}, f32[1,2,3,1,64,256]{5,4,3,1,2,0:T(8,128)}, u32[]{:S(2)}, u32[]{:S(2)}) collective-permute-start(f32[1,2,3,1,64,256]{5,4,3,1,2,0:T(8,128)} %get-tuple-element.30), channel_id=1, source_target_pairs={{0,1},{1,2},{2,3},{3,4},{4,5},{5,6},{6,7},{7,8},{8,9},{9,10},{10,1... | collective-permute-start | bytes 1179656 | tf_op jit(solution)/shard_map/ppermute | solution.py:21
  22.0 1.3 collective-permute-start.5
  24.0 1.3 convert_element_type.71
  26.0 4.6 %scatter_fusion = f32[4,64,256]{2,1,0:T(8,128)S(1)} fusion(f32[4,64,256]{2,1,0:T(8,128)S(1)} %broadcast_in_dim.16, s32[64]{0:T(128)S(1)} %fusion.137, f32[64]{0:T(128)S(1)} %get-tuple-element.14), kind=kCustom, calls=%fused_computation | custom fusion | flops 64 | bytes 1536 | tf_op jit(solution)/shard_map/scatter-add | solution.py:81
  30.7 1.0 constant_dynamic-update-slice_fusion.2
  31.9 1.0 constant_dynamic-update-slice_fusion
  33.1 0.6 fusion.6
  33.8 0.6 fusion.9
  34.3 0.4 copy-done.1
  34.8 0.6 copy-done.4
  35.3 0.4 divide_bitcast_fusion.3
  35.9 0.2 fusion
  36.3 4.0 %collective-permute-start.2 = (f32[1,2,3,1,64,256]{5,4,3,1,2,0:T(8,128)S(1)}, f32[1,2,3,1,64,256]{5,4,3,1,2,0:T(8,128)S(1)}, u32[]{:S(2)}, u32[]{:S(2)}) collective-permute-start(f32[1,2,3,1,64,256]{5,4,3,1,2,0:T(8,128)S(1)} %copy.52), channel_id=1, source_target_pairs={{0,1},{1,2},{2,3},{3,4},{4,5},{5,6},{6,7},{7,8},{8,9},{9,10},{10,1... | collective-permute-start | bytes 1179656 | tf_op jit(solution)/shard_map/ppermute | solution.py:21
  40.3 1.3 collective-permute-start.3
  41.6 3.1 %collective-permute-done.4 = f32[1,2,3,1,64,256]{5,4,3,1,2,0:T(8,128)} collective-permute-done((f32[1,2,3,1,64,256]{5,4,3,1,2,0:T(8,128)}, f32[1,2,3,1,64,256]{5,4,3,1,2,0:T(8,128)}, u32[]{:S(2)}, u32[]{:S(2)}) %collective-permute-start.4) | collective-permute-done | bytes 393248 | tf_op jit(solution)/shard_map/ppermute | solution.py:21
  44.7 1.4 pad_maximum_fusion
  46.1 0.3 slice_bitcast_fusion.4
  46.4 5.5 %collective-permute-done.2 = f32[1,2,3,1,64,256]{5,4,3,1,2,0:T(8,128)S(1)} collective-permute-done((f32[1,2,3,1,64,256]{5,4,3,1,2,0:T(8,128)S(1)}, f32[1,2,3,1,64,256]{5,4,3,1,2,0:T(8,128)S(1)}, u32[]{:S(2)}, u32[]{:S(2)}) %collective-permute-start.2) | collective-permute-done | bytes 393248 | tf_op jit(solution)/shard_map/ppermute | solution.py:21
  52.2 5.0 %collective-permute-done.3 = f32[1,2,3,1,64,256]{5,4,3,1,2,0:T(8,128)S(1)} collective-permute-done((f32[1,2,3,1,64,256]{5,4,3,1,2,0:T(8,128)S(1)}, f32[1,2,3,1,64,256]{5,4,3,1,2,0:T(8,128)S(1)}, u32[]{:S(2)}, u32[]{:S(2)}) %collective-permute-start.3) | collective-permute-done | bytes 393248 | tf_op jit(solution)/shard_map/ppermute | solution.py:23
  57.2 0.3 slice_bitcast_fusion.9
  57.4 1.4 fusion.30
  58.9 0.5 fusion.33
  59.4 0.5 fusion.21
  60.0 0.5 divide_bitcast_fusion.1
  60.6 0.9 copy-done.6
  61.6 0.5 copy_subtract_fusion
  62.1 0.5 fusion.102
  62.9 5.8 %collective-permute-start.6 = (f32[1,2,3,1,64,256]{5,4,3,1,2,0:T(8,128)S(1)}, f32[1,2,3,1,64,256]{5,4,3,1,2,0:T(8,128)S(1)}, u32[]{:S(2)}, u32[]{:S(2)}) collective-permute-start(f32[1,2,3,1,64,256]{5,4,3,1,2,0:T(8,128)S(1)} %get-tuple-element.29), channel_id=1, source_target_pairs={{0,1},{1,2},{2,3},{3,4},{4,5},{5,6},{6,7},{7,8},{8,9},{9,10},{10,1... | collective-permute-start | bytes 1179656 | tf_op jit(solution)/shard_map/ppermute | solution.py:21
  68.7 0.4 fusion.1
  69.1 1.5 collective-permute-start.7
  70.6 0.2 fusion.2
  70.8 2.6 collective-permute-done.6
  73.7 15.4 %collective-permute-done.7 = f32[1,2,3,1,64,256]{5,4,3,1,2,0:T(8,128)S(1)} collective-permute-done((f32[1,2,3,1,64,256]{5,4,3,1,2,0:T(8,128)S(1)}, f32[1,2,3,1,64,256]{5,4,3,1,2,0:T(8,128)S(1)}, u32[]{:S(2)}, u32[]{:S(2)}) %collective-permute-start.7) | collective-permute-done | bytes 393248 | tf_op jit(solution)/shard_map/ppermute | solution.py:23
  89.1 0.3 slice_bitcast_fusion.1
  89.4 0.6 fusion.42
  90.0 0.5 fusion.45
  90.6 0.5 add_divide_fusion
  91.3 0.4 fusion.3
  91.7 0.3 fusion.108
  92.1 0.8 pad_maximum_fusion.9
  92.9 168.2 %all-reduce.51.cloned.1.call-done = f32[2,4,64,256]{3,2,1,0:T(8,128)} async-done(((f32[2,4,64,256]{3,2,1,0:T(8,128)}), f32[2,4,64,256]{3,2,1,0:T(8,128)}) %all-reduce.51.cloned.1.call-update) | async-done | bytes 524304 | tf_op jit(solution)/shard_map/psum | solution.py:135
  261.1 1.5 constant_dynamic-slice_fusion
  (41 shorter events, 2.3 us)
Async XLA Ops:
  7.2 8.9 %copy-start.3 = (bf16[1,2,3,4,64,256]{5,4,3,2,1,0:T(8,128)(2,1)S(1)}, bf16[1,2,3,4,64,256]{5,4,3,2,1,0:T(8,128)(2,1)}, u32[]{:S(2)}) copy-start(bf16[1,2,3,4,64,256]{5,4,3,2,1,0:T(8,128)(2,1)} %param.12) | copy-start | bytes 2359300
  7.2 253.9 %all-reduce.51.cloned.1.call-start = ((), (), s32[]{:S(2)}) async-start(), calls=%async_computation | async-start | bytes 1048576 | tf_op jit(solution)/shard_map/psum | solution.py:135
  9.2 21.5 %collective-permute-start = (f32[1,2,3,1,64,256]{5,4,3,1,2,0:T(8,128)}, f32[1,2,3,1,64,256]{5,4,3,1,2,0:T(8,128)}, u32[]{:S(2)}, u32[]{:S(2)}) collective-permute-start(f32[1,2,3,1,64,256]{5,4,3,1,2,0:T(8,128)} %copy.50), channel_id=1, source_target_pairs={{0,1},{1,2},{2,3},{3,4},{4,5},{5,6},{6,7},{7,8},{8,9},{9,10},{10,1... | collective-permute-start | bytes 1179656 | tf_op jit(solution)/shard_map/ppermute | solution.py:21
  14.7 9.3 %copy-start.7 = (s32[64]{0:T(128)S(1)}, s32[64]{0:T(128)}, u32[]{:S(2)}) copy-start(s32[64]{0:T(128)} %param.15) | copy-start | bytes 772
  14.7 9.3 %copy-start = (bf16[1,2,3,4,64,256]{5,4,3,2,1,0:T(8,128)(2,1)S(1)}, bf16[1,2,3,4,64,256]{5,4,3,2,1,0:T(8,128)(2,1)}, u32[]{:S(2)}) copy-start(bf16[1,2,3,4,64,256]{5,4,3,2,1,0:T(8,128)(2,1)} %param.11) | copy-start | bytes 2359300
  14.7 17.2 %collective-permute-start.1 = (f32[1,2,3,1,64,256]{5,4,3,1,2,0:T(8,128)}, f32[1,2,3,1,64,256]{5,4,3,1,2,0:T(8,128)}, u32[]{:S(2)}, u32[]{:S(2)}) collective-permute-start(f32[1,2,3,1,64,256]{5,4,3,1,2,0:T(8,128)} %copy.51), channel_id=1, source_target_pairs={{1,0},{2,1},{3,2},{4,3},{5,4},{6,5},{7,6},{8,7},{9,8},{10,9},{11,1... | collective-permute-start | bytes 1179656 | tf_op jit(solution)/shard_map/ppermute | solution.py:23
  17.3 27.4 %collective-permute-start.4 = (f32[1,2,3,1,64,256]{5,4,3,1,2,0:T(8,128)}, f32[1,2,3,1,64,256]{5,4,3,1,2,0:T(8,128)}, u32[]{:S(2)}, u32[]{:S(2)}) collective-permute-start(f32[1,2,3,1,64,256]{5,4,3,1,2,0:T(8,128)} %get-tuple-element.30), channel_id=1, source_target_pairs={{0,1},{1,2},{2,3},{3,4},{4,5},{5,6},{6,7},{7,8},{8,9},{9,10},{10,1... | collective-permute-start | bytes 1179656 | tf_op jit(solution)/shard_map/ppermute | solution.py:21
  22.0 22.7 %collective-permute-start.5 = (f32[1,2,3,1,64,256]{5,4,3,1,2,0:T(8,128)}, f32[1,2,3,1,64,256]{5,4,3,1,2,0:T(8,128)}, u32[]{:S(2)}, u32[]{:S(2)}) collective-permute-start(f32[1,2,3,1,64,256]{5,4,3,1,2,0:T(8,128)} %get-tuple-element.31), channel_id=1, source_target_pairs={{1,0},{2,1},{3,2},{4,3},{5,4},{6,5},{7,6},{8,7},{9,8},{10,9},{11,1... | collective-permute-start | bytes 1179656 | tf_op jit(solution)/shard_map/ppermute | solution.py:23
  33.7 1.0 copy-start.1
  33.7 1.0 copy-start.2
  33.7 1.6 copy-start.4
  36.3 15.6 %collective-permute-start.2 = (f32[1,2,3,1,64,256]{5,4,3,1,2,0:T(8,128)S(1)}, f32[1,2,3,1,64,256]{5,4,3,1,2,0:T(8,128)S(1)}, u32[]{:S(2)}, u32[]{:S(2)}) collective-permute-start(f32[1,2,3,1,64,256]{5,4,3,1,2,0:T(8,128)S(1)} %copy.52), channel_id=1, source_target_pairs={{0,1},{1,2},{2,3},{3,4},{4,5},{5,6},{6,7},{7,8},{8,9},{9,10},{10,1... | collective-permute-start | bytes 1179656 | tf_op jit(solution)/shard_map/ppermute | solution.py:21
  40.3 16.9 %collective-permute-start.3 = (f32[1,2,3,1,64,256]{5,4,3,1,2,0:T(8,128)S(1)}, f32[1,2,3,1,64,256]{5,4,3,1,2,0:T(8,128)S(1)}, u32[]{:S(2)}, u32[]{:S(2)}) collective-permute-start(f32[1,2,3,1,64,256]{5,4,3,1,2,0:T(8,128)S(1)} %copy.53), channel_id=1, source_target_pairs={{1,0},{2,1},{3,2},{4,3},{5,4},{6,5},{7,6},{8,7},{9,8},{10,9},{11,1... | collective-permute-start | bytes 1179656 | tf_op jit(solution)/shard_map/ppermute | solution.py:23
  60.4 1.1 copy-start.6
  62.9 10.5 %collective-permute-start.6 = (f32[1,2,3,1,64,256]{5,4,3,1,2,0:T(8,128)S(1)}, f32[1,2,3,1,64,256]{5,4,3,1,2,0:T(8,128)S(1)}, u32[]{:S(2)}, u32[]{:S(2)}) collective-permute-start(f32[1,2,3,1,64,256]{5,4,3,1,2,0:T(8,128)S(1)} %get-tuple-element.29), channel_id=1, source_target_pairs={{0,1},{1,2},{2,3},{3,4},{4,5},{5,6},{6,7},{7,8},{8,9},{9,10},{10,1... | collective-permute-start | bytes 1179656 | tf_op jit(solution)/shard_map/ppermute | solution.py:21
  69.1 22.6 %copy-start.5 = (f32[1,2,3,4,64,256]{5,4,3,2,1,0:T(8,128)}, f32[1,2,3,4,64,256]{5,4,3,2,1,0:T(8,128)S(1)}, u32[]{:S(2)}) copy-start(f32[1,2,3,4,64,256]{5,4,3,2,1,0:T(8,128)S(1)} %fusion.1) | copy-start | bytes 4718596
  69.1 20.0 %collective-permute-start.7 = (f32[1,2,3,1,64,256]{5,4,3,1,2,0:T(8,128)S(1)}, f32[1,2,3,1,64,256]{5,4,3,1,2,0:T(8,128)S(1)}, u32[]{:S(2)}, u32[]{:S(2)}) collective-permute-start(f32[1,2,3,1,64,256]{5,4,3,1,2,0:T(8,128)S(1)} %get-tuple-element.28), channel_id=1, source_target_pairs={{1,0},{2,1},{3,2},{4,3},{5,4},{6,5},{7,6},{8,7},{9,8},{10,9},{11,1... | collective-permute-start | bytes 1179656 | tf_op jit(solution)/shard_map/ppermute | solution.py:23
Sparse Core Ops, SparseCore 0:
  93.0 168.0 all-reduce.50
where the time goes:
time: 270 us; the launch traced here: 269 us
  waiting for transfers between devices  200 us (74%)
  starting transfers between devices  24.8 us (9%)
  other arithmetic  18.7 us (7%)
  between operations  15.8 us (6%)
  local copies, waits for them, and re-layouts  10.3 us (4%)
    psum x1, waiting for transfers between devices, on_device(): summed = lax.psum(local_grad, 'freq')  168 us
    ppermute x4, waiting for transfers between devices, padded_2(): lax.ppermute(head, axis, [((i + 1) % count, i) for i in range(ends)])  20.4 us
    ppermute x4, starting transfers between devices, padded_2(): lax.ppermute(tail, axis, [(i, (i + 1) % count) for i in range(ends)])  19.3 us
    ppermute x4, waiting for transfers between devices, padded_2(): lax.ppermute(tail, axis, [(i, (i + 1) % count) for i in range(ends)])  11.2 us
    ppermute x4, starting transfers between devices, padded_2(): lax.ppermute(head, axis, [((i + 1) % count, i) for i in range(ends)])  5.46 us
  transfers between devices with their start and end apart: 9, of which 6 were waited for; matrix products, arithmetic and copies ran while one was open for 6% of the time, Pallas kernels for 0%

commit v1 on v0

--- a/solution.py
+++ b/solution.py
@@ -132,9 +132,12 @@
     for sweep in range(ITERS):
         adjoint = local_sweep(adjoint, adjoint_rhs, sig_pair, wave_scale, inside_pad)
     local_grad = gradient_terms(efield, adjoint, wave_scale)
-    summed = lax.psum(local_grad, "freq")
-    share_rows = size_y // lax.axis_size("freq")
-    gradient = lax.dynamic_slice_in_dim(summed, lax.axis_index("freq") * share_rows, share_rows, 2)
+    count = lax.axis_size("freq")
+    share_rows = size_y // count
+    blocks = local_grad.reshape(2, slab_width, count, share_rows, size_z)
+    blocks = jnp.moveaxis(blocks, 2, 0)
+    gathered = lax.all_to_all(blocks, "freq", 0, 0)
+    gradient = jnp.sum(gathered, axis=0)
     return (gradient, efield)
 
 

time: 270 us -> 116 us (0.43)
  the two profiles are of different devices: /device:TPU:1 before, /device:TPU:128 now
where the time goes in v1:
time: 116 us; the launch traced here: 115 us
  waiting for transfers between devices  33.2 us (29%)
  starting transfers between devices  32.1 us (28%)
  other arithmetic  19.3 us (17%)
  blocking collectives  19.2 us (17%)
  local copies, waits for them, and re-layouts  8.86 us (8%)
  between operations  2.43 us (2%)
    ppermute x4, waiting for transfers between devices, padded_2(): lax.ppermute(tail, axis, [(i, (i + 1) % count) for i in range(ends)])  24.3 us
    ppermute x4, starting transfers between devices, padded_2(): lax.ppermute(head, axis, [((i + 1) % count, i) for i in range(ends)])  21.3 us
    all_to_all x1, blocking collectives, on_device(): gathered = lax.all_to_all(blocks, 'freq', 0, 0)  19.2 us
    ppermute x4, starting transfers between devices, padded_2(): lax.ppermute(tail, axis, [(i, (i + 1) % count) for i in range(ends)])  10.8 us
    ppermute x4, waiting for transfers between devices, padded_2(): lax.ppermute(head, axis, [((i + 1) % count, i) for i in range(ends)])  8.82 us
    unnamed x23, local copies, waits for them, and re-layouts  4.64 us
    scatter-add x1, other arithmetic, make_source(): counts.at[jnp.clip(cell_x, 0, slab_width - 1), cell_y, cell_z].add(weights)  4.59 us
    mul x3, other arithmetic, curl_masked(): twist_z = (ahead_diff(comp_y, -3) - ahead_diff(comp_x, -2)) * inside  2.81 us
  transfers between devices with their start and end apart: 8, of which 6 were waited for; matrix products, arithmetic and copies ran while one was open for 13% of the time, Pallas kernels for 0%

profile of v1, /device:TPU:128, one launch (start us, length us, event | category | flops | bytes accessed | tf_op | source)
XLA Modules:
  0.0 115.1 jit_solution(11229316347454781291)
XLA Ops:
  0.6 1.2 %fusion.148 = (f32[1,2,3,1,64,256]{5,4,3,2,1,0:T(8,128)S(1)}, f32[1,2,3,1,64,256]{5,4,3,2,1,0:T(8,128)S(1)}) fusion(bf16[1,2,3,4,64,256]{5,4,3,2,1,0:T(8,128)(2,1)} %param.11), kind=kLoop, calls=%fused_computation.278 | loop fusion | bytes 1572864 | tf_op jit(solution)/shard_map/slice | solution.py:17
  1.8 0.8 copy.87
  2.6 3.4 %collective-permute-start = (f32[1,2,3,1,64,256]{5,4,3,1,2,0:T(8,128)}, f32[1,2,3,1,64,256]{5,4,3,1,2,0:T(8,128)}, u32[]{:S(2)}, u32[]{:S(2)}) collective-permute-start(f32[1,2,3,1,64,256]{5,4,3,1,2,0:T(8,128)} %copy.87), channel_id=1, source_target_pairs={{0,1},{1,2},{2,3},{3,4},{4,5},{5,6},{6,7},{7,8},{8,9},{9,10},{10,1... | collective-permute-start | bytes 1179656 | tf_op jit(solution)/shard_map/ppermute | solution.py:21
  6.0 0.8 copy.88
  6.8 4.7 %collective-permute-start.1 = (f32[1,2,3,1,64,256]{5,4,3,1,2,0:T(8,128)}, f32[1,2,3,1,64,256]{5,4,3,1,2,0:T(8,128)}, u32[]{:S(2)}, u32[]{:S(2)}) collective-permute-start(f32[1,2,3,1,64,256]{5,4,3,1,2,0:T(8,128)} %copy.88), channel_id=1, source_target_pairs={{1,0},{2,1},{3,2},{4,3},{5,4},{6,5},{7,6},{8,7},{9,8},{10,9},{11,1... | collective-permute-start | bytes 1179656 | tf_op jit(solution)/shard_map/ppermute | solution.py:23
  11.7 1.0 fusion.146
  12.7 1.9 %collective-permute-start.4 = (f32[1,2,3,1,64,256]{5,4,3,1,2,0:T(8,128)}, f32[1,2,3,1,64,256]{5,4,3,1,2,0:T(8,128)}, u32[]{:S(2)}, u32[]{:S(2)}) collective-permute-start(f32[1,2,3,1,64,256]{5,4,3,1,2,0:T(8,128)} %get-tuple-element.30), channel_id=1, source_target_pairs={{0,1},{1,2},{2,3},{3,4},{4,5},{5,6},{6,7},{7,8},{8,9},{9,10},{10,1... | collective-permute-start | bytes 1179656 | tf_op jit(solution)/shard_map/ppermute | solution.py:21
  14.6 6.0 %collective-permute-start.5 = (f32[1,2,3,1,64,256]{5,4,3,1,2,0:T(8,128)}, f32[1,2,3,1,64,256]{5,4,3,1,2,0:T(8,128)}, u32[]{:S(2)}, u32[]{:S(2)}) collective-permute-start(f32[1,2,3,1,64,256]{5,4,3,1,2,0:T(8,128)} %get-tuple-element.31), channel_id=1, source_target_pairs={{1,0},{2,1},{3,2},{4,3},{5,4},{6,5},{7,6},{8,7},{9,8},{10,9},{11,1... | collective-permute-start | bytes 1179656 | tf_op jit(solution)/shard_map/ppermute | solution.py:23
  21.3 1.3 %convert_element_type.71 = f32[1,2,3,4,64,256]{5,4,3,2,1,0:T(8,128)} convert(bf16[1,2,3,4,64,256]{5,4,3,2,1,0:T(8,128)(2,1)S(1)} %copy-done) | non-fusion elementwise | flops 393216 | bytes 2359296 | tf_op jit(solution)/shard_map/convert_element_type | solution.py:123
  23.3 4.6 %scatter_fusion = f32[4,64,256]{2,1,0:T(8,128)S(1)} fusion(f32[4,64,256]{2,1,0:T(8,128)S(1)} %broadcast_in_dim.16, s32[64]{0:T(128)S(1)} %fusion.136, f32[64]{0:T(128)S(1)} %get-tuple-element.14), kind=kCustom, calls=%fused_computation | custom fusion | flops 64 | bytes 1536 | tf_op jit(solution)/shard_map/scatter-add | solution.py:81
  28.0 4.7 %collective-permute-done = f32[1,2,3,1,64,256]{5,4,3,1,2,0:T(8,128)} collective-permute-done((f32[1,2,3,1,64,256]{5,4,3,1,2,0:T(8,128)}, f32[1,2,3,1,64,256]{5,4,3,1,2,0:T(8,128)}, u32[]{:S(2)}, u32[]{:S(2)}) %collective-permute-start) | collective-permute-done | bytes 393248 | tf_op jit(solution)/shard_map/ppermute | solution.py:21
  32.7 1.0 constant_dynamic-update-slice_fusion.2
  33.9 0.8 collective-permute-done.1
  34.7 1.0 constant_dynamic-update-slice_fusion
  35.9 0.6 fusion.6
  36.6 0.6 fusion.9
  37.1 0.4 copy-done.1
  37.6 0.6 copy-done.4
  38.1 0.4 divide_bitcast_fusion.3
  38.7 0.3 fusion
  39.1 3.6 %collective-permute-start.2 = (f32[1,2,3,1,64,256]{5,4,3,1,2,0:T(8,128)S(1)}, f32[1,2,3,1,64,256]{5,4,3,1,2,0:T(8,128)S(1)}, u32[]{:S(2)}, u32[]{:S(2)}) collective-permute-start(f32[1,2,3,1,64,256]{5,4,3,1,2,0:T(8,128)S(1)} %copy.89), channel_id=1, source_target_pairs={{0,1},{1,2},{2,3},{3,4},{4,5},{5,6},{6,7},{7,8},{8,9},{9,10},{10,1... | collective-permute-start | bytes 1179656 | tf_op jit(solution)/shard_map/ppermute | solution.py:21
  42.7 4.4 %collective-permute-start.3 = (f32[1,2,3,1,64,256]{5,4,3,1,2,0:T(8,128)S(1)}, f32[1,2,3,1,64,256]{5,4,3,1,2,0:T(8,128)S(1)}, u32[]{:S(2)}, u32[]{:S(2)}) collective-permute-start(f32[1,2,3,1,64,256]{5,4,3,1,2,0:T(8,128)S(1)} %copy.90), channel_id=1, source_target_pairs={{1,0},{2,1},{3,2},{4,3},{5,4},{6,5},{7,6},{8,7},{9,8},{10,9},{11,1... | collective-permute-start | bytes 1179656 | tf_op jit(solution)/shard_map/ppermute | solution.py:23
  47.1 1.4 %pad_maximum_fusion = f32[1,2,3,6,64,256]{5,4,3,1,2,0:T(8,128)S(1)} fusion(f32[1,2,3,1,64,256]{5,4,3,1,2,0:T(8,128)} %collective-permute-done.5, f32[1,2,3,4,64,256]{5,4,3,1,2,0:T(8,128)S(1)} %copy_convert_fusion, f32[1,2,3,1,64,256]{5,4,3,1,2,0:T(8,128)} %collective-permute-done.4), kind=kLoop, calls=%fused_computation.1 | loop fusion | flops 1179648 | bytes 4718592 | tf_op jit(solution)/shard_map/concatenate | solution.py:19
  48.5 0.3 slice_bitcast_fusion.4
  48.8 9.4 %collective-permute-done.2 = f32[1,2,3,1,64,256]{5,4,3,1,2,0:T(8,128)S(1)} collective-permute-done((f32[1,2,3,1,64,256]{5,4,3,1,2,0:T(8,128)S(1)}, f32[1,2,3,1,64,256]{5,4,3,1,2,0:T(8,128)S(1)}, u32[]{:S(2)}, u32[]{:S(2)}) %collective-permute-start.2) | collective-permute-done | bytes 393248 | tf_op jit(solution)/shard_map/ppermute | solution.py:21
  58.2 0.2 constant_dynamic-update-slice_fusion.4
  58.5 4.0 %collective-permute-done.3 = f32[1,2,3,1,64,256]{5,4,3,1,2,0:T(8,128)S(1)} collective-permute-done((f32[1,2,3,1,64,256]{5,4,3,1,2,0:T(8,128)S(1)}, f32[1,2,3,1,64,256]{5,4,3,1,2,0:T(8,128)S(1)}, u32[]{:S(2)}, u32[]{:S(2)}) %collective-permute-start.3) | collective-permute-done | bytes 393248 | tf_op jit(solution)/shard_map/ppermute | solution.py:23
  62.7 1.5 %fusion.30 = (f32[1,2,6,64,256]{4,3,2,1,0:T(8,128)S(1)}, f32[1,2,6,64,256]{4,3,2,1,0:T(8,128)S(1)}, f32[1,2,6,64,256]{4,3,2,1,0:T(8,128)S(1)}, f32[1,2,6,64,256]...) fusion(f32[1,2,6,64,256]{4,3,2,1,0:T(8,128)S(1)} %get-tuple-element.19, ...), kind=kLoop, calls=%fused_computation.89 | loop fusion | flops 4718592 | bytes 9437208 | tf_op jit(solution)/shard_map/mul | solution.py:52
  64.2 0.5 fusion.33
  64.7 0.5 fusion.21
  65.3 0.5 divide_bitcast_fusion.1
  66.0 0.9 copy-done.6
  66.9 0.5 copy_subtract_fusion
  67.5 0.5 fusion.102
  68.3 1.9 %collective-permute-start.6 = (f32[1,2,3,1,64,256]{5,4,3,1,2,0:T(8,128)S(1)}, f32[1,2,3,1,64,256]{5,4,3,1,2,0:T(8,128)S(1)}, u32[]{:S(2)}, u32[]{:S(2)}) collective-permute-start(f32[1,2,3,1,64,256]{5,4,3,1,2,0:T(8,128)S(1)} %get-tuple-element.29), channel_id=1, source_target_pairs={{0,1},{1,2},{2,3},{3,4},{4,5},{5,6},{6,7},{7,8},{8,9},{9,10},{10,1... | collective-permute-start | bytes 1179656 | tf_op jit(solution)/shard_map/ppermute | solution.py:21
  70.2 0.4 fusion.1
  70.7 6.2 %collective-permute-start.7 = (f32[1,2,3,1,64,256]{5,4,3,1,2,0:T(8,128)S(1)}, f32[1,2,3,1,64,256]{5,4,3,1,2,0:T(8,128)S(1)}, u32[]{:S(2)}, u32[]{:S(2)}) collective-permute-start(f32[1,2,3,1,64,256]{5,4,3,1,2,0:T(8,128)S(1)} %get-tuple-element.28), channel_id=1, source_target_pairs={{1,0},{2,1},{3,2},{4,3},{5,4},{6,5},{7,6},{8,7},{9,8},{10,9},{11,1... | collective-permute-start | bytes 1179656 | tf_op jit(solution)/shard_map/ppermute | solution.py:23
  76.9 0.3 fusion.2
  77.2 10.2 %collective-permute-done.6 = f32[1,2,3,1,64,256]{5,4,3,1,2,0:T(8,128)S(1)} collective-permute-done((f32[1,2,3,1,64,256]{5,4,3,1,2,0:T(8,128)S(1)}, f32[1,2,3,1,64,256]{5,4,3,1,2,0:T(8,128)S(1)}, u32[]{:S(2)}, u32[]{:S(2)}) %collective-permute-start.6) | collective-permute-done | bytes 393248 | tf_op jit(solution)/shard_map/ppermute | solution.py:21
  87.5 0.2 constant_dynamic-update-slice_fusion.7
  87.7 4.0 %collective-permute-done.7 = f32[1,2,3,1,64,256]{5,4,3,1,2,0:T(8,128)S(1)} collective-permute-done((f32[1,2,3,1,64,256]{5,4,3,1,2,0:T(8,128)S(1)}, f32[1,2,3,1,64,256]{5,4,3,1,2,0:T(8,128)S(1)}, u32[]{:S(2)}, u32[]{:S(2)}) %collective-permute-start.7) | collective-permute-done | bytes 393248 | tf_op jit(solution)/shard_map/ppermute | solution.py:23
  92.0 0.7 fusion.42
  92.7 0.5 fusion.45
  93.2 0.6 add_divide_fusion
  94.0 0.4 fusion.3
  94.5 0.3 fusion.108
  95.2 19.2 %all_to_all.5 = f32[16,2,4,4,256]{4,3,2,1,0:T(4,128)S(1)} all-to-all(f32[16,2,4,4,256]{4,3,2,1,0:T(4,128)S(1)} %copy_bitcast_fusion), channel_id=1, replica_groups=mesh['freq'=16,'gx'=32] {'freq'}, dimensions={0} | all-to-all | bytes 1048576 | tf_op jit(solution)/shard_map/all_to_all | solution.py:139
  114.4 0.7 reduce_sum.8
  (41 shorter events, 2.6 us)
Async XLA Ops:
  0.6 10.8 %copy-start.3 = (bf16[1,2,3,4,64,256]{5,4,3,2,1,0:T(8,128)(2,1)S(1)}, bf16[1,2,3,4,64,256]{5,4,3,2,1,0:T(8,128)(2,1)}, u32[]{:S(2)}) copy-start(bf16[1,2,3,4,64,256]{5,4,3,2,1,0:T(8,128)(2,1)} %param.12) | copy-start | bytes 2359300
  2.6 30.1 %collective-permute-start = (f32[1,2,3,1,64,256]{5,4,3,1,2,0:T(8,128)}, f32[1,2,3,1,64,256]{5,4,3,1,2,0:T(8,128)}, u32[]{:S(2)}, u32[]{:S(2)}) collective-permute-start(f32[1,2,3,1,64,256]{5,4,3,1,2,0:T(8,128)} %copy.87), channel_id=1, source_target_pairs={{0,1},{1,2},{2,3},{3,4},{4,5},{5,6},{6,7},{7,8},{8,9},{9,10},{10,1... | collective-permute-start | bytes 1179656 | tf_op jit(solution)/shard_map/ppermute | solution.py:21
  6.8 14.5 %copy-start.7 = (s32[64]{0:T(128)S(1)}, s32[64]{0:T(128)}, u32[]{:S(2)}) copy-start(s32[64]{0:T(128)} %param.15) | copy-start | bytes 772
  6.8 14.6 %copy-start = (bf16[1,2,3,4,64,256]{5,4,3,2,1,0:T(8,128)(2,1)S(1)}, bf16[1,2,3,4,64,256]{5,4,3,2,1,0:T(8,128)(2,1)}, u32[]{:S(2)}) copy-start(bf16[1,2,3,4,64,256]{5,4,3,2,1,0:T(8,128)(2,1)} %param.11) | copy-start | bytes 2359300
  6.8 27.9 %collective-permute-start.1 = (f32[1,2,3,1,64,256]{5,4,3,1,2,0:T(8,128)}, f32[1,2,3,1,64,256]{5,4,3,1,2,0:T(8,128)}, u32[]{:S(2)}, u32[]{:S(2)}) collective-permute-start(f32[1,2,3,1,64,256]{5,4,3,1,2,0:T(8,128)} %copy.88), channel_id=1, source_target_pairs={{1,0},{2,1},{3,2},{4,3},{5,4},{6,5},{7,6},{8,7},{9,8},{10,9},{11,1... | collective-permute-start | bytes 1179656 | tf_op jit(solution)/shard_map/ppermute | solution.py:23
  12.7 34.4 %collective-permute-start.4 = (f32[1,2,3,1,64,256]{5,4,3,1,2,0:T(8,128)}, f32[1,2,3,1,64,256]{5,4,3,1,2,0:T(8,128)}, u32[]{:S(2)}, u32[]{:S(2)}) collective-permute-start(f32[1,2,3,1,64,256]{5,4,3,1,2,0:T(8,128)} %get-tuple-element.30), channel_id=1, source_target_pairs={{0,1},{1,2},{2,3},{3,4},{4,5},{5,6},{6,7},{7,8},{8,9},{9,10},{10,1... | collective-permute-start | bytes 1179656 | tf_op jit(solution)/shard_map/ppermute | solution.py:21
  14.6 32.5 %collective-permute-start.5 = (f32[1,2,3,1,64,256]{5,4,3,1,2,0:T(8,128)}, f32[1,2,3,1,64,256]{5,4,3,1,2,0:T(8,128)}, u32[]{:S(2)}, u32[]{:S(2)}) collective-permute-start(f32[1,2,3,1,64,256]{5,4,3,1,2,0:T(8,128)} %get-tuple-element.31), channel_id=1, source_target_pairs={{1,0},{2,1},{3,2},{4,3},{5,4},{6,5},{7,6},{8,7},{9,8},{10,9},{11,1... | collective-permute-start | bytes 1179656 | tf_op jit(solution)/shard_map/ppermute | solution.py:23
  36.5 1.0 copy-start.1
  36.5 1.0 copy-start.2
  36.6 1.6 %copy-start.4 = (f32[1,2,3,4,64,256]{5,4,3,2,1,0:T(8,128)S(1)}, f32[1,2,3,4,64,256]{5,4,3,2,1,0:T(8,128)}, u32[]{:S(2)}) copy-start(f32[1,2,3,4,64,256]{5,4,3,2,1,0:T(8,128)} %convert_element_type.71) | copy-start | bytes 4718596
  39.1 19.1 %collective-permute-start.2 = (f32[1,2,3,1,64,256]{5,4,3,1,2,0:T(8,128)S(1)}, f32[1,2,3,1,64,256]{5,4,3,1,2,0:T(8,128)S(1)}, u32[]{:S(2)}, u32[]{:S(2)}) collective-permute-start(f32[1,2,3,1,64,256]{5,4,3,1,2,0:T(8,128)S(1)} %copy.89), channel_id=1, source_target_pairs={{0,1},{1,2},{2,3},{3,4},{4,5},{5,6},{6,7},{7,8},{8,9},{9,10},{10,1... | collective-permute-start | bytes 1179656 | tf_op jit(solution)/shard_map/ppermute | solution.py:21
  42.7 19.8 %collective-permute-start.3 = (f32[1,2,3,1,64,256]{5,4,3,1,2,0:T(8,128)S(1)}, f32[1,2,3,1,64,256]{5,4,3,1,2,0:T(8,128)S(1)}, u32[]{:S(2)}, u32[]{:S(2)}) collective-permute-start(f32[1,2,3,1,64,256]{5,4,3,1,2,0:T(8,128)S(1)} %copy.90), channel_id=1, source_target_pairs={{1,0},{2,1},{3,2},{4,3},{5,4},{6,5},{7,6},{8,7},{9,8},{10,9},{11,1... | collective-permute-start | bytes 1179656 | tf_op jit(solution)/shard_map/ppermute | solution.py:23
  65.8 1.1 copy-start.6
  68.3 19.1 %collective-permute-start.6 = (f32[1,2,3,1,64,256]{5,4,3,1,2,0:T(8,128)S(1)}, f32[1,2,3,1,64,256]{5,4,3,1,2,0:T(8,128)S(1)}, u32[]{:S(2)}, u32[]{:S(2)}) collective-permute-start(f32[1,2,3,1,64,256]{5,4,3,1,2,0:T(8,128)S(1)} %get-tuple-element.29), channel_id=1, source_target_pairs={{0,1},{1,2},{2,3},{3,4},{4,5},{5,6},{6,7},{7,8},{8,9},{9,10},{10,1... | collective-permute-start | bytes 1179656 | tf_op jit(solution)/shard_map/ppermute | solution.py:21
  70.7 23.8 %copy-start.5 = (f32[1,2,3,4,64,256]{5,4,3,2,1,0:T(8,128)}, f32[1,2,3,4,64,256]{5,4,3,2,1,0:T(8,128)S(1)}, u32[]{:S(2)}) copy-start(f32[1,2,3,4,64,256]{5,4,3,2,1,0:T(8,128)S(1)} %fusion.1) | copy-start | bytes 4718596
  70.7 21.0 %collective-permute-start.7 = (f32[1,2,3,1,64,256]{5,4,3,1,2,0:T(8,128)S(1)}, f32[1,2,3,1,64,256]{5,4,3,1,2,0:T(8,128)S(1)}, u32[]{:S(2)}, u32[]{:S(2)}) collective-permute-start(f32[1,2,3,1,64,256]{5,4,3,1,2,0:T(8,128)S(1)} %get-tuple-element.28), channel_id=1, source_target_pairs={{1,0},{2,1},{3,2},{4,3},{5,4},{6,5},{7,6},{8,7},{9,8},{10,9},{11,1... | collective-permute-start | bytes 1179656 | tf_op jit(solution)/shard_map/ppermute | solution.py:23

commit v2 on v0

v2 whole, which is shorter than its diff:
```python
import jax
import jax.numpy as jnp
from jax import lax
from jax.experimental import pallas as pl
from jax.experimental.pallas import tpu as pltpu
from jax.sharding import PartitionSpec as P

ITERS = 2
THETA = 0.5
SOURCE_GAIN = 8.0
ROWS = 8

VMEM = pl.BlockSpec(memory_space=pltpu.VMEM)
SMEM = pl.BlockSpec(memory_space=pltpu.SMEM)


def position(axis):
    index = lax.axis_index(axis)
    even = 1 - lax.rem(index, 2)
    return index, even


def side_layer(side, even, last):
    right = even if side == 0 else 1 - even
    return last * right, right.astype(jnp.float32)


def lane_of(shape):
    return lax.broadcasted_iota(jnp.int32, shape, len(shape) - 1)


def next_z(values):
    size = values.shape[-1]
    moved = pltpu.roll(values, size - 1, 1)
    return jnp.where(lane_of(values.shape) == size - 1, 0.0, moved)


def last_z(values):
    moved = pltpu.roll(values, 1, 1)
    return jnp.where(lane_of(values.shape) == 0, 0.0, moved)


def factors(sigma, wave):
    coupling = wave * sigma
    inverse = THETA / (16.0 + coupling * coupling)
    return coupling, 4.0 * inverse, coupling * inverse


def chunks(size_y):
    return [slice(y, y + ROWS) for y in range(0, size_y, ROWS)]


def behind_row(ref, index, y, size_y):
    now = ref[index + (slice(y, y + ROWS),)]
    if y == 0:
        row = lax.broadcasted_iota(jnp.int32, now.shape, 0)
        return now, jnp.where(row == 0, 0.0, pltpu.roll(now, 1, 0))
    return now, ref[index + (slice(y - 1, y - 1 + ROWS),)]


def ahead_row(ref, index, y, size_y):
    now = ref[index + (slice(y, y + ROWS),)]
    if y + ROWS == size_y:
        row = lax.broadcasted_iota(jnp.int32, now.shape, 0)
        return now, jnp.where(row == ROWS - 1, 0.0, pltpu.roll(now, ROWS - 1, 0))
    return now, ref[index + (slice(y + 1, y + 1 + ROWS),)]


def write_faces(face, out, right, size_y):
    for part in range(2):
        for y in range(0, size_y, ROWS):
            rows = slice(y, y + ROWS)
            ex, ex_next = ahead_row(face, (part, 0), y, size_y)
            out[part, 0, rows] = face[part, 1, rows] + right * (ex_next - ex)
            out[part, 1, rows] = face[part, 2, rows] + right * (next_z(ex) - ex)


def fix(halo, y, right, wave, sig_h, sig_v, size_y):
    _, h_four, h_coup = factors(sig_h, wave)
    _, v_four, v_coup = factors(sig_v, wave)
    extra = []
    for part in range(2):
        u, u_last = behind_row(halo, (part, 0), y, size_y)
        v = halo[part, 1, y : y + ROWS]
        extra.append((right * ((last_z(v) - v) - (u - u_last)), u, v))
    real, imag = [], []
    for comp in range(3):
        four, coup = (h_four, h_coup) if comp < 2 else (v_four, v_coup)
        real.append(four * extra[0][comp] + coup * extra[1][comp])
        imag.append(four * extra[1][comp] - coup * extra[0][comp])
    return real, imag


def twists(field, twist, edge, layers, size_y):
    def one(layer, carry):
        for part in range(2):
            for y in range(0, size_y, ROWS):
                rows = slice(y, y + ROWS)
                ex, ex_next = ahead_row(field, (layer, part, 0), y, size_y)
                ey = field[layer, part, 1, rows]
                ez, ez_next = ahead_row(field, (layer, part, 2), y, size_y)
                ey_right = field[layer + 1, part, 1, rows]
                ez_right = field[layer + 1, part, 2, rows]
                twist[layer + 1, part, 0, rows] = (ez_next - ez) - (next_z(ey) - ey)
                twist[layer + 1, part, 1, rows] = (next_z(ex) - ex) - (ez_right - ez)
                twist[layer + 1, part, 2, rows] = (ey_right - ey) - (ex_next - ex)
        return carry

    lax.fori_loop(0, layers, one, 0)
    for part in range(2):
        for rows in chunks(size_y):
            twist[0, part, 1, rows] = -edge * field[0, part, 2, rows]
            twist[0, part, 2, rows] = edge * field[0, part, 1, rows]


def curled(twist, layer, y, size_y):
    rows = slice(y, y + ROWS)
    result = []
    for part in range(2):
        hx, hx_last = behind_row(twist, (layer + 1, part, 0), y, size_y)
        hz, hz_last = behind_row(twist, (layer + 1, part, 2), y, size_y)
        hy = twist[layer + 1, part, 1, rows]
        hy_left = twist[layer, part, 1, rows]
        hz_left = twist[layer, part, 2, rows]
        result.append(
            (
                (hz - hz_last) - (hy - last_z(hy)),
                (hx - last_z(hx)) - (hz - hz_left),
                (hy - hy_left) - (hx - hx_last),
            )
        )
    return result


def relaxed(field, twist, layer, y, size_y, wave, sig_h, sig_v, source):
    rows = slice(y, y + ROWS)
    sides = (factors(sig_h, wave), factors(sig_v, wave))
    curl = curled(twist, layer, y, size_y)
    real, imag = [], []
    for comp in range(3):
        coupling, four, coup = sides[0] if comp < 2 else sides[1]
        er = field[layer, 0, comp, rows]
        ei = field[layer, 1, comp, rows]
        rr = coupling * ei - curl[0][comp]
        ri = -(coupling * er) - curl[1][comp]
        br, bi = source(0, comp), source(1, comp)
        if br is not None:
            rr = rr + br
        if bi is not None:
            ri = ri + bi
        real.append(er + (four * rr + coup * ri))
        imag.append(ei + (four * ri - coup * rr))
    return real, imag


def zero_layer(field, layer, size_y):
    for part in range(2):
        for comp in (1, 2):
            for rows in chunks(size_y):
                field[layer, part, comp, rows] = jnp.zeros((ROWS, field.shape[-1]), jnp.float32)


def widen(start, field, layers, size_y):
    for layer in range(layers):
        for part in range(2):
            for comp in range(3):
                field[layer, part, comp] = start[part, comp, layer].astype(jnp.float32)


def first_faces_kernel(start, adjoint, e_p, e_z, a_p, a_z, face):
    _, even = position("gx")
    layers, size_y = start.shape[2], start.shape[3]
    for values, outs in ((start, (e_p, e_z)), (adjoint, (a_p, a_z))):
        for side in range(2):
            layer, right = side_layer(side, even, layers - 1)
            for part in range(2):
                for comp in range(3):
                    face[part, comp] = values[part, comp, layer].astype(jnp.float32)
            write_faces(face, outs[side], right, size_y)


def first_sweep_kernel(
    wave_ref, count_ref, cells_ref, start, adjoint, sigma_h, sigma_v, e_out, a_out, src, field, twist
):
    index, _ = position("gx")
    layers, size_y, size_z = sigma_h.shape
    wave = wave_ref[0]
    edge = jnp.where(index > 0, 1.0, 0.0)
    src[...] = jnp.zeros_like(src)
    gain = SOURCE_GAIN * wave

    def slot(t, carry):
        cell = cells_ref[t]
        layer = cell // (size_y * size_z) - index * layers

        @pl.when((t < count_ref[0]) & (layer >= 0) & (layer < layers))
        def _():
            row = lax.rem(cell // size_z, size_y)
            spot = lane_of((1, size_z)) == lax.rem(cell, size_z)
            old = src[layer, pl.ds(row, 1), :]
            src[layer, pl.ds(row, 1), :] = old + jnp.where(spot, gain, 0.0)

        return carry

    lax.fori_loop(0, cells_ref.shape[0], slot, 0)

    zero_layer(field, layers, size_y)
    for values, out in ((start, e_out), (adjoint, a_out)):
        widen(values, field, layers, size_y)
        twists(field, twist, edge, layers, size_y)

        def one(layer, carry, out=out):
            for y in range(0, size_y, ROWS):
                rows = slice(y, y + ROWS)

                def source(part, comp):
                    return src[layer, rows] if out is e_out and part == 1 and comp == 0 else None

                new = relaxed(field, twist, layer, y, size_y, wave, sigma_h[layer, rows], sigma_v[layer, rows], source)
                for part in range(2):
                    for comp in range(3):
                        out[layer, part, comp, rows] = new[part][comp]
            return carry

        lax.fori_loop(0, layers, one, 0)


def second_faces_kernel(side, wave_ref, halo, part_new, sigma_h, sigma_v, face, send):
    _, even = position("gx")
    layers, size_y, _ = sigma_h.shape
    layer, right = side_layer(side, even, layers - 1)
    wave = wave_ref[0]
    for y in range(0, size_y, ROWS):
        rows = slice(y, y + ROWS)
        add = fix(halo, y, right, wave, sigma_h[layer, rows], sigma_v[layer, rows], size_y)
        for part in range(2):
            for comp in range(3):
                face[part, comp, rows] = part_new[layer, part, comp, rows] + add[part][comp]
    write_faces(face, send, right, size_y)


def gather_layers(body, face_p, face_z, field, even, layers):
    p_layer, _ = side_layer(0, even, layers - 1)
    z_layer, _ = side_layer(1, even, layers - 1)
    for part in range(2):
        for comp in range(3):
            for layer in range(1, layers - 1):
                field[layer, part, comp] = body[layer, part, comp]
            field[p_layer, part, comp] = face_p[part, comp]
            field[z_layer, part, comp] = face_z[part, comp]


def rhs_of(part, new, seen):
    return new - seen if part == 0 else seen - new


def second_sweep_kernel(
    wave_ref, e_body, e_p, e_z, a_part, src, observed, sigma_h, sigma_v, e_out, a_out, field, twist
):
    index, even = position("gx")
    layers, size_y, _ = sigma_h.shape
    wave = wave_ref[0]
    edge = jnp.where(index > 0, 1.0, 0.0)
    zero_layer(field, layers, size_y)
    gather_layers(e_body, e_p, e_z, field, even, layers)
    twists(field, twist, edge, layers, size_y)

    def one(layer, carry):
        for y in range(0, size_y, ROWS):
            rows = slice(y, y + ROWS)

            def source(part, comp):
                return src[layer, rows] if part == 1 and comp == 0 else None

            new = relaxed(field, twist, layer, y, size_y, wave, sigma_h[layer, rows], sigma_v[layer, rows], source)
            for part in range(2):
                for comp in range(3):
                    e_out[layer, part, comp, rows] = new[part][comp]
        return carry

    lax.fori_loop(0, layers, one, 0)

    def inner(layer, carry):
        add_rhs(layer, e_out, (layer,), a_part, observed, wave, sigma_h, sigma_v, a_out, (layer,), size_y, None)
        return carry

    lax.fori_loop(1, layers - 1, inner, 0)


def add_rhs(layer, new, at, a_part, observed, wave, sigma_h, sigma_v, a_out, out_at, size_y, extra):
    for y in range(0, size_y, ROWS):
        rows = slice(y, y + ROWS)
        sides = (factors(sigma_h[layer, rows], wave), factors(sigma_v[layer, rows], wave))
        add = extra(y) if extra is not None else None
        for comp in range(3):
            _, four, coup = sides[0] if comp < 2 else sides[1]
            br = rhs_of(0, new[at + (0, comp, rows)], observed[0, comp, layer, rows].astype(jnp.float32))
            bi = rhs_of(1, new[at + (1, comp, rows)], observed[1, comp, layer, rows].astype(jnp.float32))
            real = a_part[layer, 0, comp, rows] + (four * br + coup * bi)
            imag = a_part[layer, 1, comp, rows] + (four * bi - coup * br)
            if add is not None:
                real = real + add[0][comp]
                imag = imag + add[1][comp]
            a_out[out_at + (0, comp, rows)] = real
            a_out[out_at + (1, comp, rows)] = imag


def third_faces_kernel(
    side, wave_ref, e_halo, a_halo, e_part, a_part, observed, sigma_h, sigma_v, e_face, a_face, send
):
    _, even = position("gx")
    layers, size_y, _ = sigma_h.shape
    layer, right = side_layer(side, even, layers - 1)
    wave = wave_ref[0]
    for y in range(0, size_y, ROWS):
        rows = slice(y, y + ROWS)
        add = fix(e_halo, y, right, wave, sigma_h[layer, rows], sigma_v[layer, rows], size_y)
        for part in range(2):
            for comp in range(3):
                e_face[part, comp, rows] = e_part[layer, part, comp, rows] + add[part][comp]

    def extra(y):
        rows = slice(y, y + ROWS)
        return fix(a_halo, y, right, wave, sigma_h[layer, rows], sigma_v[layer, rows], size_y)

    add_rhs(layer, e_face, (), a_part, observed, wave, sigma_h, sigma_v, a_face, (), size_y, extra)
    write_faces(a_face, send, right, size_y)


def grad_rows(wave, field, adjoint):
    terms = [adjoint[0][comp] * field[1][comp] + adjoint[1][comp] * field[0][comp] for comp in range(3)]
    return wave * (terms[0] + terms[1]), wave * terms[2]


def put_rows(out, layers, layer, y, pair, share):
    for which in range(2):
        for k in range(ROWS // share):
            out[y // share + k, which, layer] = pair[which][k * share : (k + 1) * share]


def last_sweep_kernel(
    wave_ref, e_body, e_p, e_z, a_body, a_p, a_z, observed, sigma_h, sigma_v, final, faces, grad, field, twist
):
    index, even = position("gx")
    layers, size_y, _ = sigma_h.shape
    share = grad.shape[3]
    wave = wave_ref[0]
    edge = jnp.where(index > 0, 1.0, 0.0)
    sides = [side_layer(side, even, layers - 1)[0] for side in range(2)]
    for part in range(2):
        for comp in range(3):
            for layer in range(1, layers - 1):
                final[part, comp, layer] = e_body[layer, part, comp]
            final[part, comp, sides[0]] = e_p[part, comp]
            final[part, comp, sides[1]] = e_z[part, comp]
    zero_layer(field, layers, size_y)
    gather_layers(a_body, a_p, a_z, field, even, layers)
    twists(field, twist, edge, layers, size_y)

    def sweep(layer, y):
        rows = slice(y, y + ROWS)
        now = [[final[part, comp, layer, rows] for comp in range(3)] for part in range(2)]

        def source(part, comp):
            return rhs_of(part, now[part][comp], observed[part, comp, layer, rows].astype(jnp.float32))

        return now, relaxed(field, twist, layer, y, size_y, wave, sigma_h[layer, rows], sigma_v[layer, rows], source)

    def inner(layer, carry):
        for y in range(0, size_y, ROWS):
            now, new = sweep(layer, y)
            put_rows(grad, layers, layer, y, grad_rows(wave, now, new), share)
        return carry

    lax.fori_loop(1, layers - 1, inner, 0)

    def outer(side, carry):
        layer = jnp.where(side == 0, sides[0], sides[1])
        for y in range(0, size_y, ROWS):
            _, new = sweep(layer, y)
            for part in range(2):
                for comp in range(3):
                    faces[side, part, comp, y : y + ROWS] = new[part][comp]
        return carry

    lax.fori_loop(0, 2, outer, 0)


def gradient_kernel(wave_ref, halo_p, halo_z, e_p, e_z, faces, inner, sigma_h, sigma_v, grad):
    _, even = position("gx")
    layers, size_y, _ = sigma_h.shape
    share = grad.shape[3]
    wave = wave_ref[0]
    for layer in range(1, layers - 1):
        for which in range(2):
            grad[:, which, layer] = inner[:, which, layer]
    for side, (halo, now) in enumerate(((halo_p, e_p), (halo_z, e_z))):
        layer, right = side_layer(side, even, layers - 1)
        for y in range(0, size_y, ROWS):
            rows = slice(y, y + ROWS)
            add = fix(halo, y, right, wave, sigma_h[layer, rows], sigma_v[layer, rows], size_y)
            new = [[faces[side, part, comp, rows] + add[part][comp] for comp in range(3)] for part in range(2)]
            old = [[now[part, comp, rows] for comp in range(3)] for part in range(2)]
            put_rows(grad, layers, layer, y, grad_rows(wave, old, new), share)


def call(kernel, name, n_smem, n_vmem, outs, scratch=()):
    return pl.pallas_call(
        kernel,
        name=name,
        out_shape=tuple(jax.ShapeDtypeStruct(shape, jnp.float32) for shape in outs),
        in_specs=[SMEM] * n_smem + [VMEM] * n_vmem,
        out_specs=tuple(VMEM for _ in outs),
        scratch_shapes=[pltpu.VMEM(shape, jnp.float32) for shape in scratch],
        compiler_params=pltpu.CompilerParams(vmem_limit_bytes=24 << 20),
    )


def on_device(
    sigma_h, sigma_v, wave_scale, field_start, adjoint_start, observed, tx_count, tx_cells
):
    layers, size_y, size_z = sigma_h.shape
    slabs = lax.axis_size("gx")
    freqs = lax.axis_size("freq")
    share = size_y // freqs
    start = field_start[0]
    adjoint = adjoint_start[0]
    seen = observed[0]

    ends = (
        [(i, i + 1) for i in range(0, slabs - 1, 2)],
        [(i, i + 1) for i in range(1, slabs - 1, 2)],
    )
    swaps = [pairs + [(b, a) for a, b in pairs] for pairs in ends]

    def swap(values, side):
        return lax.ppermute(values, "gx", swaps[side])

    plane = (size_y, size_z)
    half = (2, 2) + plane
    face = (2, 3) + plane
    body = (layers,) + face
    more = (layers + 1,) + face

    e_p, e_z, a_p, a_z = call(first_faces_kernel, "first_faces", 0, 2, [half] * 4, [face])(start, adjoint)
    e_p_in, e_z_in = swap(e_p, 0), swap(e_z, 1)
    e1, a1, src = call(
        first_sweep_kernel, "first_sweep", 3, 4, [body, body, (layers,) + plane], [more, more]
    )(wave_scale, tx_count, tx_cells, start, adjoint, sigma_h, sigma_v)
    e1, e_p_in = lax.optimization_barrier((e1, e_p_in))

    def second(side, halo):
        return call(
            lambda *refs: second_faces_kernel(side, *refs), "second_faces_%d" % side, 1, 4, [face, half]
        )(wave_scale, halo, e1, sigma_h, sigma_v)

    e1_p, e1_p_out = second(0, e_p_in)
    a_p, e1_p_out = lax.optimization_barrier((a_p, e1_p_out))
    e1_p_in = swap(e1_p_out, 0)
    a_p_in = swap(a_p, 0)
    e1_z, e1_z_out = second(1, e_z_in)
    a_z, e1_z_out = lax.optimization_barrier((a_z, e1_z_out))
    e1_z_in = swap(e1_z_out, 1)
    a_z_in = swap(a_z, 1)
    e2, a1_body = call(second_sweep_kernel, "second_sweep", 1, 8, [body, body], [more, more])(
        wave_scale, e1, e1_p, e1_z, a1, src, seen, sigma_h, sigma_v
    )
    e2, e1_p_in = lax.optimization_barrier((e2, e1_p_in))

    def third(side, e_halo, a_halo):
        return call(
            lambda *refs: third_faces_kernel(side, *refs), "third_faces_%d" % side, 1, 7, [face, face, half]
        )(wave_scale, e_halo, a_halo, e2, a1, seen, sigma_h, sigma_v)

    e2_p, a1_p, a1_p_out = third(0, e1_p_in, a_p_in)
    a1_p_in = swap(a1_p_out, 0)
    e2_z, a1_z, a1_z_out = third(1, e1_z_in, a_z_in)
    a1_z_in = swap(a1_z_out, 1)
    blocks = (freqs, 2, layers, share, size_z)
    final, faces, inner = call(
        last_sweep_kernel,
        "last_sweep",
        1,
        9,
        [(2, 3, layers) + plane, (2,) + face, blocks],
        [more, more],
    )(wave_scale, e2, e2_p, e2_z, a1_body, a1_p, a1_z, seen, sigma_h, sigma_v)
    faces, a1_p_in = lax.optimization_barrier((faces, a1_p_in))
    (terms,) = call(gradient_kernel, "gradient", 1, 8, [blocks])(
        wave_scale, a1_p_in, a1_z_in, e2_p, e2_z, faces, inner, sigma_h, sigma_v
    )
    gathered = lax.all_to_all(terms, "freq", 0, 0)
    return (jnp.sum(gathered, axis=0), final[None])


def solution(mesh):
    placed = (
        P("gx", None, None),
        P("gx", None, None),
        P("freq"),
        P("freq", None, None, "gx", None, None),
        P("freq", None, None, "gx", None, None),
        P("freq", None, None, "gx", None, None),
        P(),
        P(),
    )
    return jax.shard_map(
        on_device,
        mesh=mesh,
        in_specs=placed,
        out_specs=(P(None, "gx", "freq", None), P("freq", None, None, "gx", None, None)),
        check_vma=False,
    )
```

time: 270 us -> 80.2 us (0.30)
  the two profiles are of different devices: /device:TPU:1 before, /device:TPU:384 now
where the time goes in v2:
time: 80.2 us; the launch traced here: 79.8 us
  starting transfers between devices  29.2 us (36%)
  blocking collectives  18.9 us (24%)
  waiting for transfers between devices  15.3 us (19%)
  Pallas kernels  11.3 us (14%)
  local copies, waits for them, and re-layouts  2.33 us (3%)
  between operations  2.12 us (3%)
    ppermute x8, starting transfers between devices, swap(): return lax.ppermute(values, 'gx', swaps[side])  29.2 us
    all_to_all x1, blocking collectives, on_device(): gathered = lax.all_to_all(terms, 'freq', 0, 0)  18.9 us
    ppermute x8, waiting for transfers between devices, swap(): return lax.ppermute(values, 'gx', swaps[side])  15.3 us
    pallas_call x1, Pallas kernels, on_device(): call(first_sweep_kernel, 'first_sweep', 3, 4, [body, body, (layers,) + pl...  4.86 us
    pallas_call x1, Pallas kernels, on_device(): call(last_sweep_kernel, 'last_sweep', 1, 9, [(2, 3, layers) + plane, (2,)...  2.72 us
    unnamed x12, local copies, waits for them, and re-layouts  2.33 us
    pallas_call x1, Pallas kernels, on_device(): call(second_sweep_kernel, 'second_sweep', 1, 8, [body, body], [more, more])  1.71 us
  transfers between devices with their start and end apart: 8, of which 5 were waited for; matrix products, arithmetic and copies ran while one was open for 0% of the time, Pallas kernels for 13%

profile of v2, /device:TPU:384, one launch (start us, length us, event | category | flops | bytes accessed | tf_op | source)
XLA Modules:
  0.0 79.8 jit_solution(17269315472559150559)
XLA Ops:
  0.6 0.0 copy-start.1
  0.6 0.0 copy-start
  0.7 0.0 copy-start.3
  0.7 1.2 %copy-done.3 = bf16[1,2,3,4,64,256]{5,4,3,2,1,0:T(8,128)(2,1)S(1)} copy-done((bf16[1,2,3,4,64,256]{5,4,3,2,1,0:T(8,128)(2,1)S(1)}, bf16[1,2,3,4,64,256]{5,4,3,2,1,0:T(8,128)(2,1)}, u32[]{:S(2)}) %copy-start.3) | copy-done | bytes 786456
  1.8 0.0 copy-start.4
  1.8 1.1 %copy-done.4 = bf16[1,2,3,4,64,256]{5,4,3,2,1,0:T(8,128)(2,1)S(1)} copy-done((bf16[1,2,3,4,64,256]{5,4,3,2,1,0:T(8,128)(2,1)S(1)}, bf16[1,2,3,4,64,256]{5,4,3,2,1,0:T(8,128)(2,1)}, u32[]{:S(2)}) %copy-start.4) | copy-done | bytes 786456
  3.0 0.0 copy-start.5
  3.0 0.3 first_faces.1
  3.3 3.4 %collective-permute-start = (f32[2,2,64,256]{3,2,1,0:T(8,128)S(1)}, f32[2,2,64,256]{3,2,1,0:T(8,128)S(1)}, u32[]{:S(2)}, u32[]{:S(2)}) collective-permute-start(f32[2,2,64,256]{3,2,1,0:T(8,128)S(1)} %get-tuple-element.35), channel_id=1, source_target_pairs={{0,1},{2,3},{4,5},{6,7},{8,9},{10,11},{12,13},{14,15},{16,17},{18,... | collective-permute-start | bytes 786440 | tf_op jit(solution)/shard_map/ppermute | solution.py:437
  6.7 4.1 %collective-permute-start.1 = (f32[2,2,64,256]{3,2,1,0:T(8,128)S(1)}, f32[2,2,64,256]{3,2,1,0:T(8,128)S(1)}, u32[]{:S(2)}, u32[]{:S(2)}) collective-permute-start(f32[2,2,64,256]{3,2,1,0:T(8,128)S(1)} %get-tuple-element.39), channel_id=1, source_target_pairs={{1,2},{3,4},{5,6},{7,8},{9,10},{11,12},{13,14},{15,16},{17,18},{19... | collective-permute-start | bytes 786440 | tf_op jit(solution)/shard_map/ppermute | solution.py:437
  12.1 0.0 copy-done.1
  12.1 0.0 copy-done
  12.1 0.0 copy-done.5
  12.1 4.9 %first_sweep.1 = (f32[4,2,3,64,256]{4,3,2,1,0:T(8,128)S(1)}, f32[4,2,3,64,256]{4,3,2,1,0:T(8,128)S(1)}, f32[4,64,256]{2,1,0:T(8,128)S(1)}) custom-call(f32[1]{0:T(128)S(6)} %copy.10.wave_ref.refs_0_, s32[1]{0:T(128)S(6)} %copy.11.count_ref, s32[64]{0:T(128)S(1)} %copy-done.5, bf16[2,3,4,64,256]{4,3,2,1,0:T(8,128)(2,1)S(1)} %bitcast.9, ...), custom_call_target="tpu_custom_call" | custom-call | tf_op jit(solution)/shard_map/first_sweep/pallas_call | solution.py:447
  17.0 1.9 %collective-permute-done.refs_1_ = f32[2,2,64,256]{3,2,1,0:T(8,128)S(1)} collective-permute-done((f32[2,2,64,256]{3,2,1,0:T(8,128)S(1)}, f32[2,2,64,256]{3,2,1,0:T(8,128)S(1)}, u32[]{:S(2)}, u32[]{:S(2)}) %collective-permute-start) | collective-permute-done | bytes 262176 | tf_op jit(solution)/shard_map/ppermute | solution.py:437
  18.9 0.2 second_faces_0.1
  19.1 0.0 copy-start.2
  19.1 3.5 %collective-permute-start.2 = (f32[2,2,64,256]{3,2,1,0:T(8,128)S(1)}, f32[2,2,64,256]{3,2,1,0:T(8,128)S(1)}, u32[]{:S(2)}, u32[]{:S(2)}) collective-permute-start(f32[2,2,64,256]{3,2,1,0:T(8,128)S(1)} %get-tuple-element.46), channel_id=1, source_target_pairs={{0,1},{2,3},{4,5},{6,7},{8,9},{10,11},{12,13},{14,15},{16,17},{18,... | collective-permute-start | bytes 786440 | tf_op jit(solution)/shard_map/ppermute | solution.py:437
  22.7 2.4 %collective-permute-start.3 = (f32[2,2,64,256]{3,2,1,0:T(8,128)S(1)}, f32[2,2,64,256]{3,2,1,0:T(8,128)S(1)}, u32[]{:S(2)}, u32[]{:S(2)}) collective-permute-start(f32[2,2,64,256]{3,2,1,0:T(8,128)S(1)} %get-tuple-element.49), channel_id=1, source_target_pairs={{0,1},{2,3},{4,5},{6,7},{8,9},{10,11},{12,13},{14,15},{16,17},{18,... | collective-permute-start | bytes 786440 | tf_op jit(solution)/shard_map/ppermute | solution.py:437
  25.1 0.0 collective-permute-done.1.refs_1_
  25.1 0.2 second_faces_1.1
  25.4 5.1 %collective-permute-start.4 = (f32[2,2,64,256]{3,2,1,0:T(8,128)S(1)}, f32[2,2,64,256]{3,2,1,0:T(8,128)S(1)}, u32[]{:S(2)}, u32[]{:S(2)}) collective-permute-start(f32[2,2,64,256]{3,2,1,0:T(8,128)S(1)} %get-tuple-element.53), channel_id=1, source_target_pairs={{1,2},{3,4},{5,6},{7,8},{9,10},{11,12},{13,14},{15,16},{17,18},{19... | collective-permute-start | bytes 786440 | tf_op jit(solution)/shard_map/ppermute | solution.py:437
  30.4 2.9 %collective-permute-start.5 = (f32[2,2,64,256]{3,2,1,0:T(8,128)S(1)}, f32[2,2,64,256]{3,2,1,0:T(8,128)S(1)}, u32[]{:S(2)}, u32[]{:S(2)}) collective-permute-start(f32[2,2,64,256]{3,2,1,0:T(8,128)S(1)} %get-tuple-element.54), channel_id=1, source_target_pairs={{1,2},{3,4},{5,6},{7,8},{9,10},{11,12},{13,14},{15,16},{17,18},{19... | collective-permute-start | bytes 786440 | tf_op jit(solution)/shard_map/ppermute | solution.py:437
  33.3 0.0 copy-done.2
  33.4 1.7 %second_sweep.1 = (f32[4,2,3,64,256]{4,3,2,1,0:T(8,128)S(1)}, f32[4,2,3,64,256]{4,3,2,1,0:T(8,128)S(1)}) custom-call(f32[1]{0:T(128)S(6)} %copy.10.wave_ref.refs_0_, f32[4,2,3,64,256]{4,3,2,1,0:T(8,128)S(1)} %get-tuple-element.36.refs_2_.e_body, f32[2,3,64,256]{3,2,1,0:T(8,128)S(1)} %get-tuple-element.38.e_p, f32[2,3,64,256]{3,2,1,0:T(8,128)S(1)} %get-tuple-element.40.e_z, ...), custom_call_target="tpu_custom_call" | custom-call | tf_op jit(solution)/shard_map/second_sweep/pallas_call | solution.py:465
  35.1 6.5 %collective-permute-done.2.refs_1_ = f32[2,2,64,256]{3,2,1,0:T(8,128)S(1)} collective-permute-done((f32[2,2,64,256]{3,2,1,0:T(8,128)S(1)}, f32[2,2,64,256]{3,2,1,0:T(8,128)S(1)}, u32[]{:S(2)}, u32[]{:S(2)}) %collective-permute-start.2) | collective-permute-done | bytes 262176 | tf_op jit(solution)/shard_map/ppermute | solution.py:437
  41.5 3.4 %collective-permute-done.3.refs_2_ = f32[2,2,64,256]{3,2,1,0:T(8,128)S(1)} collective-permute-done((f32[2,2,64,256]{3,2,1,0:T(8,128)S(1)}, f32[2,2,64,256]{3,2,1,0:T(8,128)S(1)}, u32[]{:S(2)}, u32[]{:S(2)}) %collective-permute-start.3) | collective-permute-done | bytes 262176 | tf_op jit(solution)/shard_map/ppermute | solution.py:437
  44.9 0.4 third_faces_0.1
  45.4 3.6 %collective-permute-start.6 = (f32[2,2,64,256]{3,2,1,0:T(8,128)S(1)}, f32[2,2,64,256]{3,2,1,0:T(8,128)S(1)}, u32[]{:S(2)}, u32[]{:S(2)}) collective-permute-start(f32[2,2,64,256]{3,2,1,0:T(8,128)S(1)} %get-tuple-element.60), channel_id=1, source_target_pairs={{0,1},{2,3},{4,5},{6,7},{8,9},{10,11},{12,13},{14,15},{16,17},{18,... | collective-permute-start | bytes 786440 | tf_op jit(solution)/shard_map/ppermute | solution.py:437
  49.0 0.0 collective-permute-done.4.refs_1_
  49.0 0.0 collective-permute-done.5.refs_2_
  49.0 0.4 third_faces_1.1
  49.5 4.1 %collective-permute-start.7 = (f32[2,2,64,256]{3,2,1,0:T(8,128)S(1)}, f32[2,2,64,256]{3,2,1,0:T(8,128)S(1)}, u32[]{:S(2)}, u32[]{:S(2)}) collective-permute-start(f32[2,2,64,256]{3,2,1,0:T(8,128)S(1)} %get-tuple-element.62), channel_id=1, source_target_pairs={{1,2},{3,4},{5,6},{7,8},{9,10},{11,12},{13,14},{15,16},{17,18},{19... | collective-permute-start | bytes 786440 | tf_op jit(solution)/shard_map/ppermute | solution.py:437
  53.6 2.7 %last_sweep.1 = (f32[2,3,4,64,256]{4,3,2,1,0:T(8,128)}, f32[2,2,3,64,256]{4,3,2,1,0:T(8,128)S(1)}, f32[16,2,4,4,256]{4,3,2,1,0:T(4,128)S(1)}) custom-call(f32[1]{0:T(128)S(6)} %copy.10.wave_ref.refs_0_, f32[4,2,3,64,256]{4,3,2,1,0:T(8,128)S(1)} %get-tuple-element.47.refs_3_.e_body, f32[2,3,64,256]{3,2,1,0:T(8,128)S(1)} %get-tuple-element.50.e_p, ...), custom_call_target="tpu_custom_call" | custom-call | tf_op jit(solution)/shard_map/last_sweep/pallas_call | solution.py:480
  56.3 2.2 %collective-permute-done.6.halo_p = f32[2,2,64,256]{3,2,1,0:T(8,128)S(1)} collective-permute-done((f32[2,2,64,256]{3,2,1,0:T(8,128)S(1)}, f32[2,2,64,256]{3,2,1,0:T(8,128)S(1)}, u32[]{:S(2)}, u32[]{:S(2)}) %collective-permute-start.6) | collective-permute-done | bytes 262176 | tf_op jit(solution)/shard_map/ppermute | solution.py:437
  58.5 1.3 %collective-permute-done.7.halo_z = f32[2,2,64,256]{3,2,1,0:T(8,128)S(1)} collective-permute-done((f32[2,2,64,256]{3,2,1,0:T(8,128)S(1)}, f32[2,2,64,256]{3,2,1,0:T(8,128)S(1)}, u32[]{:S(2)}, u32[]{:S(2)}) %collective-permute-start.7) | collective-permute-done | bytes 262176 | tf_op jit(solution)/shard_map/ppermute | solution.py:437
  59.8 0.3 gradient.1
  60.2 18.9 %all_to_all.5 = f32[16,2,4,4,256]{4,3,2,1,0:T(4,128)S(1)} all-to-all(f32[16,2,4,4,256]{4,3,2,1,0:T(4,128)S(1)} %gradient.1), channel_id=1, replica_groups=mesh['freq'=16,'gx'=32] {'freq'}, dimensions={0} | all-to-all | bytes 1048576 | tf_op jit(solution)/shard_map/all_to_all | solution.py:492
  79.1 0.7 reduce_sum.9
Async XLA Ops:
  0.6 11.5 %copy-start.1 = (f32[4,64,256]{2,1,0:T(8,128)S(1)}, f32[4,64,256]{2,1,0:T(8,128)}, u32[]{:S(2)}) copy-start(f32[4,64,256]{2,1,0:T(8,128)} %sigma_v.7) | copy-start | bytes 786436
  0.6 11.5 %copy-start = (f32[4,64,256]{2,1,0:T(8,128)S(1)}, f32[4,64,256]{2,1,0:T(8,128)}, u32[]{:S(2)}) copy-start(f32[4,64,256]{2,1,0:T(8,128)} %sigma_h.7) | copy-start | bytes 786436
  0.7 1.2 %copy-start.3 = (bf16[1,2,3,4,64,256]{5,4,3,2,1,0:T(8,128)(2,1)S(1)}, bf16[1,2,3,4,64,256]{5,4,3,2,1,0:T(8,128)(2,1)}, u32[]{:S(2)}) copy-start(bf16[1,2,3,4,64,256]{5,4,3,2,1,0:T(8,128)(2,1)} %param.11) | copy-start | bytes 2359300
  1.8 1.1 %copy-start.4 = (bf16[1,2,3,4,64,256]{5,4,3,2,1,0:T(8,128)(2,1)S(1)}, bf16[1,2,3,4,64,256]{5,4,3,2,1,0:T(8,128)(2,1)}, u32[]{:S(2)}) copy-start(bf16[1,2,3,4,64,256]{5,4,3,2,1,0:T(8,128)(2,1)} %param.12) | copy-start | bytes 2359300
  3.0 9.2 %copy-start.5 = (s32[64]{0:T(128)S(1)}, s32[64]{0:T(128)}, u32[]{:S(2)}) copy-start(s32[64]{0:T(128)} %cells_ref.1) | copy-start | bytes 772
  3.3 15.6 %collective-permute-start = (f32[2,2,64,256]{3,2,1,0:T(8,128)S(1)}, f32[2,2,64,256]{3,2,1,0:T(8,128)S(1)}, u32[]{:S(2)}, u32[]{:S(2)}) collective-permute-start(f32[2,2,64,256]{3,2,1,0:T(8,128)S(1)} %get-tuple-element.35), channel_id=1, source_target_pairs={{0,1},{2,3},{4,5},{6,7},{8,9},{10,11},{12,13},{14,15},{16,17},{18,... | collective-permute-start | bytes 786440 | tf_op jit(solution)/shard_map/ppermute | solution.py:437
  6.7 18.4 %collective-permute-start.1 = (f32[2,2,64,256]{3,2,1,0:T(8,128)S(1)}, f32[2,2,64,256]{3,2,1,0:T(8,128)S(1)}, u32[]{:S(2)}, u32[]{:S(2)}) collective-permute-start(f32[2,2,64,256]{3,2,1,0:T(8,128)S(1)} %get-tuple-element.39), channel_id=1, source_target_pairs={{1,2},{3,4},{5,6},{7,8},{9,10},{11,12},{13,14},{15,16},{17,18},{19... | collective-permute-start | bytes 786440 | tf_op jit(solution)/shard_map/ppermute | solution.py:437
  19.1 14.2 %copy-start.2 = (bf16[1,2,3,4,64,256]{5,4,3,2,1,0:T(8,128)(2,1)S(1)}, bf16[1,2,3,4,64,256]{5,4,3,2,1,0:T(8,128)(2,1)}, u32[]{:S(2)}) copy-start(bf16[1,2,3,4,64,256]{5,4,3,2,1,0:T(8,128)(2,1)} %param.13) | copy-start | bytes 2359300
  19.1 22.4 %collective-permute-start.2 = (f32[2,2,64,256]{3,2,1,0:T(8,128)S(1)}, f32[2,2,64,256]{3,2,1,0:T(8,128)S(1)}, u32[]{:S(2)}, u32[]{:S(2)}) collective-permute-start(f32[2,2,64,256]{3,2,1,0:T(8,128)S(1)} %get-tuple-element.46), channel_id=1, source_target_pairs={{0,1},{2,3},{4,5},{6,7},{8,9},{10,11},{12,13},{14,15},{16,17},{18,... | collective-permute-start | bytes 786440 | tf_op jit(solution)/shard_map/ppermute | solution.py:437
  22.7 22.3 %collective-permute-start.3 = (f32[2,2,64,256]{3,2,1,0:T(8,128)S(1)}, f32[2,2,64,256]{3,2,1,0:T(8,128)S(1)}, u32[]{:S(2)}, u32[]{:S(2)}) collective-permute-start(f32[2,2,64,256]{3,2,1,0:T(8,128)S(1)} %get-tuple-element.49), channel_id=1, source_target_pairs={{0,1},{2,3},{4,5},{6,7},{8,9},{10,11},{12,13},{14,15},{16,17},{18,... | collective-permute-start | bytes 786440 | tf_op jit(solution)/shard_map/ppermute | solution.py:437
  25.4 23.6 %collective-permute-start.4 = (f32[2,2,64,256]{3,2,1,0:T(8,128)S(1)}, f32[2,2,64,256]{3,2,1,0:T(8,128)S(1)}, u32[]{:S(2)}, u32[]{:S(2)}) collective-permute-start(f32[2,2,64,256]{3,2,1,0:T(8,128)S(1)} %get-tuple-element.53), channel_id=1, source_target_pairs={{1,2},{3,4},{5,6},{7,8},{9,10},{11,12},{13,14},{15,16},{17,18},{19... | collective-permute-start | bytes 786440 | tf_op jit(solution)/shard_map/ppermute | solution.py:437
  30.4 18.6 %collective-permute-start.5 = (f32[2,2,64,256]{3,2,1,0:T(8,128)S(1)}, f32[2,2,64,256]{3,2,1,0:T(8,128)S(1)}, u32[]{:S(2)}, u32[]{:S(2)}) collective-permute-start(f32[2,2,64,256]{3,2,1,0:T(8,128)S(1)} %get-tuple-element.54), channel_id=1, source_target_pairs={{1,2},{3,4},{5,6},{7,8},{9,10},{11,12},{13,14},{15,16},{17,18},{19... | collective-permute-start | bytes 786440 | tf_op jit(solution)/shard_map/ppermute | solution.py:437
  45.4 13.1 %collective-permute-start.6 = (f32[2,2,64,256]{3,2,1,0:T(8,128)S(1)}, f32[2,2,64,256]{3,2,1,0:T(8,128)S(1)}, u32[]{:S(2)}, u32[]{:S(2)}) collective-permute-start(f32[2,2,64,256]{3,2,1,0:T(8,128)S(1)} %get-tuple-element.60), channel_id=1, source_target_pairs={{0,1},{2,3},{4,5},{6,7},{8,9},{10,11},{12,13},{14,15},{16,17},{18,... | collective-permute-start | bytes 786440 | tf_op jit(solution)/shard_map/ppermute | solution.py:437
  49.5 10.4 %collective-permute-start.7 = (f32[2,2,64,256]{3,2,1,0:T(8,128)S(1)}, f32[2,2,64,256]{3,2,1,0:T(8,128)S(1)}, u32[]{:S(2)}, u32[]{:S(2)}) collective-permute-start(f32[2,2,64,256]{3,2,1,0:T(8,128)S(1)} %get-tuple-element.62), channel_id=1, source_target_pairs={{1,2},{3,4},{5,6},{7,8},{9,10},{11,12},{13,14},{15,16},{17,18},{19... | collective-permute-start | bytes 786440 | tf_op jit(solution)/shard_map/ppermute | solution.py:437

commit v3 on v2

--- a/solution.py
+++ b/solution.py
@@ -9,6 +9,7 @@
 THETA = 0.5
 SOURCE_GAIN = 8.0
 ROWS = 8
+COSTS = (0, 0, 0, 0)
 
 VMEM = pl.BlockSpec(memory_space=pltpu.VMEM)
 SMEM = pl.BlockSpec(memory_space=pltpu.SMEM)
@@ -167,20 +168,36 @@
                 field[layer, part, comp] = start[part, comp, layer].astype(jnp.float32)
 
 
-def first_faces_kernel(start, adjoint, e_p, e_z, a_p, a_z, face):
+def first_faces_kernel(start, p_send, z_send, got, face, sems):
     _, even = position("gx")
     layers, size_y = start.shape[2], start.shape[3]
-    for values, outs in ((start, (e_p, e_z)), (adjoint, (a_p, a_z))):
-        for side in range(2):
-            layer, right = side_layer(side, even, layers - 1)
-            for part in range(2):
-                for comp in range(3):
-                    face[part, comp] = values[part, comp, layer].astype(jnp.float32)
-            write_faces(face, outs[side], right, size_y)
+    sides = [side_layer(side, even, layers - 1) for side in range(2)]
+    copies = [
+        pltpu.make_async_copy(start.at[:, :, sides[side][0]], got.at[side], sems.at[side]) for side in range(2)
+    ]
+    for copy in copies:
+        copy.start()
+    for side, out in enumerate((p_send, z_send)):
+        copies[side].wait()
+        for part in range(2):
+            for comp in range(3):
+                face[part, comp] = got[side, part, comp].astype(jnp.float32)
+        write_faces(face, out, sides[side][1], size_y)
+
+
+def adjoint_faces_kernel(adjoint, p_send, z_send, face):
+    _, even = position("gx")
+    layers, size_y = adjoint.shape[2], adjoint.shape[3]
+    for side, out in enumerate((p_send, z_send)):
+        layer, right = side_layer(side, even, layers - 1)
+        for part in range(2):
+            for comp in range(3):
+                face[part, comp] = adjoint[part, comp, layer].astype(jnp.float32)
+        write_faces(face, out, right, size_y)
 
 
 def first_sweep_kernel(
-    wave_ref, count_ref, cells_ref, start, adjoint, sigma_h, sigma_v, e_out, a_out, src, field, twist
+    wave_ref, count_ref, cells_ref, start, sigma_h, sigma_v, e_out, src, field, twist
 ):
     index, _ = position("gx")
     layers, size_y, size_z = sigma_h.shape
@@ -204,25 +221,38 @@
 
     lax.fori_loop(0, cells_ref.shape[0], slot, 0)
 
+    def source(part, comp, layer, rows):
+        return src[layer, rows] if part == 1 and comp == 0 else None
+
     zero_layer(field, layers, size_y)
-    for values, out in ((start, e_out), (adjoint, a_out)):
-        widen(values, field, layers, size_y)
-        twists(field, twist, edge, layers, size_y)
-
-        def one(layer, carry, out=out):
-            for y in range(0, size_y, ROWS):
-                rows = slice(y, y + ROWS)
-
-                def source(part, comp):
-                    return src[layer, rows] if out is e_out and part == 1 and comp == 0 else None
-
-                new = relaxed(field, twist, layer, y, size_y, wave, sigma_h[layer, rows], sigma_v[layer, rows], source)
-                for part in range(2):
-                    for comp in range(3):
-                        out[layer, part, comp, rows] = new[part][comp]
-            return carry
-
-        lax.fori_loop(0, layers, one, 0)
+    whole_sweep(start, field, twist, edge, wave, sigma_h, sigma_v, e_out, source)
+
+
+def first_adjoint_kernel(wave_ref, adjoint, sigma_h, sigma_v, a_out, field, twist):
+    index, _ = position("gx")
+    layers, size_y, _ = sigma_h.shape
+    edge = jnp.where(index > 0, 1.0, 0.0)
+    zero_layer(field, layers, size_y)
+    none = lambda part, comp, layer, rows: None
+    whole_sweep(adjoint, field, twist, edge, wave_ref[0], sigma_h, sigma_v, a_out, none)
+
+
+def whole_sweep(values, field, twist, edge, wave, sigma_h, sigma_v, out, source):
+    layers, size_y, _ = sigma_h.shape
+    widen(values, field, layers, size_y)
+    twists(field, twist, edge, layers, size_y)
+
+    def one(layer, carry):
+        for y in range(0, size_y, ROWS):
+            rows = slice(y, y + ROWS)
+            at = lambda part, comp: source(part, comp, layer, rows)
+            new = relaxed(field, twist, layer, y, size_y, wave, sigma_h[layer, rows], sigma_v[layer, rows], at)
+            for part in range(2):
+                for comp in range(3):
+                    out[layer, part, comp, rows] = new[part][comp]
+        return carry
+
+    lax.fori_loop(0, layers, one, 0)
 
 
 def second_faces_kernel(side, wave_ref, halo, part_new, sigma_h, sigma_v, face, send):
@@ -332,10 +362,10 @@
     return wave * (terms[0] + terms[1]), wave * terms[2]
 
 
-def put_rows(out, layers, layer, y, pair, share):
+def put_rows(out, place, y, pair, share):
     for which in range(2):
         for k in range(ROWS // share):
-            out[y // share + k, which, layer] = pair[which][k * share : (k + 1) * share]
+            out[y // share + k, which, place] = pair[which][k * share : (k + 1) * share]
 
 
 def last_sweep_kernel(
@@ -369,7 +399,7 @@
     def inner(layer, carry):
         for y in range(0, size_y, ROWS):
             now, new = sweep(layer, y)
-            put_rows(grad, layers, layer, y, grad_rows(wave, now, new), share)
+            put_rows(grad, layer - 1, y, grad_rows(wave, now, new), share)
         return carry
 
     lax.fori_loop(1, layers - 1, inner, 0)
@@ -386,33 +416,43 @@
     lax.fori_loop(0, 2, outer, 0)
 
 
-def gradient_kernel(wave_ref, halo_p, halo_z, e_p, e_z, faces, inner, sigma_h, sigma_v, grad):
+def gradient_kernel(wave_ref, halo_p, halo_z, e_p, e_z, faces, sigma_h, sigma_v, grad):
     _, even = position("gx")
     layers, size_y, _ = sigma_h.shape
     share = grad.shape[3]
     wave = wave_ref[0]
-    for layer in range(1, layers - 1):
-        for which in range(2):
-            grad[:, which, layer] = inner[:, which, layer]
     for side, (halo, now) in enumerate(((halo_p, e_p), (halo_z, e_z))):
         layer, right = side_layer(side, even, layers - 1)
+        place = right.astype(jnp.int32)
         for y in range(0, size_y, ROWS):
             rows = slice(y, y + ROWS)
             add = fix(halo, y, right, wave, sigma_h[layer, rows], sigma_v[layer, rows], size_y)
             new = [[faces[side, part, comp, rows] + add[part][comp] for comp in range(3)] for part in range(2)]
             old = [[now[part, comp, rows] for comp in range(3)] for part in range(2)]
-            put_rows(grad, layers, layer, y, grad_rows(wave, old, new), share)
-
-
-def call(kernel, name, n_smem, n_vmem, outs, scratch=()):
+            put_rows(grad, place, y, grad_rows(wave, old, new), share)
+
+
+def total_kernel(outer, inner, out):
+    freqs, _, between = inner.shape[:3]
+    for which in range(2):
+        for part, places in ((outer, (0, between + 1)), (inner, range(1, between + 1))):
+            for k, layer in enumerate(places):
+                total = part[0, which, k]
+                for freq in range(1, freqs):
+                    total = total + part[freq, which, k]
+                out[which, layer] = total
+
+
+def call(kernel, name, specs, outs, scratch=(), cost=0):
     return pl.pallas_call(
         kernel,
         name=name,
         out_shape=tuple(jax.ShapeDtypeStruct(shape, jnp.float32) for shape in outs),
-        in_specs=[SMEM] * n_smem + [VMEM] * n_vmem,
+        in_specs=specs,
         out_specs=tuple(VMEM for _ in outs),
-        scratch_shapes=[pltpu.VMEM(shape, jnp.float32) for shape in scratch],
+        scratch_shapes=[s if not isinstance(s, tuple) else pltpu.VMEM(s, jnp.float32) for s in scratch],
         compiler_params=pltpu.CompilerParams(vmem_limit_bytes=24 << 20),
+        cost_estimate=pl.CostEstimate(flops=cost, bytes_accessed=cost, transcendentals=0) if cost else None,
     )
 
 
@@ -441,56 +481,80 @@
     face = (2, 3) + plane
     body = (layers,) + face
     more = (layers + 1,) + face
-
-    e_p, e_z, a_p, a_z = call(first_faces_kernel, "first_faces", 0, 2, [half] * 4, [face])(start, adjoint)
+    hbm = pl.BlockSpec(memory_space=pltpu.HBM)
+
+    e_p, e_z = call(
+        first_faces_kernel,
+        "first_faces",
+        [hbm],
+        [half] * 2,
+        [pltpu.VMEM((2,) + face, jnp.bfloat16), face, pltpu.SemaphoreType.DMA((2,))],
+    )(start)
     e_p_in, e_z_in = swap(e_p, 0), swap(e_z, 1)
-    e1, a1, src = call(
-        first_sweep_kernel, "first_sweep", 3, 4, [body, body, (layers,) + plane], [more, more]
-    )(wave_scale, tx_count, tx_cells, start, adjoint, sigma_h, sigma_v)
-    e1, e_p_in = lax.optimization_barrier((e1, e_p_in))
+    e1, src = call(
+        first_sweep_kernel,
+        "first_sweep",
+        [SMEM] * 3 + [VMEM] * 3,
+        [body, (layers,) + plane],
+        [more, more],
+        COSTS[0],
+    )(wave_scale, tx_count, tx_cells, start, sigma_h, sigma_v)
+    a_p, a_z = call(adjoint_faces_kernel, "adjoint_faces", [VMEM], [half] * 2, [face])(adjoint)
+    a_p, a_z, src = lax.optimization_barrier((a_p, a_z, src))
+    a_p_in, a_z_in = swap(a_p, 0), swap(a_z, 1)
+    (a1,) = call(
+        first_adjoint_kernel, "first_adjoint", [SMEM] + [VMEM] * 3, [body], [more, more], COSTS[1]
+    )(wave_scale, adjoint, sigma_h, sigma_v)
+    a1, e1, e_p_in = lax.optimization_barrier((a1, e1, e_p_in))
 
     def second(side, halo):
         return call(
-            lambda *refs: second_faces_kernel(side, *refs), "second_faces_%d" % side, 1, 4, [face, half]
+            lambda *refs: second_faces_kernel(side, *refs),
+            "second_faces_%d" % side,
+            [SMEM] + [VMEM] * 4,
+            [face, half],
         )(wave_scale, halo, e1, sigma_h, sigma_v)
 
     e1_p, e1_p_out = second(0, e_p_in)
-    a_p, e1_p_out = lax.optimization_barrier((a_p, e1_p_out))
     e1_p_in = swap(e1_p_out, 0)
-    a_p_in = swap(a_p, 0)
     e1_z, e1_z_out = second(1, e_z_in)
-    a_z, e1_z_out = lax.optimization_barrier((a_z, e1_z_out))
     e1_z_in = swap(e1_z_out, 1)
-    a_z_in = swap(a_z, 1)
-    e2, a1_body = call(second_sweep_kernel, "second_sweep", 1, 8, [body, body], [more, more])(
-        wave_scale, e1, e1_p, e1_z, a1, src, seen, sigma_h, sigma_v
-    )
+    e1_z, a_z_in, a_p_in = lax.optimization_barrier((e1_z, a_z_in, a_p_in))
+    e2, a1_body = call(
+        second_sweep_kernel, "second_sweep", [SMEM] + [VMEM] * 8, [body, body], [more, more], COSTS[2]
+    )(wave_scale, e1, e1_p, e1_z, a1, src, seen, sigma_h, sigma_v)
     e2, e1_p_in = lax.optimization_barrier((e2, e1_p_in))
 
     def third(side, e_halo, a_halo):
         return call(
-            lambda *refs: third_faces_kernel(side, *refs), "third_faces_%d" % side, 1, 7, [face, face, half]
+            lambda *refs: third_faces_kernel(side, *refs),
+            "third_faces_%d" % side,
+            [SMEM] + [VMEM] * 7,
+            [face, face, half],
         )(wave_scale, e_halo, a_halo, e2, a1, seen, sigma_h, sigma_v)
 
     e2_p, a1_p, a1_p_out = third(0, e1_p_in, a_p_in)
     a1_p_in = swap(a1_p_out, 0)
     e2_z, a1_z, a1_z_out = third(1, e1_z_in, a_z_in)
     a1_z_in = swap(a1_z_out, 1)
-    blocks = (freqs, 2, layers, share, size_z)
+    inner_blocks = (freqs, 2, layers - 2, share, size_z)
+    outer_blocks = (freqs, 2, 2, share, size_z)
     final, faces, inner = call(
         last_sweep_kernel,
         "last_sweep",
-        1,
-        9,
-        [(2, 3, layers) + plane, (2,) + face, blocks],
+        [SMEM] + [VMEM] * 9,
+        [(2, 3, layers) + plane, (2,) + face, inner_blocks],
         [more, more],
+        COSTS[3],
     )(wave_scale, e2, e2_p, e2_z, a1_body, a1_p, a1_z, seen, sigma_h, sigma_v)
     faces, a1_p_in = lax.optimization_barrier((faces, a1_p_in))
-    (terms,) = call(gradient_kernel, "gradient", 1, 8, [blocks])(
-        wave_scale, a1_p_in, a1_z_in, e2_p, e2_z, faces, inner, sigma_h, sigma_v
+    inner_in = lax.all_to_all(inner, "freq", 0, 0)
+    (outer,) = call(gradient_kernel, "gradient", [SMEM] + [VMEM] * 7, [outer_blocks])(
+        wave_scale, a1_p_in, a1_z_in, e2_p, e2_z, faces, sigma_h, sigma_v
     )
-    gathered = lax.all_to_all(terms, "freq", 0, 0)
-    return (jnp.sum(gathered, axis=0), final[None])
+    outer_in = lax.all_to_all(outer, "freq", 0, 0)
+    (gradient,) = call(total_kernel, "total", [VMEM] * 2, [(2, layers, share, size_z)])(outer_in, inner_in)
+    return (gradient, final[None])
 
 
 def solution(mesh):

time: 80.2 us -> 85.5 us (1.066)
  the two profiles are of different devices: /device:TPU:384 before, /device:TPU:194 now
where the time goes in v3:
time: 85.5 us; the launch traced here: 85 us
  starting transfers between devices  35.6 us (42%)
  waiting for transfers between devices  19.9 us (23%)
  Pallas kernels  12.2 us (14%)
  blocking collectives  12.1 us (14%)
  local copies, waits for them, and re-layouts  2.98 us (3%)
  between operations  2.18 us (3%)
    ppermute x8, starting transfers between devices, swap(): return lax.ppermute(values, 'gx', swaps[side])  29.4 us
    all_to_all x1, blocking collectives, on_device(): outer_in = lax.all_to_all(outer, 'freq', 0, 0)  12.1 us
    ppermute x8, waiting for transfers between devices, swap(): return lax.ppermute(values, 'gx', swaps[side])  10.7 us
    all_to_all x1, waiting for transfers between devices, on_device(): inner_in = lax.all_to_all(inner, 'freq', 0, 0)  9.21 us
    all_to_all x1, starting transfers between devices, on_device(): inner_in = lax.all_to_all(inner, 'freq', 0, 0)  6.22 us
    pallas_call x1, Pallas kernels, on_device(): call(first_sweep_kernel, 'first_sweep', [SMEM] * 3 + [VMEM] * 3, [body, (...  3.44 us
    unnamed x14, local copies, waits for them, and re-layouts  2.98 us
    pallas_call x1, Pallas kernels, on_device(): call(last_sweep_kernel, 'last_sweep', [SMEM] + [VMEM] * 9, [(2, 3, layers...  2.79 us
  transfers between devices with their start and end apart: 9, of which 3 were waited for; matrix products, arithmetic and copies ran while one was open for 0% of the time, Pallas kernels for 13%

profile of v3, /device:TPU:194, one launch (start us, length us, event | category | flops | bytes accessed | tf_op | source)
XLA Modules:
  0.0 85.0 jit_solution(13967725243473705366)
XLA Ops:
  0.6 0.0 copy-start.1
  0.6 0.0 copy-start
  0.6 0.0 copy-start.3
  0.7 1.2 %copy-done.3 = bf16[1,2,3,4,64,256]{5,4,3,2,1,0:T(8,128)(2,1)S(1)} copy-done((bf16[1,2,3,4,64,256]{5,4,3,2,1,0:T(8,128)(2,1)S(1)}, bf16[1,2,3,4,64,256]{5,4,3,2,1,0:T(8,128)(2,1)}, u32[]{:S(2)}) %copy-start.3) | copy-done | bytes 786456
  1.8 0.0 copy-start.4
  1.8 0.3 first_faces.1
  2.2 2.4 %collective-permute-start = (f32[2,2,64,256]{3,2,1,0:T(8,128)S(1)}, f32[2,2,64,256]{3,2,1,0:T(8,128)S(1)}, u32[]{:S(2)}, u32[]{:S(2)}) collective-permute-start(f32[2,2,64,256]{3,2,1,0:T(8,128)S(1)} %get-tuple-element.37), channel_id=1, source_target_pairs={{0,1},{2,3},{4,5},{6,7},{8,9},{10,11},{12,13},{14,15},{16,17},{18,... | collective-permute-start | bytes 786440 | tf_op jit(solution)/shard_map/ppermute | solution.py:477
  4.6 4.8 %collective-permute-start.1 = (f32[2,2,64,256]{3,2,1,0:T(8,128)S(1)}, f32[2,2,64,256]{3,2,1,0:T(8,128)S(1)}, u32[]{:S(2)}, u32[]{:S(2)}) collective-permute-start(f32[2,2,64,256]{3,2,1,0:T(8,128)S(1)} %get-tuple-element.41), channel_id=1, source_target_pairs={{1,2},{3,4},{5,6},{7,8},{9,10},{11,12},{13,14},{15,16},{17,18},{19... | collective-permute-start | bytes 786440 | tf_op jit(solution)/shard_map/ppermute | solution.py:477
  10.7 0.0 copy-start.5
  10.7 1.1 %copy-done.5 = bf16[1,2,3,4,64,256]{5,4,3,2,1,0:T(8,128)(2,1)S(1)} copy-done((bf16[1,2,3,4,64,256]{5,4,3,2,1,0:T(8,128)(2,1)S(1)}, bf16[1,2,3,4,64,256]{5,4,3,2,1,0:T(8,128)(2,1)}, u32[]{:S(2)}) %copy-start.5) | copy-done | bytes 786456
  11.8 0.2 adjoint_faces.1
  12.0 0.0 copy-done.1
  12.0 0.0 copy-done
  12.0 0.0 copy-done.4
  12.0 0.0 copy-start.6
  12.1 0.6 copy-done.6
  12.7 3.4 %first_sweep.1 = (f32[4,2,3,64,256]{4,3,2,1,0:T(8,128)S(1)}, f32[4,64,256]{2,1,0:T(8,128)S(1)}) custom-call(f32[1]{0:T(128)S(6)} %copy.10.wave_ref.refs_0_, s32[1]{0:T(128)S(6)} %copy.11.count_ref, s32[64]{0:T(128)S(1)} %copy-done.6, bf16[2,3,4,64,256]{4,3,2,1,0:T(8,128)(2,1)S(1)} %bitcast.9, f32[4,64,256]{2,1,0:T(8,128)S(1)} %copy-done, ...), custom_call_target="tpu_custom_call" | custom-call | tf_op jit(solution)/shard_map/first_sweep/pallas_call | solution.py:494
  16.2 2.0 %collective-permute-start.2 = (f32[2,2,64,256]{3,2,1,0:T(8,128)S(1)}, f32[2,2,64,256]{3,2,1,0:T(8,128)S(1)}, u32[]{:S(2)}, u32[]{:S(2)}) collective-permute-start(f32[2,2,64,256]{3,2,1,0:T(8,128)S(1)} %get-tuple-element.46), channel_id=1, source_target_pairs={{1,2},{3,4},{5,6},{7,8},{9,10},{11,12},{13,14},{15,16},{17,18},{19... | collective-permute-start | bytes 786440 | tf_op jit(solution)/shard_map/ppermute | solution.py:477
  18.1 3.4 %collective-permute-start.3 = (f32[2,2,64,256]{3,2,1,0:T(8,128)S(1)}, f32[2,2,64,256]{3,2,1,0:T(8,128)S(1)}, u32[]{:S(2)}, u32[]{:S(2)}) collective-permute-start(f32[2,2,64,256]{3,2,1,0:T(8,128)S(1)} %get-tuple-element.47), channel_id=1, source_target_pairs={{0,1},{2,3},{4,5},{6,7},{8,9},{10,11},{12,13},{14,15},{16,17},{18,... | collective-permute-start | bytes 786440 | tf_op jit(solution)/shard_map/ppermute | solution.py:477
  21.6 1.5 %first_adjoint.1.a_part.refs_4_ = f32[4,2,3,64,256]{4,3,2,1,0:T(8,128)S(1)} custom-call(f32[1]{0:T(128)S(6)} %copy.10.wave_ref.refs_0_, bf16[2,3,4,64,256]{4,3,2,1,0:T(8,128)(2,1)S(1)} %bitcast.11, f32[4,64,256]{2,1,0:T(8,128)S(1)} %copy-done, f32[4,64,256]{2,1,0:T(8,128)S(1)} %copy-done.1), custom_call_target="tpu_custom_call" | custom-call | tf_op jit(solution)/shard_map/first_adjoint/pallas_call | solution.py:505
  23.0 0.0 collective-permute-done.refs_1_
  23.1 0.2 second_faces_0.1
  23.3 0.0 copy-start.2
  23.3 2.6 %collective-permute-start.4 = (f32[2,2,64,256]{3,2,1,0:T(8,128)S(1)}, f32[2,2,64,256]{3,2,1,0:T(8,128)S(1)}, u32[]{:S(2)}, u32[]{:S(2)}) collective-permute-start(f32[2,2,64,256]{3,2,1,0:T(8,128)S(1)} %get-tuple-element.52), channel_id=1, source_target_pairs={{0,1},{2,3},{4,5},{6,7},{8,9},{10,11},{12,13},{14,15},{16,17},{18,... | collective-permute-start | bytes 786440 | tf_op jit(solution)/shard_map/ppermute | solution.py:477
  25.9 0.0 collective-permute-done.1.refs_1_
  25.9 0.2 second_faces_1.1
  26.1 4.8 %collective-permute-start.5 = (f32[2,2,64,256]{3,2,1,0:T(8,128)S(1)}, f32[2,2,64,256]{3,2,1,0:T(8,128)S(1)}, u32[]{:S(2)}, u32[]{:S(2)}) collective-permute-start(f32[2,2,64,256]{3,2,1,0:T(8,128)S(1)} %get-tuple-element.57), channel_id=1, source_target_pairs={{1,2},{3,4},{5,6},{7,8},{9,10},{11,12},{13,14},{15,16},{17,18},{19... | collective-permute-start | bytes 786440 | tf_op jit(solution)/shard_map/ppermute | solution.py:477
  30.9 0.0 collective-permute-done.2.refs_2_
  30.9 6.9 %collective-permute-done.3.refs_2_ = f32[2,2,64,256]{3,2,1,0:T(8,128)S(1)} collective-permute-done((f32[2,2,64,256]{3,2,1,0:T(8,128)S(1)}, f32[2,2,64,256]{3,2,1,0:T(8,128)S(1)}, u32[]{:S(2)}, u32[]{:S(2)}) %collective-permute-start.3) | collective-permute-done | bytes 262176 | tf_op jit(solution)/shard_map/ppermute | solution.py:477
  37.8 0.0 copy-done.2
  37.8 1.7 %second_sweep.1 = (f32[4,2,3,64,256]{4,3,2,1,0:T(8,128)S(1)}, f32[4,2,3,64,256]{4,3,2,1,0:T(8,128)S(1)}) custom-call(f32[1]{0:T(128)S(6)} %copy.10.wave_ref.refs_0_, f32[4,2,3,64,256]{4,3,2,1,0:T(8,128)S(1)} %get-tuple-element.38.refs_2_.e_body, f32[2,3,64,256]{3,2,1,0:T(8,128)S(1)} %get-tuple-element.40.e_p, f32[2,3,64,256]{3,2,1,0:T(8,128)S(1)} %get-tuple-element.48.e_z, ...), custom_call_target="tpu_custom_call" | custom-call | tf_op jit(solution)/shard_map/second_sweep/pallas_call | solution.py:523
  39.5 3.8 %collective-permute-done.4.refs_1_ = f32[2,2,64,256]{3,2,1,0:T(8,128)S(1)} collective-permute-done((f32[2,2,64,256]{3,2,1,0:T(8,128)S(1)}, f32[2,2,64,256]{3,2,1,0:T(8,128)S(1)}, u32[]{:S(2)}, u32[]{:S(2)}) %collective-permute-start.4) | collective-permute-done | bytes 262176 | tf_op jit(solution)/shard_map/ppermute | solution.py:477
  43.3 0.4 third_faces_0.1
  43.7 1.9 %collective-permute-start.6 = (f32[2,2,64,256]{3,2,1,0:T(8,128)S(1)}, f32[2,2,64,256]{3,2,1,0:T(8,128)S(1)}, u32[]{:S(2)}, u32[]{:S(2)}) collective-permute-start(f32[2,2,64,256]{3,2,1,0:T(8,128)S(1)} %get-tuple-element.64), channel_id=1, source_target_pairs={{0,1},{2,3},{4,5},{6,7},{8,9},{10,11},{12,13},{14,15},{16,17},{18,... | collective-permute-start | bytes 786440 | tf_op jit(solution)/shard_map/ppermute | solution.py:477
  45.6 0.0 collective-permute-done.5.refs_1_
  45.6 0.4 third_faces_1.1
  46.1 7.5 %collective-permute-start.7 = (f32[2,2,64,256]{3,2,1,0:T(8,128)S(1)}, f32[2,2,64,256]{3,2,1,0:T(8,128)S(1)}, u32[]{:S(2)}, u32[]{:S(2)}) collective-permute-start(f32[2,2,64,256]{3,2,1,0:T(8,128)S(1)} %get-tuple-element.66), channel_id=1, source_target_pairs={{1,2},{3,4},{5,6},{7,8},{9,10},{11,12},{13,14},{15,16},{17,18},{19... | collective-permute-start | bytes 786440 | tf_op jit(solution)/shard_map/ppermute | solution.py:477
  53.6 2.8 %last_sweep.1 = (f32[2,3,4,64,256]{4,3,2,1,0:T(8,128)}, f32[2,2,3,64,256]{4,3,2,1,0:T(8,128)S(1)}, f32[16,2,2,4,256]{4,3,2,1,0:T(4,128)}) custom-call(f32[1]{0:T(128)S(6)} %copy.10.wave_ref.refs_0_, f32[4,2,3,64,256]{4,3,2,1,0:T(8,128)S(1)} %get-tuple-element.53.refs_3_.e_body, f32[2,3,64,256]{3,2,1,0:T(8,128)S(1)} %get-tuple-element.56.e_p, ...), custom_call_target="tpu_custom_call" | custom-call | tf_op jit(solution)/shard_map/last_sweep/pallas_call | solution.py:542
  56.4 6.2 %all-to-all-start.1 = ((f32[16,2,2,4,256]{4,3,2,1,0:T(4,128)}), f32[16,2,2,4,256]{4,3,2,1,0:T(4,128)S(1)}, u32[]{:S(2)}, u32[]{:S(2)}) async-start(f32[16,2,2,4,256]{4,3,2,1,0:T(4,128)} %get-tuple-element.68), calls=%async_computation.1 | async-start | bytes 524288 | tf_op jit(solution)/shard_map/all_to_all | solution.py:551
  62.6 0.0 collective-permute-done.6.halo_p
  62.6 0.0 collective-permute-done.7.halo_z
  62.6 0.3 gradient.1
  63.0 9.2 %all-to-all-done.1.inner = f32[16,2,2,4,256]{4,3,2,1,0:T(4,128)S(1)} async-done(((f32[16,2,2,4,256]{4,3,2,1,0:T(4,128)}), f32[16,2,2,4,256]{4,3,2,1,0:T(4,128)S(1)}, u32[]{:S(2)}, u32[]{:S(2)}) %all-to-all-start.1) | async-done | bytes 262176 | tf_op jit(solution)/shard_map/all_to_all | solution.py:551
  72.2 12.1 %all_to_all.10.outer = f32[16,2,2,4,256]{4,3,2,1,0:T(4,128)S(1)} all-to-all(f32[16,2,2,4,256]{4,3,2,1,0:T(4,128)S(1)} %gradient.1), channel_id=1, replica_groups=mesh['freq'=16,'gx'=32] {'freq'}, dimensions={0} | all-to-all | bytes 524288 | tf_op jit(solution)/shard_map/all_to_all | solution.py:555
  84.3 0.6 total.1
Async XLA Ops:
  0.6 11.4 %copy-start.1 = (f32[4,64,256]{2,1,0:T(8,128)S(1)}, f32[4,64,256]{2,1,0:T(8,128)}, u32[]{:S(2)}) copy-start(f32[4,64,256]{2,1,0:T(8,128)} %sigma_v.9) | copy-start | bytes 786436
  0.6 11.4 %copy-start = (f32[4,64,256]{2,1,0:T(8,128)S(1)}, f32[4,64,256]{2,1,0:T(8,128)}, u32[]{:S(2)}) copy-start(f32[4,64,256]{2,1,0:T(8,128)} %sigma_h.9) | copy-start | bytes 786436
  0.6 1.2 %copy-start.3 = (bf16[1,2,3,4,64,256]{5,4,3,2,1,0:T(8,128)(2,1)S(1)}, bf16[1,2,3,4,64,256]{5,4,3,2,1,0:T(8,128)(2,1)}, u32[]{:S(2)}) copy-start(bf16[1,2,3,4,64,256]{5,4,3,2,1,0:T(8,128)(2,1)} %param.11) | copy-start | bytes 2359300
  1.8 10.2 %copy-start.4 = (bf16[1,2,3,4,64,256]{5,4,3,2,1,0:T(8,128)(2,1)S(1)}, bf16[1,2,3,4,64,256]{5,4,3,2,1,0:T(8,128)(2,1)}, u32[]{:S(2)}) copy-start(bf16[1,2,3,4,64,256]{5,4,3,2,1,0:T(8,128)(2,1)} %param.11) | copy-start | bytes 2359300
  2.2 20.9 %collective-permute-start = (f32[2,2,64,256]{3,2,1,0:T(8,128)S(1)}, f32[2,2,64,256]{3,2,1,0:T(8,128)S(1)}, u32[]{:S(2)}, u32[]{:S(2)}) collective-permute-start(f32[2,2,64,256]{3,2,1,0:T(8,128)S(1)} %get-tuple-element.37), channel_id=1, source_target_pairs={{0,1},{2,3},{4,5},{6,7},{8,9},{10,11},{12,13},{14,15},{16,17},{18,... | collective-permute-start | bytes 786440 | tf_op jit(solution)/shard_map/ppermute | solution.py:477
  4.6 21.2 %collective-permute-start.1 = (f32[2,2,64,256]{3,2,1,0:T(8,128)S(1)}, f32[2,2,64,256]{3,2,1,0:T(8,128)S(1)}, u32[]{:S(2)}, u32[]{:S(2)}) collective-permute-start(f32[2,2,64,256]{3,2,1,0:T(8,128)S(1)} %get-tuple-element.41), channel_id=1, source_target_pairs={{1,2},{3,4},{5,6},{7,8},{9,10},{11,12},{13,14},{15,16},{17,18},{19... | collective-permute-start | bytes 786440 | tf_op jit(solution)/shard_map/ppermute | solution.py:477
  10.7 1.1 %copy-start.5 = (bf16[1,2,3,4,64,256]{5,4,3,2,1,0:T(8,128)(2,1)S(1)}, bf16[1,2,3,4,64,256]{5,4,3,2,1,0:T(8,128)(2,1)}, u32[]{:S(2)}) copy-start(bf16[1,2,3,4,64,256]{5,4,3,2,1,0:T(8,128)(2,1)} %param.12) | copy-start | bytes 2359300
  12.0 0.7 copy-start.6
  16.2 14.7 %collective-permute-start.2 = (f32[2,2,64,256]{3,2,1,0:T(8,128)S(1)}, f32[2,2,64,256]{3,2,1,0:T(8,128)S(1)}, u32[]{:S(2)}, u32[]{:S(2)}) collective-permute-start(f32[2,2,64,256]{3,2,1,0:T(8,128)S(1)} %get-tuple-element.46), channel_id=1, source_target_pairs={{1,2},{3,4},{5,6},{7,8},{9,10},{11,12},{13,14},{15,16},{17,18},{19... | collective-permute-start | bytes 786440 | tf_op jit(solution)/shard_map/ppermute | solution.py:477
  18.1 19.6 %collective-permute-start.3 = (f32[2,2,64,256]{3,2,1,0:T(8,128)S(1)}, f32[2,2,64,256]{3,2,1,0:T(8,128)S(1)}, u32[]{:S(2)}, u32[]{:S(2)}) collective-permute-start(f32[2,2,64,256]{3,2,1,0:T(8,128)S(1)} %get-tuple-element.47), channel_id=1, source_target_pairs={{0,1},{2,3},{4,5},{6,7},{8,9},{10,11},{12,13},{14,15},{16,17},{18,... | collective-permute-start | bytes 786440 | tf_op jit(solution)/shard_map/ppermute | solution.py:477
  23.3 14.5 %copy-start.2 = (bf16[1,2,3,4,64,256]{5,4,3,2,1,0:T(8,128)(2,1)S(1)}, bf16[1,2,3,4,64,256]{5,4,3,2,1,0:T(8,128)(2,1)}, u32[]{:S(2)}) copy-start(bf16[1,2,3,4,64,256]{5,4,3,2,1,0:T(8,128)(2,1)} %param.13) | copy-start | bytes 2359300
  23.3 20.0 %collective-permute-start.4 = (f32[2,2,64,256]{3,2,1,0:T(8,128)S(1)}, f32[2,2,64,256]{3,2,1,0:T(8,128)S(1)}, u32[]{:S(2)}, u32[]{:S(2)}) collective-permute-start(f32[2,2,64,256]{3,2,1,0:T(8,128)S(1)} %get-tuple-element.52), channel_id=1, source_target_pairs={{0,1},{2,3},{4,5},{6,7},{8,9},{10,11},{12,13},{14,15},{16,17},{18,... | collective-permute-start | bytes 786440 | tf_op jit(solution)/shard_map/ppermute | solution.py:477
  26.1 19.5 %collective-permute-start.5 = (f32[2,2,64,256]{3,2,1,0:T(8,128)S(1)}, f32[2,2,64,256]{3,2,1,0:T(8,128)S(1)}, u32[]{:S(2)}, u32[]{:S(2)}) collective-permute-start(f32[2,2,64,256]{3,2,1,0:T(8,128)S(1)} %get-tuple-element.57), channel_id=1, source_target_pairs={{1,2},{3,4},{5,6},{7,8},{9,10},{11,12},{13,14},{15,16},{17,18},{19... | collective-permute-start | bytes 786440 | tf_op jit(solution)/shard_map/ppermute | solution.py:477
  43.7 18.9 %collective-permute-start.6 = (f32[2,2,64,256]{3,2,1,0:T(8,128)S(1)}, f32[2,2,64,256]{3,2,1,0:T(8,128)S(1)}, u32[]{:S(2)}, u32[]{:S(2)}) collective-permute-start(f32[2,2,64,256]{3,2,1,0:T(8,128)S(1)} %get-tuple-element.64), channel_id=1, source_target_pairs={{0,1},{2,3},{4,5},{6,7},{8,9},{10,11},{12,13},{14,15},{16,17},{18,... | collective-permute-start | bytes 786440 | tf_op jit(solution)/shard_map/ppermute | solution.py:477
  46.1 16.6 %collective-permute-start.7 = (f32[2,2,64,256]{3,2,1,0:T(8,128)S(1)}, f32[2,2,64,256]{3,2,1,0:T(8,128)S(1)}, u32[]{:S(2)}, u32[]{:S(2)}) collective-permute-start(f32[2,2,64,256]{3,2,1,0:T(8,128)S(1)} %get-tuple-element.66), channel_id=1, source_target_pairs={{1,2},{3,4},{5,6},{7,8},{9,10},{11,12},{13,14},{15,16},{17,18},{19... | collective-permute-start | bytes 786440 | tf_op jit(solution)/shard_map/ppermute | solution.py:477
  56.4 15.8 %all-to-all-start.1 = ((f32[16,2,2,4,256]{4,3,2,1,0:T(4,128)}), f32[16,2,2,4,256]{4,3,2,1,0:T(4,128)S(1)}, u32[]{:S(2)}, u32[]{:S(2)}) async-start(f32[16,2,2,4,256]{4,3,2,1,0:T(4,128)} %get-tuple-element.68), calls=%async_computation.1 | async-start | bytes 524288 | tf_op jit(solution)/shard_map/all_to_all | solution.py:551

commit v4 on v3

--- a/solution.py
+++ b/solution.py
@@ -9,10 +9,8 @@
 THETA = 0.5
 SOURCE_GAIN = 8.0
 ROWS = 8
-COSTS = (0, 0, 0, 0)
 
 VMEM = pl.BlockSpec(memory_space=pltpu.VMEM)
-SMEM = pl.BlockSpec(memory_space=pltpu.SMEM)
 
 
 def position(axis):
@@ -196,36 +194,40 @@
         write_faces(face, out, right, size_y)
 
 
-def first_sweep_kernel(
-    wave_ref, count_ref, cells_ref, start, sigma_h, sigma_v, e_out, src, field, twist
-):
+def first_sweep_kernel(wave_ref, count_ref, cells_ref, start, sigma_h, sigma_v, e_out, src, field, twist):
     index, _ = position("gx")
     layers, size_y, size_z = sigma_h.shape
-    wave = wave_ref[0]
+    wave = wave_ref[...]
     edge = jnp.where(index > 0, 1.0, 0.0)
-    src[...] = jnp.zeros_like(src)
-    gain = SOURCE_GAIN * wave
-
-    def slot(t, carry):
-        cell = cells_ref[t]
-        layer = cell // (size_y * size_z) - index * layers
-
-        @pl.when((t < count_ref[0]) & (layer >= 0) & (layer < layers))
-        def _():
-            row = lax.rem(cell // size_z, size_y)
-            spot = lane_of((1, size_z)) == lax.rem(cell, size_z)
-            old = src[layer, pl.ds(row, 1), :]
-            src[layer, pl.ds(row, 1), :] = old + jnp.where(spot, gain, 0.0)
-
-        return carry
-
-    lax.fori_loop(0, cells_ref.shape[0], slot, 0)
+    add_slots(wave, count_ref[...], cells_ref[...], index * (layers * size_y), src)
 
     def source(part, comp, layer, rows):
         return src[layer, rows] if part == 1 and comp == 0 else None
 
     zero_layer(field, layers, size_y)
     whole_sweep(start, field, twist, edge, wave, sigma_h, sigma_v, e_out, source)
+
+
+def add_slots(wave, count, cells, first, src):
+    layers, size_y, size_z = src.shape
+    slots = cells.shape[1]
+    shift = size_z.bit_length() - 1
+    assert size_z == 1 << shift
+    row = lax.shift_right_logical(cells, shift) - first
+    spot = jnp.bitwise_and(cells, size_z - 1)
+    live = lane_of((1, slots)) < count
+    row = jnp.where(live, row, -1)
+    at_row = lax.broadcasted_iota(jnp.int32, (layers * size_y, slots), 0) == row
+    at_spot = lax.broadcasted_iota(jnp.int32, (size_z, slots), 0) == spot
+    counts = lax.dot_general(
+        jnp.where(at_row, 1.0, 0.0).astype(jnp.bfloat16),
+        jnp.where(at_spot, 1.0, 0.0).astype(jnp.bfloat16),
+        (((1,), (1,)), ((), ())),
+        preferred_element_type=jnp.float32,
+    )
+    gain = SOURCE_GAIN * wave
+    for layer in range(layers):
+        src[layer] = gain * counts[layer * size_y : (layer + 1) * size_y]
 
 
 def first_adjoint_kernel(wave_ref, adjoint, sigma_h, sigma_v, a_out, field, twist):
@@ -234,7 +236,7 @@
     edge = jnp.where(index > 0, 1.0, 0.0)
     zero_layer(field, layers, size_y)
     none = lambda part, comp, layer, rows: None
-    whole_sweep(adjoint, field, twist, edge, wave_ref[0], sigma_h, sigma_v, a_out, none)
+    whole_sweep(adjoint, field, twist, edge, wave_ref[...], sigma_h, sigma_v, a_out, none)
 
 
 def whole_sweep(values, field, twist, edge, wave, sigma_h, sigma_v, out, source):
@@ -259,7 +261,7 @@
     _, even = position("gx")
     layers, size_y, _ = sigma_h.shape
     layer, right = side_layer(side, even, layers - 1)
-    wave = wave_ref[0]
+    wave = wave_ref[...]
     for y in range(0, size_y, ROWS):
         rows = slice(y, y + ROWS)
         add = fix(halo, y, right, wave, sigma_h[layer, rows], sigma_v[layer, rows], size_y)
@@ -289,7 +291,7 @@
 ):
     index, even = position("gx")
     layers, size_y, _ = sigma_h.shape
-    wave = wave_ref[0]
+    wave = wave_ref[...]
     edge = jnp.where(index > 0, 1.0, 0.0)
     zero_layer(field, layers, size_y)
     gather_layers(e_body, e_p, e_z, field, even, layers)
@@ -341,7 +343,7 @@
     _, even = position("gx")
     layers, size_y, _ = sigma_h.shape
     layer, right = side_layer(side, even, layers - 1)
-    wave = wave_ref[0]
+    wave = wave_ref[...]
     for y in range(0, size_y, ROWS):
         rows = slice(y, y + ROWS)
         add = fix(e_halo, y, right, wave, sigma_h[layer, rows], sigma_v[layer, rows], size_y)
@@ -374,7 +376,7 @@
     index, even = position("gx")
     layers, size_y, _ = sigma_h.shape
     share = grad.shape[3]
-    wave = wave_ref[0]
+    wave = wave_ref[...]
     edge = jnp.where(index > 0, 1.0, 0.0)
     sides = [side_layer(side, even, layers - 1)[0] for side in range(2)]
     for part in range(2):
@@ -416,34 +418,25 @@
     lax.fori_loop(0, 2, outer, 0)
 
 
-def gradient_kernel(wave_ref, halo_p, halo_z, e_p, e_z, faces, sigma_h, sigma_v, grad):
+def gradient_kernel(wave_ref, halo_p, halo_z, e_p, e_z, faces, inner, sigma_h, sigma_v, grad):
     _, even = position("gx")
     layers, size_y, _ = sigma_h.shape
     share = grad.shape[3]
-    wave = wave_ref[0]
+    wave = wave_ref[...]
+    for layer in range(1, layers - 1):
+        for which in range(2):
+            grad[:, which, layer] = inner[:, which, layer - 1]
     for side, (halo, now) in enumerate(((halo_p, e_p), (halo_z, e_z))):
         layer, right = side_layer(side, even, layers - 1)
-        place = right.astype(jnp.int32)
         for y in range(0, size_y, ROWS):
             rows = slice(y, y + ROWS)
             add = fix(halo, y, right, wave, sigma_h[layer, rows], sigma_v[layer, rows], size_y)
             new = [[faces[side, part, comp, rows] + add[part][comp] for comp in range(3)] for part in range(2)]
             old = [[now[part, comp, rows] for comp in range(3)] for part in range(2)]
-            put_rows(grad, place, y, grad_rows(wave, old, new), share)
-
-
-def total_kernel(outer, inner, out):
-    freqs, _, between = inner.shape[:3]
-    for which in range(2):
-        for part, places in ((outer, (0, between + 1)), (inner, range(1, between + 1))):
-            for k, layer in enumerate(places):
-                total = part[0, which, k]
-                for freq in range(1, freqs):
-                    total = total + part[freq, which, k]
-                out[which, layer] = total
-
-
-def call(kernel, name, specs, outs, scratch=(), cost=0):
+            put_rows(grad, layer, y, grad_rows(wave, old, new), share)
+
+
+def call(kernel, name, specs, outs, scratch=()):
     return pl.pallas_call(
         kernel,
         name=name,
@@ -452,7 +445,6 @@
         out_specs=tuple(VMEM for _ in outs),
         scratch_shapes=[s if not isinstance(s, tuple) else pltpu.VMEM(s, jnp.float32) for s in scratch],
         compiler_params=pltpu.CompilerParams(vmem_limit_bytes=24 << 20),
-        cost_estimate=pl.CostEstimate(flops=cost, bytes_accessed=cost, transcendentals=0) if cost else None,
     )
 
 
@@ -466,6 +458,7 @@
     start = field_start[0]
     adjoint = adjoint_start[0]
     seen = observed[0]
+    wave = wave_scale[None]
 
     ends = (
         [(i, i + 1) for i in range(0, slabs - 1, 2)],
@@ -491,29 +484,27 @@
         [pltpu.VMEM((2,) + face, jnp.bfloat16), face, pltpu.SemaphoreType.DMA((2,))],
     )(start)
     e_p_in, e_z_in = swap(e_p, 0), swap(e_z, 1)
+    a_p, a_z = call(adjoint_faces_kernel, "adjoint_faces", [VMEM], [half] * 2, [face])(adjoint)
+    a_p_in, a_z_in = swap(a_p, 0), swap(a_z, 1)
     e1, src = call(
         first_sweep_kernel,
         "first_sweep",
-        [SMEM] * 3 + [VMEM] * 3,
+        [VMEM] * 6,
         [body, (layers,) + plane],
         [more, more],
-        COSTS[0],
-    )(wave_scale, tx_count, tx_cells, start, sigma_h, sigma_v)
-    a_p, a_z = call(adjoint_faces_kernel, "adjoint_faces", [VMEM], [half] * 2, [face])(adjoint)
-    a_p, a_z, src = lax.optimization_barrier((a_p, a_z, src))
-    a_p_in, a_z_in = swap(a_p, 0), swap(a_z, 1)
+    )(wave, tx_count[None], tx_cells[None], start, sigma_h, sigma_v)
     (a1,) = call(
-        first_adjoint_kernel, "first_adjoint", [SMEM] + [VMEM] * 3, [body], [more, more], COSTS[1]
-    )(wave_scale, adjoint, sigma_h, sigma_v)
+        first_adjoint_kernel, "first_adjoint", [VMEM] * 4, [body], [more, more]
+    )(wave, adjoint, sigma_h, sigma_v)
     a1, e1, e_p_in = lax.optimization_barrier((a1, e1, e_p_in))
 
     def second(side, halo):
         return call(
             lambda *refs: second_faces_kernel(side, *refs),
             "second_faces_%d" % side,
-            [SMEM] + [VMEM] * 4,
+            [VMEM] * 5,
             [face, half],
-        )(wave_scale, halo, e1, sigma_h, sigma_v)
+        )(wave, halo, e1, sigma_h, sigma_v)
 
     e1_p, e1_p_out = second(0, e_p_in)
     e1_p_in = swap(e1_p_out, 0)
@@ -521,40 +512,37 @@
     e1_z_in = swap(e1_z_out, 1)
     e1_z, a_z_in, a_p_in = lax.optimization_barrier((e1_z, a_z_in, a_p_in))
     e2, a1_body = call(
-        second_sweep_kernel, "second_sweep", [SMEM] + [VMEM] * 8, [body, body], [more, more], COSTS[2]
-    )(wave_scale, e1, e1_p, e1_z, a1, src, seen, sigma_h, sigma_v)
+        second_sweep_kernel, "second_sweep", [VMEM] * 9, [body, body], [more, more]
+    )(wave, e1, e1_p, e1_z, a1, src, seen, sigma_h, sigma_v)
     e2, e1_p_in = lax.optimization_barrier((e2, e1_p_in))
 
     def third(side, e_halo, a_halo):
         return call(
             lambda *refs: third_faces_kernel(side, *refs),
             "third_faces_%d" % side,
-            [SMEM] + [VMEM] * 7,
+            [VMEM] * 8,
             [face, face, half],
-        )(wave_scale, e_halo, a_halo, e2, a1, seen, sigma_h, sigma_v)
+        )(wave, e_halo, a_halo, e2, a1, seen, sigma_h, sigma_v)
 
     e2_p, a1_p, a1_p_out = third(0, e1_p_in, a_p_in)
     a1_p_in = swap(a1_p_out, 0)
     e2_z, a1_z, a1_z_out = third(1, e1_z_in, a_z_in)
     a1_z_in = swap(a1_z_out, 1)
     inner_blocks = (freqs, 2, layers - 2, share, size_z)
-    outer_blocks = (freqs, 2, 2, share, size_z)
+    blocks = (freqs, 2, layers, share, size_z)
     final, faces, inner = call(
         last_sweep_kernel,
         "last_sweep",
-        [SMEM] + [VMEM] * 9,
+        [VMEM] * 10,
         [(2, 3, layers) + plane, (2,) + face, inner_blocks],
         [more, more],
-        COSTS[3],
-    )(wave_scale, e2, e2_p, e2_z, a1_body, a1_p, a1_z, seen, sigma_h, sigma_v)
+    )(wave, e2, e2_p, e2_z, a1_body, a1_p, a1_z, seen, sigma_h, sigma_v)
     faces, a1_p_in = lax.optimization_barrier((faces, a1_p_in))
-    inner_in = lax.all_to_all(inner, "freq", 0, 0)
-    (outer,) = call(gradient_kernel, "gradient", [SMEM] + [VMEM] * 7, [outer_blocks])(
-        wave_scale, a1_p_in, a1_z_in, e2_p, e2_z, faces, sigma_h, sigma_v
+    (terms,) = call(gradient_kernel, "gradient", [VMEM] * 9, [blocks])(
+        wave, a1_p_in, a1_z_in, e2_p, e2_z, faces, inner, sigma_h, sigma_v
     )
-    outer_in = lax.all_to_all(outer, "freq", 0, 0)
-    (gradient,) = call(total_kernel, "total", [VMEM] * 2, [(2, layers, share, size_z)])(outer_in, inner_in)
-    return (gradient, final[None])
+    gathered = lax.all_to_all(terms, "freq", 0, 0)
+    return (jnp.sum(gathered, axis=0), final[None])
 
 
 def solution(mesh):

time: 85.5 us -> 76.6 us (0.90)
  the two profiles are of different devices: /device:TPU:194 before, /device:TPU:96 now
where the time goes in v4:
time: 76.6 us; the launch traced here: 76.1 us
  starting transfers between devices  24.8 us (32%)
  blocking collectives  19.1 us (25%)
  waiting for transfers between devices  16.3 us (21%)
  Pallas kernels  10.7 us (14%)
  local copies, waits for them, and re-layouts  2.34 us (3%)
  between operations  2.19 us (3%)
    ppermute x8, starting transfers between devices, swap(): return lax.ppermute(values, 'gx', swaps[side])  24.8 us
    all_to_all x1, blocking collectives, on_device(): gathered = lax.all_to_all(terms, 'freq', 0, 0)  19.1 us
    ppermute x8, waiting for transfers between devices, swap(): return lax.ppermute(values, 'gx', swaps[side])  16.3 us
    pallas_call x1, Pallas kernels, on_device(): call(last_sweep_kernel, 'last_sweep', [VMEM] * 10, [(2, 3, layers) + plan...  3.1 us
    unnamed x14, local copies, waits for them, and re-layouts  2.34 us
    pallas_call x1, Pallas kernels, on_device(): call(second_sweep_kernel, 'second_sweep', [VMEM] * 9, [body, body], [more...  1.98 us
    pallas_call x1, Pallas kernels, on_device(): call(first_sweep_kernel, 'first_sweep', [VMEM] * 6, [body, (layers,) + pl...  1.78 us
    pallas_call x1, Pallas kernels, on_device(): call(first_adjoint_kernel, 'first_adjoint', [VMEM] * 4, [body], [more, mo...  1.62 us
  transfers between devices with their start and end apart: 8, of which 3 were waited for; matrix products, arithmetic and copies ran while one was open for 0% of the time, Pallas kernels for 13%

profile of v4, /device:TPU:96, one launch (start us, length us, event | category | flops | bytes accessed | tf_op | source)
XLA Modules:
  0.0 76.1 jit_solution(2908477237088844576)
XLA Ops:
  0.6 0.0 copy-start.1
  0.6 0.0 copy-start
  0.6 0.0 copy-start.4
  0.7 1.2 %copy-done.4 = bf16[1,2,3,4,64,256]{5,4,3,2,1,0:T(8,128)(2,1)S(1)} copy-done((bf16[1,2,3,4,64,256]{5,4,3,2,1,0:T(8,128)(2,1)S(1)}, bf16[1,2,3,4,64,256]{5,4,3,2,1,0:T(8,128)(2,1)}, u32[]{:S(2)}) %copy-start.4) | copy-done | bytes 786456
  1.8 0.3 first_faces.1
  2.2 3.4 %collective-permute-start = (f32[2,2,64,256]{3,2,1,0:T(8,128)S(1)}, f32[2,2,64,256]{3,2,1,0:T(8,128)S(1)}, u32[]{:S(2)}, u32[]{:S(2)}) collective-permute-start(f32[2,2,64,256]{3,2,1,0:T(8,128)S(1)} %get-tuple-element.34), channel_id=1, source_target_pairs={{0,1},{2,3},{4,5},{6,7},{8,9},{10,11},{12,13},{14,15},{16,17},{18,... | collective-permute-start | bytes 786440 | tf_op jit(solution)/shard_map/ppermute | solution.py:470
  5.6 2.0 %collective-permute-start.1 = (f32[2,2,64,256]{3,2,1,0:T(8,128)S(1)}, f32[2,2,64,256]{3,2,1,0:T(8,128)S(1)}, u32[]{:S(2)}, u32[]{:S(2)}) collective-permute-start(f32[2,2,64,256]{3,2,1,0:T(8,128)S(1)} %get-tuple-element.38), channel_id=1, source_target_pairs={{1,2},{3,4},{5,6},{7,8},{9,10},{11,12},{13,14},{15,16},{17,18},{19... | collective-permute-start | bytes 786440 | tf_op jit(solution)/shard_map/ppermute | solution.py:470
  7.6 0.0 copy-start.3
  7.6 1.1 %copy-done.3 = bf16[1,2,3,4,64,256]{5,4,3,2,1,0:T(8,128)(2,1)S(1)} copy-done((bf16[1,2,3,4,64,256]{5,4,3,2,1,0:T(8,128)(2,1)S(1)}, bf16[1,2,3,4,64,256]{5,4,3,2,1,0:T(8,128)(2,1)}, u32[]{:S(2)}) %copy-start.3) | copy-done | bytes 786456
  8.7 0.2 adjoint_faces.1
  8.9 0.0 copy-start.5
  8.9 0.0 copy-start.6
  8.9 4.9 %collective-permute-start.2 = (f32[2,2,64,256]{3,2,1,0:T(8,128)S(1)}, f32[2,2,64,256]{3,2,1,0:T(8,128)S(1)}, u32[]{:S(2)}, u32[]{:S(2)}) collective-permute-start(f32[2,2,64,256]{3,2,1,0:T(8,128)S(1)} %get-tuple-element.40), channel_id=1, source_target_pairs={{1,2},{3,4},{5,6},{7,8},{9,10},{11,12},{13,14},{15,16},{17,18},{19... | collective-permute-start | bytes 786440 | tf_op jit(solution)/shard_map/ppermute | solution.py:470
  13.8 3.7 %collective-permute-start.3 = (f32[2,2,64,256]{3,2,1,0:T(8,128)S(1)}, f32[2,2,64,256]{3,2,1,0:T(8,128)S(1)}, u32[]{:S(2)}, u32[]{:S(2)}) collective-permute-start(f32[2,2,64,256]{3,2,1,0:T(8,128)S(1)} %get-tuple-element.41), channel_id=1, source_target_pairs={{0,1},{2,3},{4,5},{6,7},{8,9},{10,11},{12,13},{14,15},{16,17},{18,... | collective-permute-start | bytes 786440 | tf_op jit(solution)/shard_map/ppermute | solution.py:470
  18.8 0.0 copy-done.1
  18.8 0.0 copy-done
  18.8 1.6 %first_adjoint.1.a_part.refs_4_ = f32[4,2,3,64,256]{4,3,2,1,0:T(8,128)S(1)} custom-call(f32[1,1]{1,0:T(1,128)} %bitcast.7.wave_ref, bf16[2,3,4,64,256]{4,3,2,1,0:T(8,128)(2,1)S(1)} %bitcast.22, f32[4,64,256]{2,1,0:T(8,128)S(1)} %copy-done, f32[4,64,256]{2,1,0:T(8,128)S(1)} %copy-done.1), custom_call_target="tpu_custom_call" | custom-call | tf_op jit(solution)/shard_map/first_adjoint/pallas_call | solution.py:496
  20.4 0.0 copy-done.5
  20.4 0.0 copy-done.6
  20.5 1.8 %first_sweep.1 = (f32[4,2,3,64,256]{4,3,2,1,0:T(8,128)S(1)}, f32[4,64,256]{2,1,0:T(8,128)S(1)}) custom-call(f32[1,1]{1,0:T(1,128)} %bitcast.8.wave_ref, s32[1,1]{1,0:T(1,128)} %bitcast.16.count_ref, s32[1,64]{1,0:T(1,128)S(1)} %bitcast.25, bf16[2,3,4,64,256]{4,3,2,1,0:T(8,128)(2,1)S(1)} %bitcast.24, f32[4,64,256]{2,1,0:T(8,128)S(1)} %copy-done, ...), custom_call_target="tpu_custom_call" | custom-call | tf_op jit(solution)/shard_map/first_sweep/pallas_call | solution.py:489
  22.2 2.3 %collective-permute-done.refs_1_ = f32[2,2,64,256]{3,2,1,0:T(8,128)S(1)} collective-permute-done((f32[2,2,64,256]{3,2,1,0:T(8,128)S(1)}, f32[2,2,64,256]{3,2,1,0:T(8,128)S(1)}, u32[]{:S(2)}, u32[]{:S(2)}) %collective-permute-start) | collective-permute-done | bytes 262176 | tf_op jit(solution)/shard_map/ppermute | solution.py:470
  24.5 0.3 second_faces_0.1
  24.8 0.0 copy-start.2
  24.8 2.1 %collective-permute-start.4 = (f32[2,2,64,256]{3,2,1,0:T(8,128)S(1)}, f32[2,2,64,256]{3,2,1,0:T(8,128)S(1)}, u32[]{:S(2)}, u32[]{:S(2)}) collective-permute-start(f32[2,2,64,256]{3,2,1,0:T(8,128)S(1)} %get-tuple-element.46), channel_id=1, source_target_pairs={{0,1},{2,3},{4,5},{6,7},{8,9},{10,11},{12,13},{14,15},{16,17},{18,... | collective-permute-start | bytes 786440 | tf_op jit(solution)/shard_map/ppermute | solution.py:470
  26.8 0.0 collective-permute-done.1.refs_1_
  26.9 0.3 second_faces_1.1
  27.1 3.5 %collective-permute-start.5 = (f32[2,2,64,256]{3,2,1,0:T(8,128)S(1)}, f32[2,2,64,256]{3,2,1,0:T(8,128)S(1)}, u32[]{:S(2)}, u32[]{:S(2)}) collective-permute-start(f32[2,2,64,256]{3,2,1,0:T(8,128)S(1)} %get-tuple-element.51), channel_id=1, source_target_pairs={{1,2},{3,4},{5,6},{7,8},{9,10},{11,12},{13,14},{15,16},{17,18},{19... | collective-permute-start | bytes 786440 | tf_op jit(solution)/shard_map/ppermute | solution.py:470
  30.6 0.0 collective-permute-done.2.refs_2_
  30.6 0.0 collective-permute-done.3.refs_2_
  30.6 0.0 copy-done.2
  30.6 2.0 %second_sweep.1 = (f32[4,2,3,64,256]{4,3,2,1,0:T(8,128)S(1)}, f32[4,2,3,64,256]{4,3,2,1,0:T(8,128)S(1)}) custom-call(f32[1,1]{1,0:T(1,128)} %bitcast.11.wave_ref, f32[4,2,3,64,256]{4,3,2,1,0:T(8,128)S(1)} %get-tuple-element.35.refs_2_.e_body, f32[2,3,64,256]{3,2,1,0:T(8,128)S(1)} %get-tuple-element.37.e_p, f32[2,3,64,256]{3,2,1,0:T(8,128)S(1)} %get-tuple-element.42.e_z, ...), custom_call_target="tpu_custom_call" | custom-call | tf_op jit(solution)/shard_map/second_sweep/pallas_call | solution.py:514
  32.6 7.6 %collective-permute-done.4.refs_1_ = f32[2,2,64,256]{3,2,1,0:T(8,128)S(1)} collective-permute-done((f32[2,2,64,256]{3,2,1,0:T(8,128)S(1)}, f32[2,2,64,256]{3,2,1,0:T(8,128)S(1)}, u32[]{:S(2)}, u32[]{:S(2)}) %collective-permute-start.4) | collective-permute-done | bytes 262176 | tf_op jit(solution)/shard_map/ppermute | solution.py:470
  40.2 0.4 third_faces_0.1
  40.6 3.4 %collective-permute-start.6 = (f32[2,2,64,256]{3,2,1,0:T(8,128)S(1)}, f32[2,2,64,256]{3,2,1,0:T(8,128)S(1)}, u32[]{:S(2)}, u32[]{:S(2)}) collective-permute-start(f32[2,2,64,256]{3,2,1,0:T(8,128)S(1)} %get-tuple-element.58), channel_id=1, source_target_pairs={{0,1},{2,3},{4,5},{6,7},{8,9},{10,11},{12,13},{14,15},{16,17},{18,... | collective-permute-start | bytes 786440 | tf_op jit(solution)/shard_map/ppermute | solution.py:470
  44.1 0.0 collective-permute-done.5.refs_1_
  44.1 0.4 third_faces_1.1
  44.5 2.0 %collective-permute-start.7 = (f32[2,2,64,256]{3,2,1,0:T(8,128)S(1)}, f32[2,2,64,256]{3,2,1,0:T(8,128)S(1)}, u32[]{:S(2)}, u32[]{:S(2)}) collective-permute-start(f32[2,2,64,256]{3,2,1,0:T(8,128)S(1)} %get-tuple-element.60), channel_id=1, source_target_pairs={{1,2},{3,4},{5,6},{7,8},{9,10},{11,12},{13,14},{15,16},{17,18},{19... | collective-permute-start | bytes 786440 | tf_op jit(solution)/shard_map/ppermute | solution.py:470
  46.5 3.1 %last_sweep.1 = (f32[2,3,4,64,256]{4,3,2,1,0:T(8,128)}, f32[2,2,3,64,256]{4,3,2,1,0:T(8,128)S(1)}, f32[16,2,2,4,256]{4,3,2,1,0:T(4,128)S(1)}) custom-call(f32[1,1]{1,0:T(1,128)} %bitcast.14.wave_ref, f32[4,2,3,64,256]{4,3,2,1,0:T(8,128)S(1)} %get-tuple-element.47.refs_3_.e_body, f32[2,3,64,256]{3,2,1,0:T(8,128)S(1)} %get-tuple-element.50.e_p, ...), custom_call_target="tpu_custom_call" | custom-call | tf_op jit(solution)/shard_map/last_sweep/pallas_call | solution.py:533
  49.6 6.4 %collective-permute-done.6.halo_p = f32[2,2,64,256]{3,2,1,0:T(8,128)S(1)} collective-permute-done((f32[2,2,64,256]{3,2,1,0:T(8,128)S(1)}, f32[2,2,64,256]{3,2,1,0:T(8,128)S(1)}, u32[]{:S(2)}, u32[]{:S(2)}) %collective-permute-start.6) | collective-permute-done | bytes 262176 | tf_op jit(solution)/shard_map/ppermute | solution.py:470
  56.0 0.0 collective-permute-done.7.halo_z
  56.0 0.4 gradient.1
  56.4 19.1 %all_to_all.5 = f32[16,2,4,4,256]{4,3,2,1,0:T(4,128)S(1)} all-to-all(f32[16,2,4,4,256]{4,3,2,1,0:T(4,128)S(1)} %gradient.1), channel_id=1, replica_groups=mesh['freq'=16,'gx'=32] {'freq'}, dimensions={0} | all-to-all | bytes 1048576 | tf_op jit(solution)/shard_map/all_to_all | solution.py:544
  75.4 0.7 reduce_sum.9
Async XLA Ops:
  0.6 18.2 %copy-start.1 = (f32[4,64,256]{2,1,0:T(8,128)S(1)}, f32[4,64,256]{2,1,0:T(8,128)}, u32[]{:S(2)}) copy-start(f32[4,64,256]{2,1,0:T(8,128)} %sigma_v.9) | copy-start | bytes 786436
  0.6 18.2 %copy-start = (f32[4,64,256]{2,1,0:T(8,128)S(1)}, f32[4,64,256]{2,1,0:T(8,128)}, u32[]{:S(2)}) copy-start(f32[4,64,256]{2,1,0:T(8,128)} %sigma_h.9) | copy-start | bytes 786436
  0.6 1.2 %copy-start.4 = (bf16[1,2,3,4,64,256]{5,4,3,2,1,0:T(8,128)(2,1)S(1)}, bf16[1,2,3,4,64,256]{5,4,3,2,1,0:T(8,128)(2,1)}, u32[]{:S(2)}) copy-start(bf16[1,2,3,4,64,256]{5,4,3,2,1,0:T(8,128)(2,1)} %param.11) | copy-start | bytes 2359300
  2.2 22.3 %collective-permute-start = (f32[2,2,64,256]{3,2,1,0:T(8,128)S(1)}, f32[2,2,64,256]{3,2,1,0:T(8,128)S(1)}, u32[]{:S(2)}, u32[]{:S(2)}) collective-permute-start(f32[2,2,64,256]{3,2,1,0:T(8,128)S(1)} %get-tuple-element.34), channel_id=1, source_target_pairs={{0,1},{2,3},{4,5},{6,7},{8,9},{10,11},{12,13},{14,15},{16,17},{18,... | collective-permute-start | bytes 786440 | tf_op jit(solution)/shard_map/ppermute | solution.py:470
  5.6 21.2 %collective-permute-start.1 = (f32[2,2,64,256]{3,2,1,0:T(8,128)S(1)}, f32[2,2,64,256]{3,2,1,0:T(8,128)S(1)}, u32[]{:S(2)}, u32[]{:S(2)}) collective-permute-start(f32[2,2,64,256]{3,2,1,0:T(8,128)S(1)} %get-tuple-element.38), channel_id=1, source_target_pairs={{1,2},{3,4},{5,6},{7,8},{9,10},{11,12},{13,14},{15,16},{17,18},{19... | collective-permute-start | bytes 786440 | tf_op jit(solution)/shard_map/ppermute | solution.py:470
  7.6 1.1 %copy-start.3 = (bf16[1,2,3,4,64,256]{5,4,3,2,1,0:T(8,128)(2,1)S(1)}, bf16[1,2,3,4,64,256]{5,4,3,2,1,0:T(8,128)(2,1)}, u32[]{:S(2)}) copy-start(bf16[1,2,3,4,64,256]{5,4,3,2,1,0:T(8,128)(2,1)} %param.12) | copy-start | bytes 2359300
  8.9 11.5 %copy-start.5 = (bf16[1,2,3,4,64,256]{5,4,3,2,1,0:T(8,128)(2,1)S(1)}, bf16[1,2,3,4,64,256]{5,4,3,2,1,0:T(8,128)(2,1)}, u32[]{:S(2)}) copy-start(bf16[1,2,3,4,64,256]{5,4,3,2,1,0:T(8,128)(2,1)} %param.11) | copy-start | bytes 2359300
  8.9 11.5 %copy-start.6 = (s32[64]{0:T(128)S(1)}, s32[64]{0:T(128)}, u32[]{:S(2)}) copy-start(s32[64]{0:T(128)} %param.15) | copy-start | bytes 772
  8.9 21.7 %collective-permute-start.2 = (f32[2,2,64,256]{3,2,1,0:T(8,128)S(1)}, f32[2,2,64,256]{3,2,1,0:T(8,128)S(1)}, u32[]{:S(2)}, u32[]{:S(2)}) collective-permute-start(f32[2,2,64,256]{3,2,1,0:T(8,128)S(1)} %get-tuple-element.40), channel_id=1, source_target_pairs={{1,2},{3,4},{5,6},{7,8},{9,10},{11,12},{13,14},{15,16},{17,18},{19... | collective-permute-start | bytes 786440 | tf_op jit(solution)/shard_map/ppermute | solution.py:470
  13.8 16.8 %collective-permute-start.3 = (f32[2,2,64,256]{3,2,1,0:T(8,128)S(1)}, f32[2,2,64,256]{3,2,1,0:T(8,128)S(1)}, u32[]{:S(2)}, u32[]{:S(2)}) collective-permute-start(f32[2,2,64,256]{3,2,1,0:T(8,128)S(1)} %get-tuple-element.41), channel_id=1, source_target_pairs={{0,1},{2,3},{4,5},{6,7},{8,9},{10,11},{12,13},{14,15},{16,17},{18,... | collective-permute-start | bytes 786440 | tf_op jit(solution)/shard_map/ppermute | solution.py:470
  24.8 5.8 %copy-start.2 = (bf16[1,2,3,4,64,256]{5,4,3,2,1,0:T(8,128)(2,1)S(1)}, bf16[1,2,3,4,64,256]{5,4,3,2,1,0:T(8,128)(2,1)}, u32[]{:S(2)}) copy-start(bf16[1,2,3,4,64,256]{5,4,3,2,1,0:T(8,128)(2,1)} %param.13) | copy-start | bytes 2359300
  24.8 15.4 %collective-permute-start.4 = (f32[2,2,64,256]{3,2,1,0:T(8,128)S(1)}, f32[2,2,64,256]{3,2,1,0:T(8,128)S(1)}, u32[]{:S(2)}, u32[]{:S(2)}) collective-permute-start(f32[2,2,64,256]{3,2,1,0:T(8,128)S(1)} %get-tuple-element.46), channel_id=1, source_target_pairs={{0,1},{2,3},{4,5},{6,7},{8,9},{10,11},{12,13},{14,15},{16,17},{18,... | collective-permute-start | bytes 786440 | tf_op jit(solution)/shard_map/ppermute | solution.py:470
  27.1 17.0 %collective-permute-start.5 = (f32[2,2,64,256]{3,2,1,0:T(8,128)S(1)}, f32[2,2,64,256]{3,2,1,0:T(8,128)S(1)}, u32[]{:S(2)}, u32[]{:S(2)}) collective-permute-start(f32[2,2,64,256]{3,2,1,0:T(8,128)S(1)} %get-tuple-element.51), channel_id=1, source_target_pairs={{1,2},{3,4},{5,6},{7,8},{9,10},{11,12},{13,14},{15,16},{17,18},{19... | collective-permute-start | bytes 786440 | tf_op jit(solution)/shard_map/ppermute | solution.py:470
  40.6 15.4 %collective-permute-start.6 = (f32[2,2,64,256]{3,2,1,0:T(8,128)S(1)}, f32[2,2,64,256]{3,2,1,0:T(8,128)S(1)}, u32[]{:S(2)}, u32[]{:S(2)}) collective-permute-start(f32[2,2,64,256]{3,2,1,0:T(8,128)S(1)} %get-tuple-element.58), channel_id=1, source_target_pairs={{0,1},{2,3},{4,5},{6,7},{8,9},{10,11},{12,13},{14,15},{16,17},{18,... | collective-permute-start | bytes 786440 | tf_op jit(solution)/shard_map/ppermute | solution.py:470
  44.5 11.5 %collective-permute-start.7 = (f32[2,2,64,256]{3,2,1,0:T(8,128)S(1)}, f32[2,2,64,256]{3,2,1,0:T(8,128)S(1)}, u32[]{:S(2)}, u32[]{:S(2)}) collective-permute-start(f32[2,2,64,256]{3,2,1,0:T(8,128)S(1)} %get-tuple-element.60), channel_id=1, source_target_pairs={{1,2},{3,4},{5,6},{7,8},{9,10},{11,12},{13,14},{15,16},{17,18},{19... | collective-permute-start | bytes 786440 | tf_op jit(solution)/shard_map/ppermute | solution.py:470

commit v5 on v4

--- a/solution.py
+++ b/solution.py
@@ -173,9 +173,9 @@
     copies = [
         pltpu.make_async_copy(start.at[:, :, sides[side][0]], got.at[side], sems.at[side]) for side in range(2)
     ]
-    for copy in copies:
+    for copy in copies[::-1]:
         copy.start()
-    for side, out in enumerate((p_send, z_send)):
+    for side, out in ((1, z_send), (0, p_send)):
         copies[side].wait()
         for part in range(2):
             for comp in range(3):
@@ -483,9 +483,9 @@
         [half] * 2,
         [pltpu.VMEM((2,) + face, jnp.bfloat16), face, pltpu.SemaphoreType.DMA((2,))],
     )(start)
-    e_p_in, e_z_in = swap(e_p, 0), swap(e_z, 1)
+    e_z_in, e_p_in = swap(e_z, 1), swap(e_p, 0)
     a_p, a_z = call(adjoint_faces_kernel, "adjoint_faces", [VMEM], [half] * 2, [face])(adjoint)
-    a_p_in, a_z_in = swap(a_p, 0), swap(a_z, 1)
+    a_z_in = swap(a_z, 1)
     e1, src = call(
         first_sweep_kernel,
         "first_sweep",
@@ -496,7 +496,7 @@
     (a1,) = call(
         first_adjoint_kernel, "first_adjoint", [VMEM] * 4, [body], [more, more]
     )(wave, adjoint, sigma_h, sigma_v)
-    a1, e1, e_p_in = lax.optimization_barrier((a1, e1, e_p_in))
+    a1, e1, e_z_in = lax.optimization_barrier((a1, e1, e_z_in))
 
     def second(side, halo):
         return call(
@@ -506,15 +506,17 @@
             [face, half],
         )(wave, halo, e1, sigma_h, sigma_v)
 
+    e1_z, e1_z_out = second(1, e_z_in)
+    e1_z_in = swap(e1_z_out, 1)
     e1_p, e1_p_out = second(0, e_p_in)
     e1_p_in = swap(e1_p_out, 0)
-    e1_z, e1_z_out = second(1, e_z_in)
-    e1_z_in = swap(e1_z_out, 1)
-    e1_z, a_z_in, a_p_in = lax.optimization_barrier((e1_z, a_z_in, a_p_in))
+    e1_p, a_z_in = lax.optimization_barrier((e1_p, a_z_in))
     e2, a1_body = call(
         second_sweep_kernel, "second_sweep", [VMEM] * 9, [body, body], [more, more]
     )(wave, e1, e1_p, e1_z, a1, src, seen, sigma_h, sigma_v)
-    e2, e1_p_in = lax.optimization_barrier((e2, e1_p_in))
+    e2, a_p = lax.optimization_barrier((e2, a_p))
+    a_p_in = swap(a_p, 0)
+    e2, e1_z_in = lax.optimization_barrier((e2, e1_z_in))
 
     def third(side, e_halo, a_halo):
         return call(
@@ -524,10 +526,10 @@
             [face, face, half],
         )(wave, e_halo, a_halo, e2, a1, seen, sigma_h, sigma_v)
 
+    e2_z, a1_z, a1_z_out = third(1, e1_z_in, a_z_in)
+    a1_z_in = swap(a1_z_out, 1)
     e2_p, a1_p, a1_p_out = third(0, e1_p_in, a_p_in)
     a1_p_in = swap(a1_p_out, 0)
-    e2_z, a1_z, a1_z_out = third(1, e1_z_in, a_z_in)
-    a1_z_in = swap(a1_z_out, 1)
     inner_blocks = (freqs, 2, layers - 2, share, size_z)
     blocks = (freqs, 2, layers, share, size_z)
     final, faces, inner = call(
@@ -537,7 +539,7 @@
         [(2, 3, layers) + plane, (2,) + face, inner_blocks],
         [more, more],
     )(wave, e2, e2_p, e2_z, a1_body, a1_p, a1_z, seen, sigma_h, sigma_v)
-    faces, a1_p_in = lax.optimization_barrier((faces, a1_p_in))
+    faces, a1_z_in = lax.optimization_barrier((faces, a1_z_in))
     (terms,) = call(gradient_kernel, "gradient", [VMEM] * 9, [blocks])(
         wave, a1_p_in, a1_z_in, e2_p, e2_z, faces, inner, sigma_h, sigma_v
     )

time: 76.6 us -> 83.1 us (1.085)
  the two profiles are of different devices: /device:TPU:96 before, /device:TPU:256 now
where the time goes in v5:
time: 83.1 us; the launch traced here: 82.7 us
  starting transfers between devices  24.5 us (29%)
  waiting for transfers between devices  23.1 us (28%)
  blocking collectives  19.2 us (23%)
  Pallas kernels  10.7 us (13%)
  local copies, waits for them, and re-layouts  2.34 us (3%)
  between operations  2.18 us (3%)
    ppermute x8, starting transfers between devices, swap(): return lax.ppermute(values, 'gx', swaps[side])  24.5 us
    ppermute x8, waiting for transfers between devices, swap(): return lax.ppermute(values, 'gx', swaps[side])  23.1 us
    all_to_all x1, blocking collectives, on_device(): gathered = lax.all_to_all(terms, 'freq', 0, 0)  19.2 us
    pallas_call x1, Pallas kernels, on_device(): call(last_sweep_kernel, 'last_sweep', [VMEM] * 10, [(2, 3, layers) + plan...  3.1 us
    unnamed x14, local copies, waits for them, and re-layouts  2.34 us
    pallas_call x1, Pallas kernels, on_device(): call(second_sweep_kernel, 'second_sweep', [VMEM] * 9, [body, body], [more...  1.98 us
    pallas_call x1, Pallas kernels, on_device(): call(first_sweep_kernel, 'first_sweep', [VMEM] * 6, [body, (layers,) + pl...  1.78 us
  transfers between devices with their start and end apart: 8, of which 4 were waited for; matrix products, arithmetic and copies ran while one was open for 0% of the time, Pallas kernels for 12%

profile of v5, /device:TPU:256, one launch (start us, length us, event | category | flops | bytes accessed | tf_op | source)
XLA Modules:
  0.0 82.7 jit_solution(10368282263427545955)
XLA Ops:
  0.6 0.0 copy-start.1
  0.6 0.0 copy-start
  0.6 0.0 copy-start.4
  0.7 1.2 %copy-done.4 = bf16[1,2,3,4,64,256]{5,4,3,2,1,0:T(8,128)(2,1)S(1)} copy-done((bf16[1,2,3,4,64,256]{5,4,3,2,1,0:T(8,128)(2,1)S(1)}, bf16[1,2,3,4,64,256]{5,4,3,2,1,0:T(8,128)(2,1)}, u32[]{:S(2)}) %copy-start.4) | copy-done | bytes 786456
  1.8 0.3 first_faces.1
  2.2 2.9 %collective-permute-start.1 = (f32[2,2,64,256]{3,2,1,0:T(8,128)S(1)}, f32[2,2,64,256]{3,2,1,0:T(8,128)S(1)}, u32[]{:S(2)}, u32[]{:S(2)}) collective-permute-start(f32[2,2,64,256]{3,2,1,0:T(8,128)S(1)} %get-tuple-element.36), channel_id=1, source_target_pairs={{1,2},{3,4},{5,6},{7,8},{9,10},{11,12},{13,14},{15,16},{17,18},{19... | collective-permute-start | bytes 786440 | tf_op jit(solution)/shard_map/ppermute | solution.py:470
  5.1 3.4 %collective-permute-start = (f32[2,2,64,256]{3,2,1,0:T(8,128)S(1)}, f32[2,2,64,256]{3,2,1,0:T(8,128)S(1)}, u32[]{:S(2)}, u32[]{:S(2)}) collective-permute-start(f32[2,2,64,256]{3,2,1,0:T(8,128)S(1)} %get-tuple-element.34), channel_id=1, source_target_pairs={{0,1},{2,3},{4,5},{6,7},{8,9},{10,11},{12,13},{14,15},{16,17},{18,... | collective-permute-start | bytes 786440 | tf_op jit(solution)/shard_map/ppermute | solution.py:470
  8.5 0.0 copy-start.3
  8.5 1.1 %copy-done.3 = bf16[1,2,3,4,64,256]{5,4,3,2,1,0:T(8,128)(2,1)S(1)} copy-done((bf16[1,2,3,4,64,256]{5,4,3,2,1,0:T(8,128)(2,1)S(1)}, bf16[1,2,3,4,64,256]{5,4,3,2,1,0:T(8,128)(2,1)}, u32[]{:S(2)}) %copy-start.3) | copy-done | bytes 786456
  9.6 0.2 adjoint_faces.1
  9.8 0.0 copy-start.5
  9.8 0.0 copy-start.6
  9.8 3.7 %collective-permute-start.3 = (f32[2,2,64,256]{3,2,1,0:T(8,128)S(1)}, f32[2,2,64,256]{3,2,1,0:T(8,128)S(1)}, u32[]{:S(2)}, u32[]{:S(2)}) collective-permute-start(f32[2,2,64,256]{3,2,1,0:T(8,128)S(1)} %get-tuple-element.40), channel_id=1, source_target_pairs={{1,2},{3,4},{5,6},{7,8},{9,10},{11,12},{13,14},{15,16},{17,18},{19... | collective-permute-start | bytes 786440 | tf_op jit(solution)/shard_map/ppermute | solution.py:470
  14.9 0.0 copy-done.1
  14.9 0.0 copy-done
  14.9 1.6 %first_adjoint.1.a_part.refs_4_ = f32[4,2,3,64,256]{4,3,2,1,0:T(8,128)S(1)} custom-call(f32[1,1]{1,0:T(1,128)} %bitcast.7.wave_ref, bf16[2,3,4,64,256]{4,3,2,1,0:T(8,128)(2,1)S(1)} %bitcast.22, f32[4,64,256]{2,1,0:T(8,128)S(1)} %copy-done, f32[4,64,256]{2,1,0:T(8,128)S(1)} %copy-done.1), custom_call_target="tpu_custom_call" | custom-call | tf_op jit(solution)/shard_map/first_adjoint/pallas_call | solution.py:496
  16.5 0.0 copy-done.5
  16.5 0.0 copy-done.6
  16.5 1.8 %first_sweep.1 = (f32[4,2,3,64,256]{4,3,2,1,0:T(8,128)S(1)}, f32[4,64,256]{2,1,0:T(8,128)S(1)}) custom-call(f32[1,1]{1,0:T(1,128)} %bitcast.8.wave_ref, s32[1,1]{1,0:T(1,128)} %bitcast.16.count_ref, s32[1,64]{1,0:T(1,128)S(1)} %bitcast.25, bf16[2,3,4,64,256]{4,3,2,1,0:T(8,128)(2,1)S(1)} %bitcast.24, f32[4,64,256]{2,1,0:T(8,128)S(1)} %copy-done, ...), custom_call_target="tpu_custom_call" | custom-call | tf_op jit(solution)/shard_map/first_sweep/pallas_call | solution.py:489
  18.3 0.0 collective-permute-done.1.refs_1_
  18.3 0.3 second_faces_1.1
  18.6 0.0 copy-start.2
  18.6 4.5 %collective-permute-start.5 = (f32[2,2,64,256]{3,2,1,0:T(8,128)S(1)}, f32[2,2,64,256]{3,2,1,0:T(8,128)S(1)}, u32[]{:S(2)}, u32[]{:S(2)}) collective-permute-start(f32[2,2,64,256]{3,2,1,0:T(8,128)S(1)} %get-tuple-element.50), channel_id=1, source_target_pairs={{1,2},{3,4},{5,6},{7,8},{9,10},{11,12},{13,14},{15,16},{17,18},{19... | collective-permute-start | bytes 786440 | tf_op jit(solution)/shard_map/ppermute | solution.py:470
  23.1 8.0 %collective-permute-done.refs_1_ = f32[2,2,64,256]{3,2,1,0:T(8,128)S(1)} collective-permute-done((f32[2,2,64,256]{3,2,1,0:T(8,128)S(1)}, f32[2,2,64,256]{3,2,1,0:T(8,128)S(1)}, u32[]{:S(2)}, u32[]{:S(2)}) %collective-permute-start) | collective-permute-done | bytes 262176 | tf_op jit(solution)/shard_map/ppermute | solution.py:470
  31.1 0.3 second_faces_0.1
  31.3 0.0 collective-permute-done.3.refs_2_
  31.4 2.2 %collective-permute-start.2 = (f32[2,2,64,256]{3,2,1,0:T(8,128)S(1)}, f32[2,2,64,256]{3,2,1,0:T(8,128)S(1)}, u32[]{:S(2)}, u32[]{:S(2)}) collective-permute-start(f32[2,2,64,256]{3,2,1,0:T(8,128)S(1)} %get-tuple-element.38), channel_id=1, source_target_pairs={{0,1},{2,3},{4,5},{6,7},{8,9},{10,11},{12,13},{14,15},{16,17},{18,... | collective-permute-start | bytes 786440 | tf_op jit(solution)/shard_map/ppermute | solution.py:470
  33.6 0.0 copy-done.2
  33.6 2.0 %second_sweep.1 = (f32[4,2,3,64,256]{4,3,2,1,0:T(8,128)S(1)}, f32[4,2,3,64,256]{4,3,2,1,0:T(8,128)S(1)}) custom-call(f32[1,1]{1,0:T(1,128)} %bitcast.11.wave_ref, f32[4,2,3,64,256]{4,3,2,1,0:T(8,128)S(1)} %get-tuple-element.37.refs_2_.e_body, f32[2,3,64,256]{3,2,1,0:T(8,128)S(1)} %get-tuple-element.41.e_p, f32[2,3,64,256]{3,2,1,0:T(8,128)S(1)} %get-tuple-element.43.e_z, ...), custom_call_target="tpu_custom_call" | custom-call | tf_op jit(solution)/shard_map/second_sweep/pallas_call | solution.py:514
  35.5 3.7 %collective-permute-start.4 = (f32[2,2,64,256]{3,2,1,0:T(8,128)S(1)}, f32[2,2,64,256]{3,2,1,0:T(8,128)S(1)}, u32[]{:S(2)}, u32[]{:S(2)}) collective-permute-start(f32[2,2,64,256]{3,2,1,0:T(8,128)S(1)} %get-tuple-element.48), channel_id=1, source_target_pairs={{0,1},{2,3},{4,5},{6,7},{8,9},{10,11},{12,13},{14,15},{16,17},{18,... | collective-permute-start | bytes 786440 | tf_op jit(solution)/shard_map/ppermute | solution.py:470
  39.2 0.0 collective-permute-done.5.refs_1_
  39.2 0.4 third_faces_1.1
  39.7 1.9 %collective-permute-start.7 = (f32[2,2,64,256]{3,2,1,0:T(8,128)S(1)}, f32[2,2,64,256]{3,2,1,0:T(8,128)S(1)}, u32[]{:S(2)}, u32[]{:S(2)}) collective-permute-start(f32[2,2,64,256]{3,2,1,0:T(8,128)S(1)} %get-tuple-element.61), channel_id=1, source_target_pairs={{1,2},{3,4},{5,6},{7,8},{9,10},{11,12},{13,14},{15,16},{17,18},{19... | collective-permute-start | bytes 786440 | tf_op jit(solution)/shard_map/ppermute | solution.py:470
  41.6 0.8 %collective-permute-done.2.refs_1_ = f32[2,2,64,256]{3,2,1,0:T(8,128)S(1)} collective-permute-done((f32[2,2,64,256]{3,2,1,0:T(8,128)S(1)}, f32[2,2,64,256]{3,2,1,0:T(8,128)S(1)}, u32[]{:S(2)}, u32[]{:S(2)}) %collective-permute-start.2) | collective-permute-done | bytes 262176 | tf_op jit(solution)/shard_map/ppermute | solution.py:470
  42.4 10.3 %collective-permute-done.4.refs_2_ = f32[2,2,64,256]{3,2,1,0:T(8,128)S(1)} collective-permute-done((f32[2,2,64,256]{3,2,1,0:T(8,128)S(1)}, f32[2,2,64,256]{3,2,1,0:T(8,128)S(1)}, u32[]{:S(2)}, u32[]{:S(2)}) %collective-permute-start.4) | collective-permute-done | bytes 262176 | tf_op jit(solution)/shard_map/ppermute | solution.py:470
  52.7 0.4 third_faces_0.1
  53.1 2.2 %collective-permute-start.6 = (f32[2,2,64,256]{3,2,1,0:T(8,128)S(1)}, f32[2,2,64,256]{3,2,1,0:T(8,128)S(1)}, u32[]{:S(2)}, u32[]{:S(2)}) collective-permute-start(f32[2,2,64,256]{3,2,1,0:T(8,128)S(1)} %get-tuple-element.52), channel_id=1, source_target_pairs={{0,1},{2,3},{4,5},{6,7},{8,9},{10,11},{12,13},{14,15},{16,17},{18,... | collective-permute-start | bytes 786440 | tf_op jit(solution)/shard_map/ppermute | solution.py:470
  55.3 3.1 %last_sweep.1 = (f32[2,3,4,64,256]{4,3,2,1,0:T(8,128)}, f32[2,2,3,64,256]{4,3,2,1,0:T(8,128)S(1)}, f32[16,2,2,4,256]{4,3,2,1,0:T(4,128)S(1)}) custom-call(f32[1,1]{1,0:T(1,128)} %bitcast.14.wave_ref, f32[4,2,3,64,256]{4,3,2,1,0:T(8,128)S(1)} %get-tuple-element.51.refs_3_.e_body, f32[2,3,64,256]{3,2,1,0:T(8,128)S(1)} %get-tuple-element.53.e_p, ...), custom_call_target="tpu_custom_call" | custom-call | tf_op jit(solution)/shard_map/last_sweep/pallas_call | solution.py:535
  58.5 0.0 collective-permute-done.7.halo_z
  58.5 4.0 %collective-permute-done.6.halo_p = f32[2,2,64,256]{3,2,1,0:T(8,128)S(1)} collective-permute-done((f32[2,2,64,256]{3,2,1,0:T(8,128)S(1)}, f32[2,2,64,256]{3,2,1,0:T(8,128)S(1)}, u32[]{:S(2)}, u32[]{:S(2)}) %collective-permute-start.6) | collective-permute-done | bytes 262176 | tf_op jit(solution)/shard_map/ppermute | solution.py:470
  62.4 0.4 gradient.1
  62.8 19.2 %all_to_all.5 = f32[16,2,4,4,256]{4,3,2,1,0:T(4,128)S(1)} all-to-all(f32[16,2,4,4,256]{4,3,2,1,0:T(4,128)S(1)} %gradient.1), channel_id=1, replica_groups=mesh['freq'=16,'gx'=32] {'freq'}, dimensions={0} | all-to-all | bytes 1048576 | tf_op jit(solution)/shard_map/all_to_all | solution.py:546
  82.0 0.7 reduce_sum.9
Async XLA Ops:
  0.6 14.2 %copy-start.1 = (f32[4,64,256]{2,1,0:T(8,128)S(1)}, f32[4,64,256]{2,1,0:T(8,128)}, u32[]{:S(2)}) copy-start(f32[4,64,256]{2,1,0:T(8,128)} %sigma_v.9) | copy-start | bytes 786436
  0.6 14.2 %copy-start = (f32[4,64,256]{2,1,0:T(8,128)S(1)}, f32[4,64,256]{2,1,0:T(8,128)}, u32[]{:S(2)}) copy-start(f32[4,64,256]{2,1,0:T(8,128)} %sigma_h.9) | copy-start | bytes 786436
  0.6 1.2 %copy-start.4 = (bf16[1,2,3,4,64,256]{5,4,3,2,1,0:T(8,128)(2,1)S(1)}, bf16[1,2,3,4,64,256]{5,4,3,2,1,0:T(8,128)(2,1)}, u32[]{:S(2)}) copy-start(bf16[1,2,3,4,64,256]{5,4,3,2,1,0:T(8,128)(2,1)} %param.11) | copy-start | bytes 2359300
  2.2 16.1 %collective-permute-start.1 = (f32[2,2,64,256]{3,2,1,0:T(8,128)S(1)}, f32[2,2,64,256]{3,2,1,0:T(8,128)S(1)}, u32[]{:S(2)}, u32[]{:S(2)}) collective-permute-start(f32[2,2,64,256]{3,2,1,0:T(8,128)S(1)} %get-tuple-element.36), channel_id=1, source_target_pairs={{1,2},{3,4},{5,6},{7,8},{9,10},{11,12},{13,14},{15,16},{17,18},{19... | collective-permute-start | bytes 786440 | tf_op jit(solution)/shard_map/ppermute | solution.py:470
  5.1 26.0 %collective-permute-start = (f32[2,2,64,256]{3,2,1,0:T(8,128)S(1)}, f32[2,2,64,256]{3,2,1,0:T(8,128)S(1)}, u32[]{:S(2)}, u32[]{:S(2)}) collective-permute-start(f32[2,2,64,256]{3,2,1,0:T(8,128)S(1)} %get-tuple-element.34), channel_id=1, source_target_pairs={{0,1},{2,3},{4,5},{6,7},{8,9},{10,11},{12,13},{14,15},{16,17},{18,... | collective-permute-start | bytes 786440 | tf_op jit(solution)/shard_map/ppermute | solution.py:470
  8.5 1.1 %copy-start.3 = (bf16[1,2,3,4,64,256]{5,4,3,2,1,0:T(8,128)(2,1)S(1)}, bf16[1,2,3,4,64,256]{5,4,3,2,1,0:T(8,128)(2,1)}, u32[]{:S(2)}) copy-start(bf16[1,2,3,4,64,256]{5,4,3,2,1,0:T(8,128)(2,1)} %param.12) | copy-start | bytes 2359300
  9.8 6.7 %copy-start.5 = (bf16[1,2,3,4,64,256]{5,4,3,2,1,0:T(8,128)(2,1)S(1)}, bf16[1,2,3,4,64,256]{5,4,3,2,1,0:T(8,128)(2,1)}, u32[]{:S(2)}) copy-start(bf16[1,2,3,4,64,256]{5,4,3,2,1,0:T(8,128)(2,1)} %param.11) | copy-start | bytes 2359300
  9.8 6.7 %copy-start.6 = (s32[64]{0:T(128)S(1)}, s32[64]{0:T(128)}, u32[]{:S(2)}) copy-start(s32[64]{0:T(128)} %param.15) | copy-start | bytes 772
  9.8 21.5 %collective-permute-start.3 = (f32[2,2,64,256]{3,2,1,0:T(8,128)S(1)}, f32[2,2,64,256]{3,2,1,0:T(8,128)S(1)}, u32[]{:S(2)}, u32[]{:S(2)}) collective-permute-start(f32[2,2,64,256]{3,2,1,0:T(8,128)S(1)} %get-tuple-element.40), channel_id=1, source_target_pairs={{1,2},{3,4},{5,6},{7,8},{9,10},{11,12},{13,14},{15,16},{17,18},{19... | collective-permute-start | bytes 786440 | tf_op jit(solution)/shard_map/ppermute | solution.py:470
  18.6 15.0 %copy-start.2 = (bf16[1,2,3,4,64,256]{5,4,3,2,1,0:T(8,128)(2,1)S(1)}, bf16[1,2,3,4,64,256]{5,4,3,2,1,0:T(8,128)(2,1)}, u32[]{:S(2)}) copy-start(bf16[1,2,3,4,64,256]{5,4,3,2,1,0:T(8,128)(2,1)} %param.13) | copy-start | bytes 2359300
  18.6 20.6 %collective-permute-start.5 = (f32[2,2,64,256]{3,2,1,0:T(8,128)S(1)}, f32[2,2,64,256]{3,2,1,0:T(8,128)S(1)}, u32[]{:S(2)}, u32[]{:S(2)}) collective-permute-start(f32[2,2,64,256]{3,2,1,0:T(8,128)S(1)} %get-tuple-element.50), channel_id=1, source_target_pairs={{1,2},{3,4},{5,6},{7,8},{9,10},{11,12},{13,14},{15,16},{17,18},{19... | collective-permute-start | bytes 786440 | tf_op jit(solution)/shard_map/ppermute | solution.py:470
  31.4 11.1 %collective-permute-start.2 = (f32[2,2,64,256]{3,2,1,0:T(8,128)S(1)}, f32[2,2,64,256]{3,2,1,0:T(8,128)S(1)}, u32[]{:S(2)}, u32[]{:S(2)}) collective-permute-start(f32[2,2,64,256]{3,2,1,0:T(8,128)S(1)} %get-tuple-element.38), channel_id=1, source_target_pairs={{0,1},{2,3},{4,5},{6,7},{8,9},{10,11},{12,13},{14,15},{16,17},{18,... | collective-permute-start | bytes 786440 | tf_op jit(solution)/shard_map/ppermute | solution.py:470
  35.5 17.2 %collective-permute-start.4 = (f32[2,2,64,256]{3,2,1,0:T(8,128)S(1)}, f32[2,2,64,256]{3,2,1,0:T(8,128)S(1)}, u32[]{:S(2)}, u32[]{:S(2)}) collective-permute-start(f32[2,2,64,256]{3,2,1,0:T(8,128)S(1)} %get-tuple-element.48), channel_id=1, source_target_pairs={{0,1},{2,3},{4,5},{6,7},{8,9},{10,11},{12,13},{14,15},{16,17},{18,... | collective-permute-start | bytes 786440 | tf_op jit(solution)/shard_map/ppermute | solution.py:470
  39.7 18.8 %collective-permute-start.7 = (f32[2,2,64,256]{3,2,1,0:T(8,128)S(1)}, f32[2,2,64,256]{3,2,1,0:T(8,128)S(1)}, u32[]{:S(2)}, u32[]{:S(2)}) collective-permute-start(f32[2,2,64,256]{3,2,1,0:T(8,128)S(1)} %get-tuple-element.61), channel_id=1, source_target_pairs={{1,2},{3,4},{5,6},{7,8},{9,10},{11,12},{13,14},{15,16},{17,18},{19... | collective-permute-start | bytes 786440 | tf_op jit(solution)/shard_map/ppermute | solution.py:470
  53.1 9.3 %collective-permute-start.6 = (f32[2,2,64,256]{3,2,1,0:T(8,128)S(1)}, f32[2,2,64,256]{3,2,1,0:T(8,128)S(1)}, u32[]{:S(2)}, u32[]{:S(2)}) collective-permute-start(f32[2,2,64,256]{3,2,1,0:T(8,128)S(1)} %get-tuple-element.52), channel_id=1, source_target_pairs={{0,1},{2,3},{4,5},{6,7},{8,9},{10,11},{12,13},{14,15},{16,17},{18,... | collective-permute-start | bytes 786440 | tf_op jit(solution)/shard_map/ppermute | solution.py:470

commit v6 on v5

--- a/solution.py
+++ b/solution.py
@@ -166,36 +166,33 @@
                 field[layer, part, comp] = start[part, comp, layer].astype(jnp.float32)
 
 
-def first_faces_kernel(start, p_send, z_send, got, face, sems):
+def first_faces_kernel(start, p_send, got, face, sem):
     _, even = position("gx")
     layers, size_y = start.shape[2], start.shape[3]
-    sides = [side_layer(side, even, layers - 1) for side in range(2)]
-    copies = [
-        pltpu.make_async_copy(start.at[:, :, sides[side][0]], got.at[side], sems.at[side]) for side in range(2)
-    ]
-    for copy in copies[::-1]:
-        copy.start()
-    for side, out in ((1, z_send), (0, p_send)):
-        copies[side].wait()
-        for part in range(2):
-            for comp in range(3):
-                face[part, comp] = got[side, part, comp].astype(jnp.float32)
-        write_faces(face, out, sides[side][1], size_y)
-
-
-def adjoint_faces_kernel(adjoint, p_send, z_send, face):
-    _, even = position("gx")
-    layers, size_y = adjoint.shape[2], adjoint.shape[3]
-    for side, out in enumerate((p_send, z_send)):
-        layer, right = side_layer(side, even, layers - 1)
-        for part in range(2):
-            for comp in range(3):
-                face[part, comp] = adjoint[part, comp, layer].astype(jnp.float32)
-        write_faces(face, out, right, size_y)
-
-
-def first_sweep_kernel(wave_ref, count_ref, cells_ref, start, sigma_h, sigma_v, e_out, src, field, twist):
-    index, _ = position("gx")
+    layer, right = side_layer(0, even, layers - 1)
+    copy = pltpu.make_async_copy(start.at[:, :, layer], got, sem)
+    copy.start()
+    copy.wait()
+    for part in range(2):
+        for comp in range(3):
+            face[part, comp] = got[part, comp].astype(jnp.float32)
+    write_faces(face, p_send, right, size_y)
+
+
+def faces_of(values, side, even, face, out):
+    layers, size_y = values.shape[2], values.shape[3]
+    layer, right = side_layer(side, even, layers - 1)
+    for part in range(2):
+        for comp in range(3):
+            face[part, comp] = values[part, comp, layer].astype(jnp.float32)
+    write_faces(face, out, right, size_y)
+
+
+def first_sweep_kernel(
+    wave_ref, count_ref, cells_ref, start, sigma_h, sigma_v, e_out, src, z_send, field, twist, face
+):
+    index, even = position("gx")
+    faces_of(start, 1, even, face, z_send)
     layers, size_y, size_z = sigma_h.shape
     wave = wave_ref[...]
     edge = jnp.where(index > 0, 1.0, 0.0)
@@ -230,8 +227,10 @@
         src[layer] = gain * counts[layer * size_y : (layer + 1) * size_y]
 
 
-def first_adjoint_kernel(wave_ref, adjoint, sigma_h, sigma_v, a_out, field, twist):
-    index, _ = position("gx")
+def first_adjoint_kernel(wave_ref, adjoint, sigma_h, sigma_v, a_out, p_send, z_send, field, twist, face):
+    index, even = position("gx")
+    faces_of(adjoint, 0, even, face, p_send)
+    faces_of(adjoint, 1, even, face, z_send)
     layers, size_y, _ = sigma_h.shape
     edge = jnp.where(index > 0, 1.0, 0.0)
     zero_layer(field, layers, size_y)
@@ -476,27 +475,22 @@
     more = (layers + 1,) + face
     hbm = pl.BlockSpec(memory_space=pltpu.HBM)
 
-    e_p, e_z = call(
+    (e_p,) = call(
         first_faces_kernel,
         "first_faces",
         [hbm],
-        [half] * 2,
-        [pltpu.VMEM((2,) + face, jnp.bfloat16), face, pltpu.SemaphoreType.DMA((2,))],
+        [half],
+        [pltpu.VMEM(face, jnp.bfloat16), face, pltpu.SemaphoreType.DMA],
     )(start)
-    e_z_in, e_p_in = swap(e_z, 1), swap(e_p, 0)
-    a_p, a_z = call(adjoint_faces_kernel, "adjoint_faces", [VMEM], [half] * 2, [face])(adjoint)
-    a_z_in = swap(a_z, 1)
-    e1, src = call(
+    e_p_in = swap(e_p, 0)
+    e1, src, e_z = call(
         first_sweep_kernel,
         "first_sweep",
         [VMEM] * 6,
-        [body, (layers,) + plane],
-        [more, more],
+        [body, (layers,) + plane, half],
+        [more, more, face],
     )(wave, tx_count[None], tx_cells[None], start, sigma_h, sigma_v)
-    (a1,) = call(
-        first_adjoint_kernel, "first_adjoint", [VMEM] * 4, [body], [more, more]
-    )(wave, adjoint, sigma_h, sigma_v)
-    a1, e1, e_z_in = lax.optimization_barrier((a1, e1, e_z_in))
+    e_z_in = swap(e_z, 1)
 
     def second(side, halo):
         return call(
@@ -506,17 +500,23 @@
             [face, half],
         )(wave, halo, e1, sigma_h, sigma_v)
 
-    e1_z, e1_z_out = second(1, e_z_in)
-    e1_z_in = swap(e1_z_out, 1)
     e1_p, e1_p_out = second(0, e_p_in)
     e1_p_in = swap(e1_p_out, 0)
-    e1_p, a_z_in = lax.optimization_barrier((e1_p, a_z_in))
+    adjoint, e1_p = lax.optimization_barrier((adjoint, e1_p))
+    a1, a_p, a_z = call(
+        first_adjoint_kernel, "first_adjoint", [VMEM] * 4, [body, half, half], [more, more, face]
+    )(wave, adjoint, sigma_h, sigma_v)
+    a1, e_z_in = lax.optimization_barrier((a1, e_z_in))
+    e1_z, e1_z_out = second(1, e_z_in)
+    a_p, a_z, e1_z_out = lax.optimization_barrier((a_p, a_z, e1_z_out))
+    e1_z_in = swap(e1_z_out, 1)
+    a_z_in = swap(a_z, 1)
+    e1_z, e1_p_in = lax.optimization_barrier((e1_z, e1_p_in))
+    a_p_in = swap(a_p, 0)
     e2, a1_body = call(
         second_sweep_kernel, "second_sweep", [VMEM] * 9, [body, body], [more, more]
     )(wave, e1, e1_p, e1_z, a1, src, seen, sigma_h, sigma_v)
-    e2, a_p = lax.optimization_barrier((e2, a_p))
-    a_p_in = swap(a_p, 0)
-    e2, e1_z_in = lax.optimization_barrier((e2, e1_z_in))
+    e2, e1_z_in, a_z_in = lax.optimization_barrier((e2, e1_z_in, a_z_in))
 
     def third(side, e_halo, a_halo):
         return call(

time: 83.1 us -> 78.6 us (0.946)
  the two profiles are of different devices: /device:TPU:256 before, /device:TPU:384 now
where the time goes in v6:
time: 78.6 us; the launch traced here: 78.1 us
  starting transfers between devices  25.6 us (33%)
  blocking collectives  18.9 us (24%)
  waiting for transfers between devices  16.5 us (21%)
  Pallas kernels  10.5 us (13%)
  local copies, waits for them, and re-layouts  3.75 us (5%)
  between operations  2.15 us (3%)
    ppermute x8, starting transfers between devices, swap(): return lax.ppermute(values, 'gx', swaps[side])  25.6 us
    all_to_all x1, blocking collectives, on_device(): gathered = lax.all_to_all(terms, 'freq', 0, 0)  18.9 us
    ppermute x8, waiting for transfers between devices, swap(): return lax.ppermute(values, 'gx', swaps[side])  16.5 us
    unnamed x16, local copies, waits for them, and re-layouts  3.75 us
    pallas_call x1, Pallas kernels, on_device(): call(last_sweep_kernel, 'last_sweep', [VMEM] * 10, [(2, 3, layers) + plan...  3.1 us
    pallas_call x1, Pallas kernels, on_device(): call(second_sweep_kernel, 'second_sweep', [VMEM] * 9, [body, body], [more...  1.97 us
    pallas_call x1, Pallas kernels, on_device(): call(first_sweep_kernel, 'first_sweep', [VMEM] * 6, [body, (layers,) + pl...  1.8 us
    pallas_call x1, Pallas kernels, on_device(): call(first_adjoint_kernel, 'first_adjoint', [VMEM] * 4, [body, half, half...  1.79 us
  transfers between devices with their start and end apart: 8, of which 4 were waited for; matrix products, arithmetic and copies ran while one was open for 0% of the time, Pallas kernels for 13%

profile of v6, /device:TPU:384, one launch (start us, length us, event | category | flops | bytes accessed | tf_op | source)
XLA Modules:
  0.0 78.1 jit_solution(14958136937252073466)
XLA Ops:
  0.6 0.0 copy-start.3
  0.6 0.0 copy-start.1
  0.7 0.0 copy-start.5
  0.7 1.2 %copy-done.5 = bf16[1,2,3,4,64,256]{5,4,3,2,1,0:T(8,128)(2,1)S(1)} copy-done((bf16[1,2,3,4,64,256]{5,4,3,2,1,0:T(8,128)(2,1)S(1)}, bf16[1,2,3,4,64,256]{5,4,3,2,1,0:T(8,128)(2,1)}, u32[]{:S(2)}) %copy-start.5) | copy-done | bytes 786456
  1.8 0.2 first_faces.1
  2.0 3.4 %collective-permute-start = (f32[2,2,64,256]{3,2,1,0:T(8,128)S(1)}, f32[2,2,64,256]{3,2,1,0:T(8,128)S(1)}, u32[]{:S(2)}, u32[]{:S(2)}) collective-permute-start(f32[2,2,64,256]{3,2,1,0:T(8,128)S(1)} %first_faces.1), channel_id=1, source_target_pairs={{0,1},{2,3},{4,5},{6,7},{8,9},{10,11},{12,13},{14,15},{16,17},{18,... | collective-permute-start | bytes 786440 | tf_op jit(solution)/shard_map/ppermute | solution.py:469
  6.7 0.0 copy-start
  6.7 0.9 %copy-done = f32[4,64,256]{2,1,0:T(8,128)S(1)} copy-done((f32[4,64,256]{2,1,0:T(8,128)S(1)}, f32[4,64,256]{2,1,0:T(8,128)}, u32[]{:S(2)}) %copy-start) | copy-done | bytes 262168
  7.7 0.0 copy-start.2
  7.7 0.9 %copy-done.2 = f32[4,64,256]{2,1,0:T(8,128)S(1)} copy-done((f32[4,64,256]{2,1,0:T(8,128)S(1)}, f32[4,64,256]{2,1,0:T(8,128)}, u32[]{:S(2)}) %copy-start.2) | copy-done | bytes 262168
  8.6 0.0 copy-start.7
  8.6 0.7 copy-done.7
  9.3 0.0 copy-start.6
  9.3 1.8 %first_sweep.1 = (f32[4,2,3,64,256]{4,3,2,1,0:T(8,128)S(1)}, f32[4,64,256]{2,1,0:T(8,128)S(1)}, f32[2,2,64,256]{3,2,1,0:T(8,128)S(1)}) custom-call(f32[1,1]{1,0:T(1,128)} %bitcast.7.wave_ref, s32[1,1]{1,0:T(1,128)} %bitcast.16.count_ref, s32[1,64]{1,0:T(1,128)S(1)} %bitcast.24, bf16[2,3,4,64,256]{4,3,2,1,0:T(8,128)(2,1)S(1)} %bitcast.22, ...), custom_call_target="tpu_custom_call" | custom-call | tf_op jit(solution)/shard_map/first_sweep/pallas_call | solution.py:486
  11.1 4.1 %collective-permute-start.1 = (f32[2,2,64,256]{3,2,1,0:T(8,128)S(1)}, f32[2,2,64,256]{3,2,1,0:T(8,128)S(1)}, u32[]{:S(2)}, u32[]{:S(2)}) collective-permute-start(f32[2,2,64,256]{3,2,1,0:T(8,128)S(1)} %get-tuple-element.41), channel_id=1, source_target_pairs={{1,2},{3,4},{5,6},{7,8},{9,10},{11,12},{13,14},{15,16},{17,18},{19... | collective-permute-start | bytes 786440 | tf_op jit(solution)/shard_map/ppermute | solution.py:469
  15.2 0.0 collective-permute-done.refs_1_
  15.2 0.0 copy-done.3
  15.2 0.0 copy-done.1
  15.2 0.3 second_faces_0.1
  15.5 2.2 %collective-permute-start.2 = (f32[2,2,64,256]{3,2,1,0:T(8,128)S(1)}, f32[2,2,64,256]{3,2,1,0:T(8,128)S(1)}, u32[]{:S(2)}, u32[]{:S(2)}) collective-permute-start(f32[2,2,64,256]{3,2,1,0:T(8,128)S(1)} %get-tuple-element.44), channel_id=1, source_target_pairs={{0,1},{2,3},{4,5},{6,7},{8,9},{10,11},{12,13},{14,15},{16,17},{18,... | collective-permute-start | bytes 786440 | tf_op jit(solution)/shard_map/ppermute | solution.py:469
  17.7 0.0 copy-done.6
  17.7 0.0 copy-start.4
  17.7 1.8 %first_adjoint.1 = (f32[4,2,3,64,256]{4,3,2,1,0:T(8,128)S(1)}, f32[2,2,64,256]{3,2,1,0:T(8,128)S(1)}, f32[2,2,64,256]{3,2,1,0:T(8,128)S(1)}) custom-call(f32[1,1]{1,0:T(1,128)} %bitcast.9.wave_ref, bf16[2,3,4,64,256]{4,3,2,1,0:T(8,128)(2,1)S(1)} %bitcast.23, f32[4,64,256]{2,1,0:T(8,128)S(1)} %copy-done.1, f32[4,64,256]{2,1,0:T(8,128)S(1)} %copy-done.3), custom_call_target="tpu_custom_call" | custom-call | tf_op jit(solution)/shard_map/first_adjoint/pallas_call | solution.py:506
  19.5 3.4 %collective-permute-done.1.refs_1_ = f32[2,2,64,256]{3,2,1,0:T(8,128)S(1)} collective-permute-done((f32[2,2,64,256]{3,2,1,0:T(8,128)S(1)}, f32[2,2,64,256]{3,2,1,0:T(8,128)S(1)}, u32[]{:S(2)}, u32[]{:S(2)}) %collective-permute-start.1) | collective-permute-done | bytes 262176 | tf_op jit(solution)/shard_map/ppermute | solution.py:469
  23.0 0.3 second_faces_1.1
  23.2 4.1 %collective-permute-start.4 = (f32[2,2,64,256]{3,2,1,0:T(8,128)S(1)}, f32[2,2,64,256]{3,2,1,0:T(8,128)S(1)}, u32[]{:S(2)}, u32[]{:S(2)}) collective-permute-start(f32[2,2,64,256]{3,2,1,0:T(8,128)S(1)} %get-tuple-element.55), channel_id=1, source_target_pairs={{1,2},{3,4},{5,6},{7,8},{9,10},{11,12},{13,14},{15,16},{17,18},{19... | collective-permute-start | bytes 786440 | tf_op jit(solution)/shard_map/ppermute | solution.py:469
  27.3 3.9 %collective-permute-start.5 = (f32[2,2,64,256]{3,2,1,0:T(8,128)S(1)}, f32[2,2,64,256]{3,2,1,0:T(8,128)S(1)}, u32[]{:S(2)}, u32[]{:S(2)}) collective-permute-start(f32[2,2,64,256]{3,2,1,0:T(8,128)S(1)} %get-tuple-element.56), channel_id=1, source_target_pairs={{1,2},{3,4},{5,6},{7,8},{9,10},{11,12},{13,14},{15,16},{17,18},{19... | collective-permute-start | bytes 786440 | tf_op jit(solution)/shard_map/ppermute | solution.py:469
  31.2 1.9 %collective-permute-start.3 = (f32[2,2,64,256]{3,2,1,0:T(8,128)S(1)}, f32[2,2,64,256]{3,2,1,0:T(8,128)S(1)}, u32[]{:S(2)}, u32[]{:S(2)}) collective-permute-start(f32[2,2,64,256]{3,2,1,0:T(8,128)S(1)} %get-tuple-element.49), channel_id=1, source_target_pairs={{0,1},{2,3},{4,5},{6,7},{8,9},{10,11},{12,13},{14,15},{16,17},{18,... | collective-permute-start | bytes 786440 | tf_op jit(solution)/shard_map/ppermute | solution.py:469
  33.1 6.6 %collective-permute-done.2.refs_1_ = f32[2,2,64,256]{3,2,1,0:T(8,128)S(1)} collective-permute-done((f32[2,2,64,256]{3,2,1,0:T(8,128)S(1)}, f32[2,2,64,256]{3,2,1,0:T(8,128)S(1)}, u32[]{:S(2)}, u32[]{:S(2)}) %collective-permute-start.2) | collective-permute-done | bytes 262176 | tf_op jit(solution)/shard_map/ppermute | solution.py:469
  39.7 0.0 copy-done.4
  39.7 2.0 %second_sweep.1 = (f32[4,2,3,64,256]{4,3,2,1,0:T(8,128)S(1)}, f32[4,2,3,64,256]{4,3,2,1,0:T(8,128)S(1)}) custom-call(f32[1,1]{1,0:T(1,128)} %bitcast.11.wave_ref, f32[4,2,3,64,256]{4,3,2,1,0:T(8,128)S(1)} %get-tuple-element.37.refs_2_.e_body, f32[2,3,64,256]{3,2,1,0:T(8,128)S(1)} %get-tuple-element.50.e_p, f32[2,3,64,256]{3,2,1,0:T(8,128)S(1)} %get-tuple-element.51.e_z, ...), custom_call_target="tpu_custom_call" | custom-call | tf_op jit(solution)/shard_map/second_sweep/pallas_call | solution.py:516
  41.7 0.0 collective-permute-done.4.refs_1_
  41.7 0.0 collective-permute-done.5.refs_2_
  41.7 0.4 third_faces_1.1
  42.1 4.1 %collective-permute-start.7 = (f32[2,2,64,256]{3,2,1,0:T(8,128)S(1)}, f32[2,2,64,256]{3,2,1,0:T(8,128)S(1)}, u32[]{:S(2)}, u32[]{:S(2)}) collective-permute-start(f32[2,2,64,256]{3,2,1,0:T(8,128)S(1)} %get-tuple-element.67), channel_id=1, source_target_pairs={{1,2},{3,4},{5,6},{7,8},{9,10},{11,12},{13,14},{15,16},{17,18},{19... | collective-permute-start | bytes 786440 | tf_op jit(solution)/shard_map/ppermute | solution.py:469
  46.2 0.0 collective-permute-done.3.refs_2_
  46.3 0.4 third_faces_0.1
  46.7 1.9 %collective-permute-start.6 = (f32[2,2,64,256]{3,2,1,0:T(8,128)S(1)}, f32[2,2,64,256]{3,2,1,0:T(8,128)S(1)}, u32[]{:S(2)}, u32[]{:S(2)}) collective-permute-start(f32[2,2,64,256]{3,2,1,0:T(8,128)S(1)} %get-tuple-element.58), channel_id=1, source_target_pairs={{0,1},{2,3},{4,5},{6,7},{8,9},{10,11},{12,13},{14,15},{16,17},{18,... | collective-permute-start | bytes 786440 | tf_op jit(solution)/shard_map/ppermute | solution.py:469
  48.6 3.1 %last_sweep.1 = (f32[2,3,4,64,256]{4,3,2,1,0:T(8,128)}, f32[2,2,3,64,256]{4,3,2,1,0:T(8,128)S(1)}, f32[16,2,2,4,256]{4,3,2,1,0:T(4,128)S(1)}) custom-call(f32[1,1]{1,0:T(1,128)} %bitcast.14.wave_ref, f32[4,2,3,64,256]{4,3,2,1,0:T(8,128)S(1)} %get-tuple-element.57.refs_3_.e_body, f32[2,3,64,256]{3,2,1,0:T(8,128)S(1)} %get-tuple-element.59.e_p, ...), custom_call_target="tpu_custom_call" | custom-call | tf_op jit(solution)/shard_map/last_sweep/pallas_call | solution.py:535
  51.7 0.9 %collective-permute-done.7.halo_z = f32[2,2,64,256]{3,2,1,0:T(8,128)S(1)} collective-permute-done((f32[2,2,64,256]{3,2,1,0:T(8,128)S(1)}, f32[2,2,64,256]{3,2,1,0:T(8,128)S(1)}, u32[]{:S(2)}, u32[]{:S(2)}) %collective-permute-start.7) | collective-permute-done | bytes 262176 | tf_op jit(solution)/shard_map/ppermute | solution.py:469
  52.6 5.5 %collective-permute-done.6.halo_p = f32[2,2,64,256]{3,2,1,0:T(8,128)S(1)} collective-permute-done((f32[2,2,64,256]{3,2,1,0:T(8,128)S(1)}, f32[2,2,64,256]{3,2,1,0:T(8,128)S(1)}, u32[]{:S(2)}, u32[]{:S(2)}) %collective-permute-start.6) | collective-permute-done | bytes 262176 | tf_op jit(solution)/shard_map/ppermute | solution.py:469
  58.1 0.4 gradient.1
  58.5 18.9 %all_to_all.5 = f32[16,2,4,4,256]{4,3,2,1,0:T(4,128)S(1)} all-to-all(f32[16,2,4,4,256]{4,3,2,1,0:T(4,128)S(1)} %gradient.1), channel_id=1, replica_groups=mesh['freq'=16,'gx'=32] {'freq'}, dimensions={0} | all-to-all | bytes 1048576 | tf_op jit(solution)/shard_map/all_to_all | solution.py:546
  77.4 0.7 reduce_sum.9
Async XLA Ops:
  0.6 14.6 %copy-start.3 = (f32[4,64,256]{2,1,0:T(8,128)S(1)}, f32[4,64,256]{2,1,0:T(8,128)}, u32[]{:S(2)}) copy-start(f32[4,64,256]{2,1,0:T(8,128)} %sigma_v.9) | copy-start | bytes 786436
  0.6 14.6 %copy-start.1 = (f32[4,64,256]{2,1,0:T(8,128)S(1)}, f32[4,64,256]{2,1,0:T(8,128)}, u32[]{:S(2)}) copy-start(f32[4,64,256]{2,1,0:T(8,128)} %sigma_h.9) | copy-start | bytes 786436
  0.7 1.2 %copy-start.5 = (bf16[1,2,3,4,64,256]{5,4,3,2,1,0:T(8,128)(2,1)S(1)}, bf16[1,2,3,4,64,256]{5,4,3,2,1,0:T(8,128)(2,1)}, u32[]{:S(2)}) copy-start(bf16[1,2,3,4,64,256]{5,4,3,2,1,0:T(8,128)(2,1)} %param.11) | copy-start | bytes 2359300
  2.0 13.2 %collective-permute-start = (f32[2,2,64,256]{3,2,1,0:T(8,128)S(1)}, f32[2,2,64,256]{3,2,1,0:T(8,128)S(1)}, u32[]{:S(2)}, u32[]{:S(2)}) collective-permute-start(f32[2,2,64,256]{3,2,1,0:T(8,128)S(1)} %first_faces.1), channel_id=1, source_target_pairs={{0,1},{2,3},{4,5},{6,7},{8,9},{10,11},{12,13},{14,15},{16,17},{18,... | collective-permute-start | bytes 786440 | tf_op jit(solution)/shard_map/ppermute | solution.py:469
  6.7 1.0 %copy-start = (f32[4,64,256]{2,1,0:T(8,128)S(1)}, f32[4,64,256]{2,1,0:T(8,128)}, u32[]{:S(2)}) copy-start(f32[4,64,256]{2,1,0:T(8,128)} %sigma_h.9) | copy-start | bytes 786436
  7.7 0.9 %copy-start.2 = (f32[4,64,256]{2,1,0:T(8,128)S(1)}, f32[4,64,256]{2,1,0:T(8,128)}, u32[]{:S(2)}) copy-start(f32[4,64,256]{2,1,0:T(8,128)} %sigma_v.9) | copy-start | bytes 786436
  8.6 0.7 copy-start.7
  9.3 8.4 %copy-start.6 = (bf16[1,2,3,4,64,256]{5,4,3,2,1,0:T(8,128)(2,1)S(1)}, bf16[1,2,3,4,64,256]{5,4,3,2,1,0:T(8,128)(2,1)}, u32[]{:S(2)}) copy-start(bf16[1,2,3,4,64,256]{5,4,3,2,1,0:T(8,128)(2,1)} %param.12) | copy-start | bytes 2359300
  11.1 11.9 %collective-permute-start.1 = (f32[2,2,64,256]{3,2,1,0:T(8,128)S(1)}, f32[2,2,64,256]{3,2,1,0:T(8,128)S(1)}, u32[]{:S(2)}, u32[]{:S(2)}) collective-permute-start(f32[2,2,64,256]{3,2,1,0:T(8,128)S(1)} %get-tuple-element.41), channel_id=1, source_target_pairs={{1,2},{3,4},{5,6},{7,8},{9,10},{11,12},{13,14},{15,16},{17,18},{19... | collective-permute-start | bytes 786440 | tf_op jit(solution)/shard_map/ppermute | solution.py:469
  15.5 24.2 %collective-permute-start.2 = (f32[2,2,64,256]{3,2,1,0:T(8,128)S(1)}, f32[2,2,64,256]{3,2,1,0:T(8,128)S(1)}, u32[]{:S(2)}, u32[]{:S(2)}) collective-permute-start(f32[2,2,64,256]{3,2,1,0:T(8,128)S(1)} %get-tuple-element.44), channel_id=1, source_target_pairs={{0,1},{2,3},{4,5},{6,7},{8,9},{10,11},{12,13},{14,15},{16,17},{18,... | collective-permute-start | bytes 786440 | tf_op jit(solution)/shard_map/ppermute | solution.py:469
  17.7 22.0 %copy-start.4 = (bf16[1,2,3,4,64,256]{5,4,3,2,1,0:T(8,128)(2,1)S(1)}, bf16[1,2,3,4,64,256]{5,4,3,2,1,0:T(8,128)(2,1)}, u32[]{:S(2)}) copy-start(bf16[1,2,3,4,64,256]{5,4,3,2,1,0:T(8,128)(2,1)} %param.13) | copy-start | bytes 2359300
  23.2 18.5 %collective-permute-start.4 = (f32[2,2,64,256]{3,2,1,0:T(8,128)S(1)}, f32[2,2,64,256]{3,2,1,0:T(8,128)S(1)}, u32[]{:S(2)}, u32[]{:S(2)}) collective-permute-start(f32[2,2,64,256]{3,2,1,0:T(8,128)S(1)} %get-tuple-element.55), channel_id=1, source_target_pairs={{1,2},{3,4},{5,6},{7,8},{9,10},{11,12},{13,14},{15,16},{17,18},{19... | collective-permute-start | bytes 786440 | tf_op jit(solution)/shard_map/ppermute | solution.py:469
  27.3 14.4 %collective-permute-start.5 = (f32[2,2,64,256]{3,2,1,0:T(8,128)S(1)}, f32[2,2,64,256]{3,2,1,0:T(8,128)S(1)}, u32[]{:S(2)}, u32[]{:S(2)}) collective-permute-start(f32[2,2,64,256]{3,2,1,0:T(8,128)S(1)} %get-tuple-element.56), channel_id=1, source_target_pairs={{1,2},{3,4},{5,6},{7,8},{9,10},{11,12},{13,14},{15,16},{17,18},{19... | collective-permute-start | bytes 786440 | tf_op jit(solution)/shard_map/ppermute | solution.py:469
  31.2 15.1 %collective-permute-start.3 = (f32[2,2,64,256]{3,2,1,0:T(8,128)S(1)}, f32[2,2,64,256]{3,2,1,0:T(8,128)S(1)}, u32[]{:S(2)}, u32[]{:S(2)}) collective-permute-start(f32[2,2,64,256]{3,2,1,0:T(8,128)S(1)} %get-tuple-element.49), channel_id=1, source_target_pairs={{0,1},{2,3},{4,5},{6,7},{8,9},{10,11},{12,13},{14,15},{16,17},{18,... | collective-permute-start | bytes 786440 | tf_op jit(solution)/shard_map/ppermute | solution.py:469
  42.1 10.5 %collective-permute-start.7 = (f32[2,2,64,256]{3,2,1,0:T(8,128)S(1)}, f32[2,2,64,256]{3,2,1,0:T(8,128)S(1)}, u32[]{:S(2)}, u32[]{:S(2)}) collective-permute-start(f32[2,2,64,256]{3,2,1,0:T(8,128)S(1)} %get-tuple-element.67), channel_id=1, source_target_pairs={{1,2},{3,4},{5,6},{7,8},{9,10},{11,12},{13,14},{15,16},{17,18},{19... | collective-permute-start | bytes 786440 | tf_op jit(solution)/shard_map/ppermute | solution.py:469
  46.7 11.5 %collective-permute-start.6 = (f32[2,2,64,256]{3,2,1,0:T(8,128)S(1)}, f32[2,2,64,256]{3,2,1,0:T(8,128)S(1)}, u32[]{:S(2)}, u32[]{:S(2)}) collective-permute-start(f32[2,2,64,256]{3,2,1,0:T(8,128)S(1)} %get-tuple-element.58), channel_id=1, source_target_pairs={{0,1},{2,3},{4,5},{6,7},{8,9},{10,11},{12,13},{14,15},{16,17},{18,... | collective-permute-start | bytes 786440 | tf_op jit(solution)/shard_map/ppermute | solution.py:469

commit v7 on v6

--- a/solution.py
+++ b/solution.py
@@ -166,17 +166,10 @@
                 field[layer, part, comp] = start[part, comp, layer].astype(jnp.float32)
 
 
-def first_faces_kernel(start, p_send, got, face, sem):
+def faces_kernel(values, p_send, z_send, face):
     _, even = position("gx")
-    layers, size_y = start.shape[2], start.shape[3]
-    layer, right = side_layer(0, even, layers - 1)
-    copy = pltpu.make_async_copy(start.at[:, :, layer], got, sem)
-    copy.start()
-    copy.wait()
-    for part in range(2):
-        for comp in range(3):
-            face[part, comp] = got[part, comp].astype(jnp.float32)
-    write_faces(face, p_send, right, size_y)
+    faces_of(values, 0, even, face, p_send)
+    faces_of(values, 1, even, face, z_send)
 
 
 def faces_of(values, side, even, face, out):
@@ -188,11 +181,8 @@
     write_faces(face, out, right, size_y)
 
 
-def first_sweep_kernel(
-    wave_ref, count_ref, cells_ref, start, sigma_h, sigma_v, e_out, src, z_send, field, twist, face
-):
-    index, even = position("gx")
-    faces_of(start, 1, even, face, z_send)
+def first_sweep_kernel(wave_ref, count_ref, cells_ref, start, sigma_h, sigma_v, e_out, src, field, twist):
+    index, _ = position("gx")
     layers, size_y, size_z = sigma_h.shape
     wave = wave_ref[...]
     edge = jnp.where(index > 0, 1.0, 0.0)
@@ -227,10 +217,8 @@
         src[layer] = gain * counts[layer * size_y : (layer + 1) * size_y]
 
 
-def first_adjoint_kernel(wave_ref, adjoint, sigma_h, sigma_v, a_out, p_send, z_send, field, twist, face):
-    index, even = position("gx")
-    faces_of(adjoint, 0, even, face, p_send)
-    faces_of(adjoint, 1, even, face, z_send)
+def first_adjoint_kernel(wave_ref, adjoint, sigma_h, sigma_v, a_out, field, twist):
+    index, _ = position("gx")
     layers, size_y, _ = sigma_h.shape
     edge = jnp.where(index > 0, 1.0, 0.0)
     zero_layer(field, layers, size_y)
@@ -473,24 +461,20 @@
     face = (2, 3) + plane
     body = (layers,) + face
     more = (layers + 1,) + face
-    hbm = pl.BlockSpec(memory_space=pltpu.HBM)
-
-    (e_p,) = call(
-        first_faces_kernel,
-        "first_faces",
-        [hbm],
-        [half],
-        [pltpu.VMEM(face, jnp.bfloat16), face, pltpu.SemaphoreType.DMA],
-    )(start)
+
+    count = tx_count[None]
+    e_p, e_z = call(faces_kernel, "first_faces", [VMEM], [half] * 2, [face])(start)
     e_p_in = swap(e_p, 0)
-    e1, src, e_z = call(
+    a_p, a_z = call(faces_kernel, "adjoint_faces", [VMEM], [half] * 2, [face])(adjoint)
+    e_z, a_p, a_z, wave, count, e1_start = lax.optimization_barrier((e_z, a_p, a_z, wave, count, start))
+    e_z_in = swap(e_z, 1)
+    e1, src = call(
         first_sweep_kernel,
         "first_sweep",
         [VMEM] * 6,
-        [body, (layers,) + plane, half],
-        [more, more, face],
-    )(wave, tx_count[None], tx_cells[None], start, sigma_h, sigma_v)
-    e_z_in = swap(e_z, 1)
+        [body, (layers,) + plane],
+        [more, more],
+    )(wave, count, tx_cells[None], e1_start, sigma_h, sigma_v)
 
     def second(side, halo):
         return call(
@@ -503,9 +487,9 @@
     e1_p, e1_p_out = second(0, e_p_in)
     e1_p_in = swap(e1_p_out, 0)
     adjoint, e1_p = lax.optimization_barrier((adjoint, e1_p))
-    a1, a_p, a_z = call(
-        first_adjoint_kernel, "first_adjoint", [VMEM] * 4, [body, half, half], [more, more, face]
-    )(wave, adjoint, sigma_h, sigma_v)
+    (a1,) = call(first_adjoint_kernel, "first_adjoint", [VMEM] * 4, [body], [more, more])(
+        wave, adjoint, sigma_h, sigma_v
+    )
     a1, e_z_in = lax.optimization_barrier((a1, e_z_in))
     e1_z, e1_z_out = second(1, e_z_in)
     a_p, a_z, e1_z_out = lax.optimization_barrier((a_p, a_z, e1_z_out))

time: 78.6 us -> 80.6 us (1.025)
  the two profiles are of different devices: /device:TPU:384 before, /device:TPU:96 now
where the time goes in v7:
time: 80.6 us; the launch traced here: 80.1 us
  starting transfers between devices  28.6 us (35%)
  blocking collectives  22.1 us (27%)
  waiting for transfers between devices  13 us (16%)
  Pallas kernels  10.6 us (13%)
  local copies, waits for them, and re-layouts  2.98 us (4%)
  between operations  2.16 us (3%)
    ppermute x8, starting transfers between devices, swap(): return lax.ppermute(values, 'gx', swaps[side])  28.6 us
    all_to_all x1, blocking collectives, on_device(): gathered = lax.all_to_all(terms, 'freq', 0, 0)  22.1 us
    ppermute x8, waiting for transfers between devices, swap(): return lax.ppermute(values, 'gx', swaps[side])  13 us
    pallas_call x1, Pallas kernels, on_device(): call(last_sweep_kernel, 'last_sweep', [VMEM] * 10, [(2, 3, layers) + plan...  3.1 us
    unnamed x14, local copies, waits for them, and re-layouts  2.98 us
    pallas_call x1, Pallas kernels, on_device(): call(second_sweep_kernel, 'second_sweep', [VMEM] * 9, [body, body], [more...  1.97 us
    pallas_call x1, Pallas kernels, on_device(): call(first_sweep_kernel, 'first_sweep', [VMEM] * 6, [body, (layers,) + pl...  1.78 us
    pallas_call x1, Pallas kernels, on_device(): call(first_adjoint_kernel, 'first_adjoint', [VMEM] * 4, [body], [more, mo...  1.63 us
  transfers between devices with their start and end apart: 8, of which 4 were waited for; matrix products, arithmetic and copies ran while one was open for 0% of the time, Pallas kernels for 12%

profile of v7, /device:TPU:96, one launch (start us, length us, event | category | flops | bytes accessed | tf_op | source)
XLA Modules:
  0.0 80.1 jit_solution(15157823040337084869)
XLA Ops:
  0.6 0.0 copy-start.1
  0.6 0.0 copy-start
  0.6 0.0 copy-start.3
  0.7 1.2 %copy-done.3 = bf16[1,2,3,4,64,256]{5,4,3,2,1,0:T(8,128)(2,1)S(1)} copy-done((bf16[1,2,3,4,64,256]{5,4,3,2,1,0:T(8,128)(2,1)S(1)}, bf16[1,2,3,4,64,256]{5,4,3,2,1,0:T(8,128)(2,1)}, u32[]{:S(2)}) %copy-start.3) | copy-done | bytes 786456
  1.8 0.0 copy-start.4
  1.8 0.2 first_faces.1
  2.0 3.5 %collective-permute-start = (f32[2,2,64,256]{3,2,1,0:T(8,128)S(1)}, f32[2,2,64,256]{3,2,1,0:T(8,128)S(1)}, u32[]{:S(2)}, u32[]{:S(2)}) collective-permute-start(f32[2,2,64,256]{3,2,1,0:T(8,128)S(1)} %get-tuple-element.47), channel_id=1, source_target_pairs={{0,1},{2,3},{4,5},{6,7},{8,9},{10,11},{12,13},{14,15},{16,17},{18,... | collective-permute-start | bytes 786440 | tf_op jit(solution)/shard_map/ppermute | solution.py:457
  5.6 0.0 copy-start.5
  5.6 1.1 %copy-done.5 = bf16[1,2,3,4,64,256]{5,4,3,2,1,0:T(8,128)(2,1)S(1)} copy-done((bf16[1,2,3,4,64,256]{5,4,3,2,1,0:T(8,128)(2,1)S(1)}, bf16[1,2,3,4,64,256]{5,4,3,2,1,0:T(8,128)(2,1)}, u32[]{:S(2)}) %copy-start.5) | copy-done | bytes 786456
  6.7 0.2 adjoint_faces.1
  6.9 2.0 %collective-permute-start.1 = (f32[2,2,64,256]{3,2,1,0:T(8,128)S(1)}, f32[2,2,64,256]{3,2,1,0:T(8,128)S(1)}, u32[]{:S(2)}, u32[]{:S(2)}) collective-permute-start(f32[2,2,64,256]{3,2,1,0:T(8,128)S(1)} %get-tuple-element.53), channel_id=1, source_target_pairs={{1,2},{3,4},{5,6},{7,8},{9,10},{11,12},{13,14},{15,16},{17,18},{19... | collective-permute-start | bytes 786440 | tf_op jit(solution)/shard_map/ppermute | solution.py:457
  10.2 0.0 copy-done.1
  10.2 0.0 copy-done
  10.2 0.0 copy-done.4
  10.2 0.0 copy-start.6
  10.2 0.6 copy-done.6
  10.9 1.8 %first_sweep.1 = (f32[4,2,3,64,256]{4,3,2,1,0:T(8,128)S(1)}, f32[4,64,256]{2,1,0:T(8,128)S(1)}) custom-call(f32[1,1]{1,0:T(1,128)} %bitcast.7.wave_ref, s32[1,1]{1,0:T(1,128)} %bitcast.16.count_ref, s32[1,64]{1,0:T(1,128)S(1)} %bitcast.25, bf16[2,3,4,64,256]{4,3,2,1,0:T(8,128)(2,1)S(1)} %bitcast.22, f32[4,64,256]{2,1,0:T(8,128)S(1)} %copy-done, ...), custom_call_target="tpu_custom_call" | custom-call | tf_op jit(solution)/shard_map/first_sweep/pallas_call | solution.py:471
  12.7 5.1 %collective-permute-done.refs_1_ = f32[2,2,64,256]{3,2,1,0:T(8,128)S(1)} collective-permute-done((f32[2,2,64,256]{3,2,1,0:T(8,128)S(1)}, f32[2,2,64,256]{3,2,1,0:T(8,128)S(1)}, u32[]{:S(2)}, u32[]{:S(2)}) %collective-permute-start) | collective-permute-done | bytes 262176 | tf_op jit(solution)/shard_map/ppermute | solution.py:457
  17.7 0.3 second_faces_0.1
  18.0 1.9 %collective-permute-start.2 = (f32[2,2,64,256]{3,2,1,0:T(8,128)S(1)}, f32[2,2,64,256]{3,2,1,0:T(8,128)S(1)}, u32[]{:S(2)}, u32[]{:S(2)}) collective-permute-start(f32[2,2,64,256]{3,2,1,0:T(8,128)S(1)} %get-tuple-element.56), channel_id=1, source_target_pairs={{0,1},{2,3},{4,5},{6,7},{8,9},{10,11},{12,13},{14,15},{16,17},{18,... | collective-permute-start | bytes 786440 | tf_op jit(solution)/shard_map/ppermute | solution.py:457
  19.9 1.6 %first_adjoint.1.a_part.refs_4_ = f32[4,2,3,64,256]{4,3,2,1,0:T(8,128)S(1)} custom-call(f32[1,1]{1,0:T(1,128)} %bitcast.9.wave_ref, bf16[2,3,4,64,256]{4,3,2,1,0:T(8,128)(2,1)S(1)} %bitcast.24, f32[4,64,256]{2,1,0:T(8,128)S(1)} %copy-done, f32[4,64,256]{2,1,0:T(8,128)S(1)} %copy-done.1), custom_call_target="tpu_custom_call" | custom-call | tf_op jit(solution)/shard_map/first_adjoint/pallas_call | solution.py:490
  21.5 0.0 copy-start.2
  21.6 0.0 collective-permute-done.1.refs_1_
  21.6 0.3 second_faces_1.1
  21.8 3.5 %collective-permute-start.4 = (f32[2,2,64,256]{3,2,1,0:T(8,128)S(1)}, f32[2,2,64,256]{3,2,1,0:T(8,128)S(1)}, u32[]{:S(2)}, u32[]{:S(2)}) collective-permute-start(f32[2,2,64,256]{3,2,1,0:T(8,128)S(1)} %get-tuple-element.67), channel_id=1, source_target_pairs={{1,2},{3,4},{5,6},{7,8},{9,10},{11,12},{13,14},{15,16},{17,18},{19... | collective-permute-start | bytes 786440 | tf_op jit(solution)/shard_map/ppermute | solution.py:457
  25.3 3.3 %collective-permute-start.5 = (f32[2,2,64,256]{3,2,1,0:T(8,128)S(1)}, f32[2,2,64,256]{3,2,1,0:T(8,128)S(1)}, u32[]{:S(2)}, u32[]{:S(2)}) collective-permute-start(f32[2,2,64,256]{3,2,1,0:T(8,128)S(1)} %get-tuple-element.68), channel_id=1, source_target_pairs={{1,2},{3,4},{5,6},{7,8},{9,10},{11,12},{13,14},{15,16},{17,18},{19... | collective-permute-start | bytes 786440 | tf_op jit(solution)/shard_map/ppermute | solution.py:457
  28.6 5.1 %collective-permute-start.3 = (f32[2,2,64,256]{3,2,1,0:T(8,128)S(1)}, f32[2,2,64,256]{3,2,1,0:T(8,128)S(1)}, u32[]{:S(2)}, u32[]{:S(2)}) collective-permute-start(f32[2,2,64,256]{3,2,1,0:T(8,128)S(1)} %get-tuple-element.61), channel_id=1, source_target_pairs={{0,1},{2,3},{4,5},{6,7},{8,9},{10,11},{12,13},{14,15},{16,17},{18,... | collective-permute-start | bytes 786440 | tf_op jit(solution)/shard_map/ppermute | solution.py:457
  33.7 4.2 %collective-permute-done.2.refs_1_ = f32[2,2,64,256]{3,2,1,0:T(8,128)S(1)} collective-permute-done((f32[2,2,64,256]{3,2,1,0:T(8,128)S(1)}, f32[2,2,64,256]{3,2,1,0:T(8,128)S(1)}, u32[]{:S(2)}, u32[]{:S(2)}) %collective-permute-start.2) | collective-permute-done | bytes 262176 | tf_op jit(solution)/shard_map/ppermute | solution.py:457
  37.9 0.0 copy-done.2
  37.9 2.0 %second_sweep.1 = (f32[4,2,3,64,256]{4,3,2,1,0:T(8,128)S(1)}, f32[4,2,3,64,256]{4,3,2,1,0:T(8,128)S(1)}) custom-call(f32[1,1]{1,0:T(1,128)} %bitcast.11.wave_ref, f32[4,2,3,64,256]{4,3,2,1,0:T(8,128)S(1)} %get-tuple-element.50.refs_2_.e_body, f32[2,3,64,256]{3,2,1,0:T(8,128)S(1)} %get-tuple-element.62.e_p, f32[2,3,64,256]{3,2,1,0:T(8,128)S(1)} %get-tuple-element.63.e_z, ...), custom_call_target="tpu_custom_call" | custom-call | tf_op jit(solution)/shard_map/second_sweep/pallas_call | solution.py:500
  39.9 0.0 collective-permute-done.4.refs_1_
  39.9 0.0 collective-permute-done.5.refs_2_
  39.9 0.4 third_faces_1.1
  40.3 5.0 %collective-permute-start.7 = (f32[2,2,64,256]{3,2,1,0:T(8,128)S(1)}, f32[2,2,64,256]{3,2,1,0:T(8,128)S(1)}, u32[]{:S(2)}, u32[]{:S(2)}) collective-permute-start(f32[2,2,64,256]{3,2,1,0:T(8,128)S(1)} %get-tuple-element.79), channel_id=1, source_target_pairs={{1,2},{3,4},{5,6},{7,8},{9,10},{11,12},{13,14},{15,16},{17,18},{19... | collective-permute-start | bytes 786440 | tf_op jit(solution)/shard_map/ppermute | solution.py:457
  45.4 0.6 collective-permute-done.3.refs_2_
  45.9 0.4 third_faces_0.1
  46.3 4.3 %collective-permute-start.6 = (f32[2,2,64,256]{3,2,1,0:T(8,128)S(1)}, f32[2,2,64,256]{3,2,1,0:T(8,128)S(1)}, u32[]{:S(2)}, u32[]{:S(2)}) collective-permute-start(f32[2,2,64,256]{3,2,1,0:T(8,128)S(1)} %get-tuple-element.70), channel_id=1, source_target_pairs={{0,1},{2,3},{4,5},{6,7},{8,9},{10,11},{12,13},{14,15},{16,17},{18,... | collective-permute-start | bytes 786440 | tf_op jit(solution)/shard_map/ppermute | solution.py:457
  50.6 3.1 %last_sweep.1 = (f32[2,3,4,64,256]{4,3,2,1,0:T(8,128)}, f32[2,2,3,64,256]{4,3,2,1,0:T(8,128)S(1)}, f32[16,2,2,4,256]{4,3,2,1,0:T(4,128)S(1)}) custom-call(f32[1,1]{1,0:T(1,128)} %bitcast.14.wave_ref, f32[4,2,3,64,256]{4,3,2,1,0:T(8,128)S(1)} %get-tuple-element.69.refs_3_.e_body, f32[2,3,64,256]{3,2,1,0:T(8,128)S(1)} %get-tuple-element.71.e_p, ...), custom_call_target="tpu_custom_call" | custom-call | tf_op jit(solution)/shard_map/last_sweep/pallas_call | solution.py:519
  53.7 0.0 collective-permute-done.7.halo_z
  53.7 3.2 %collective-permute-done.6.halo_p = f32[2,2,64,256]{3,2,1,0:T(8,128)S(1)} collective-permute-done((f32[2,2,64,256]{3,2,1,0:T(8,128)S(1)}, f32[2,2,64,256]{3,2,1,0:T(8,128)S(1)}, u32[]{:S(2)}, u32[]{:S(2)}) %collective-permute-start.6) | collective-permute-done | bytes 262176 | tf_op jit(solution)/shard_map/ppermute | solution.py:457
  56.9 0.4 gradient.1
  57.3 22.1 %all_to_all.5 = f32[16,2,4,4,256]{4,3,2,1,0:T(4,128)S(1)} all-to-all(f32[16,2,4,4,256]{4,3,2,1,0:T(4,128)S(1)} %gradient.1), channel_id=1, replica_groups=mesh['freq'=16,'gx'=32] {'freq'}, dimensions={0} | all-to-all | bytes 1048576 | tf_op jit(solution)/shard_map/all_to_all | solution.py:530
  79.4 0.7 reduce_sum.9
Async XLA Ops:
  0.6 9.6 %copy-start.1 = (f32[4,64,256]{2,1,0:T(8,128)S(1)}, f32[4,64,256]{2,1,0:T(8,128)}, u32[]{:S(2)}) copy-start(f32[4,64,256]{2,1,0:T(8,128)} %sigma_v.9) | copy-start | bytes 786436
  0.6 9.6 %copy-start = (f32[4,64,256]{2,1,0:T(8,128)S(1)}, f32[4,64,256]{2,1,0:T(8,128)}, u32[]{:S(2)}) copy-start(f32[4,64,256]{2,1,0:T(8,128)} %sigma_h.9) | copy-start | bytes 786436
  0.6 1.2 %copy-start.3 = (bf16[1,2,3,4,64,256]{5,4,3,2,1,0:T(8,128)(2,1)S(1)}, bf16[1,2,3,4,64,256]{5,4,3,2,1,0:T(8,128)(2,1)}, u32[]{:S(2)}) copy-start(bf16[1,2,3,4,64,256]{5,4,3,2,1,0:T(8,128)(2,1)} %param.11) | copy-start | bytes 2359300
  1.8 8.4 %copy-start.4 = (bf16[1,2,3,4,64,256]{5,4,3,2,1,0:T(8,128)(2,1)S(1)}, bf16[1,2,3,4,64,256]{5,4,3,2,1,0:T(8,128)(2,1)}, u32[]{:S(2)}) copy-start(bf16[1,2,3,4,64,256]{5,4,3,2,1,0:T(8,128)(2,1)} %param.11) | copy-start | bytes 2359300
  2.0 15.7 %collective-permute-start = (f32[2,2,64,256]{3,2,1,0:T(8,128)S(1)}, f32[2,2,64,256]{3,2,1,0:T(8,128)S(1)}, u32[]{:S(2)}, u32[]{:S(2)}) collective-permute-start(f32[2,2,64,256]{3,2,1,0:T(8,128)S(1)} %get-tuple-element.47), channel_id=1, source_target_pairs={{0,1},{2,3},{4,5},{6,7},{8,9},{10,11},{12,13},{14,15},{16,17},{18,... | collective-permute-start | bytes 786440 | tf_op jit(solution)/shard_map/ppermute | solution.py:457
  5.6 1.1 %copy-start.5 = (bf16[1,2,3,4,64,256]{5,4,3,2,1,0:T(8,128)(2,1)S(1)}, bf16[1,2,3,4,64,256]{5,4,3,2,1,0:T(8,128)(2,1)}, u32[]{:S(2)}) copy-start(bf16[1,2,3,4,64,256]{5,4,3,2,1,0:T(8,128)(2,1)} %param.12) | copy-start | bytes 2359300
  6.9 14.7 %collective-permute-start.1 = (f32[2,2,64,256]{3,2,1,0:T(8,128)S(1)}, f32[2,2,64,256]{3,2,1,0:T(8,128)S(1)}, u32[]{:S(2)}, u32[]{:S(2)}) collective-permute-start(f32[2,2,64,256]{3,2,1,0:T(8,128)S(1)} %get-tuple-element.53), channel_id=1, source_target_pairs={{1,2},{3,4},{5,6},{7,8},{9,10},{11,12},{13,14},{15,16},{17,18},{19... | collective-permute-start | bytes 786440 | tf_op jit(solution)/shard_map/ppermute | solution.py:457
  10.2 0.7 copy-start.6
  18.0 19.9 %collective-permute-start.2 = (f32[2,2,64,256]{3,2,1,0:T(8,128)S(1)}, f32[2,2,64,256]{3,2,1,0:T(8,128)S(1)}, u32[]{:S(2)}, u32[]{:S(2)}) collective-permute-start(f32[2,2,64,256]{3,2,1,0:T(8,128)S(1)} %get-tuple-element.56), channel_id=1, source_target_pairs={{0,1},{2,3},{4,5},{6,7},{8,9},{10,11},{12,13},{14,15},{16,17},{18,... | collective-permute-start | bytes 786440 | tf_op jit(solution)/shard_map/ppermute | solution.py:457
  21.5 16.4 %copy-start.2 = (bf16[1,2,3,4,64,256]{5,4,3,2,1,0:T(8,128)(2,1)S(1)}, bf16[1,2,3,4,64,256]{5,4,3,2,1,0:T(8,128)(2,1)}, u32[]{:S(2)}) copy-start(bf16[1,2,3,4,64,256]{5,4,3,2,1,0:T(8,128)(2,1)} %param.13) | copy-start | bytes 2359300
  21.8 18.1 %collective-permute-start.4 = (f32[2,2,64,256]{3,2,1,0:T(8,128)S(1)}, f32[2,2,64,256]{3,2,1,0:T(8,128)S(1)}, u32[]{:S(2)}, u32[]{:S(2)}) collective-permute-start(f32[2,2,64,256]{3,2,1,0:T(8,128)S(1)} %get-tuple-element.67), channel_id=1, source_target_pairs={{1,2},{3,4},{5,6},{7,8},{9,10},{11,12},{13,14},{15,16},{17,18},{19... | collective-permute-start | bytes 786440 | tf_op jit(solution)/shard_map/ppermute | solution.py:457
  25.3 14.6 %collective-permute-start.5 = (f32[2,2,64,256]{3,2,1,0:T(8,128)S(1)}, f32[2,2,64,256]{3,2,1,0:T(8,128)S(1)}, u32[]{:S(2)}, u32[]{:S(2)}) collective-permute-start(f32[2,2,64,256]{3,2,1,0:T(8,128)S(1)} %get-tuple-element.68), channel_id=1, source_target_pairs={{1,2},{3,4},{5,6},{7,8},{9,10},{11,12},{13,14},{15,16},{17,18},{19... | collective-permute-start | bytes 786440 | tf_op jit(solution)/shard_map/ppermute | solution.py:457
  28.6 17.3 %collective-permute-start.3 = (f32[2,2,64,256]{3,2,1,0:T(8,128)S(1)}, f32[2,2,64,256]{3,2,1,0:T(8,128)S(1)}, u32[]{:S(2)}, u32[]{:S(2)}) collective-permute-start(f32[2,2,64,256]{3,2,1,0:T(8,128)S(1)} %get-tuple-element.61), channel_id=1, source_target_pairs={{0,1},{2,3},{4,5},{6,7},{8,9},{10,11},{12,13},{14,15},{16,17},{18,... | collective-permute-start | bytes 786440 | tf_op jit(solution)/shard_map/ppermute | solution.py:457
  40.3 13.4 %collective-permute-start.7 = (f32[2,2,64,256]{3,2,1,0:T(8,128)S(1)}, f32[2,2,64,256]{3,2,1,0:T(8,128)S(1)}, u32[]{:S(2)}, u32[]{:S(2)}) collective-permute-start(f32[2,2,64,256]{3,2,1,0:T(8,128)S(1)} %get-tuple-element.79), channel_id=1, source_target_pairs={{1,2},{3,4},{5,6},{7,8},{9,10},{11,12},{13,14},{15,16},{17,18},{19... | collective-permute-start | bytes 786440 | tf_op jit(solution)/shard_map/ppermute | solution.py:457
  46.3 10.6 %collective-permute-start.6 = (f32[2,2,64,256]{3,2,1,0:T(8,128)S(1)}, f32[2,2,64,256]{3,2,1,0:T(8,128)S(1)}, u32[]{:S(2)}, u32[]{:S(2)}) collective-permute-start(f32[2,2,64,256]{3,2,1,0:T(8,128)S(1)} %get-tuple-element.70), channel_id=1, source_target_pairs={{0,1},{2,3},{4,5},{6,7},{8,9},{10,11},{12,13},{14,15},{16,17},{18,... | collective-permute-start | bytes 786440 | tf_op jit(solution)/shard_map/ppermute | solution.py:457

commit v8 on v7

--- a/solution.py
+++ b/solution.py
@@ -181,12 +181,17 @@
     write_faces(face, out, right, size_y)
 
 
-def first_sweep_kernel(wave_ref, count_ref, cells_ref, start, sigma_h, sigma_v, e_out, src, field, twist):
+def source_kernel(wave_ref, count_ref, cells_ref, src):
+    index, _ = position("gx")
+    layers, size_y, _ = src.shape
+    add_slots(wave_ref[...], count_ref[...], cells_ref[...], index * (layers * size_y), src)
+
+
+def first_sweep_kernel(wave_ref, src, start, sigma_h, sigma_v, e_out, field, twist):
     index, _ = position("gx")
     layers, size_y, size_z = sigma_h.shape
     wave = wave_ref[...]
     edge = jnp.where(index > 0, 1.0, 0.0)
-    add_slots(wave, count_ref[...], cells_ref[...], index * (layers * size_y), src)
 
     def source(part, comp, layer, rows):
         return src[layer, rows] if part == 1 and comp == 0 else None
@@ -462,19 +467,17 @@
     body = (layers,) + face
     more = (layers + 1,) + face
 
-    count = tx_count[None]
     e_p, e_z = call(faces_kernel, "first_faces", [VMEM], [half] * 2, [face])(start)
     e_p_in = swap(e_p, 0)
     a_p, a_z = call(faces_kernel, "adjoint_faces", [VMEM], [half] * 2, [face])(adjoint)
-    e_z, a_p, a_z, wave, count, e1_start = lax.optimization_barrier((e_z, a_p, a_z, wave, count, start))
+    (src,) = call(source_kernel, "source", [VMEM] * 3, [(layers,) + plane])(
+        wave, tx_count[None], tx_cells[None]
+    )
+    e_z, a_p, a_z, src, e1_start = lax.optimization_barrier((e_z, a_p, a_z, src, start))
     e_z_in = swap(e_z, 1)
-    e1, src = call(
-        first_sweep_kernel,
-        "first_sweep",
-        [VMEM] * 6,
-        [body, (layers,) + plane],
-        [more, more],
-    )(wave, count, tx_cells[None], e1_start, sigma_h, sigma_v)
+    (e1,) = call(first_sweep_kernel, "first_sweep", [VMEM] * 5, [body], [more, more])(
+        wave, src, e1_start, sigma_h, sigma_v
+    )
 
     def second(side, halo):
         return call(
@@ -492,15 +495,15 @@
     )
     a1, e_z_in = lax.optimization_barrier((a1, e_z_in))
     e1_z, e1_z_out = second(1, e_z_in)
-    a_p, a_z, e1_z_out = lax.optimization_barrier((a_p, a_z, e1_z_out))
+    a_p, e1_z_out = lax.optimization_barrier((a_p, e1_z_out))
     e1_z_in = swap(e1_z_out, 1)
-    a_z_in = swap(a_z, 1)
-    e1_z, e1_p_in = lax.optimization_barrier((e1_z, e1_p_in))
     a_p_in = swap(a_p, 0)
+    e1_z, e1_z_in, e1_p_in = lax.optimization_barrier((e1_z, e1_z_in, e1_p_in))
     e2, a1_body = call(
         second_sweep_kernel, "second_sweep", [VMEM] * 9, [body, body], [more, more]
     )(wave, e1, e1_p, e1_z, a1, src, seen, sigma_h, sigma_v)
-    e2, e1_z_in, a_z_in = lax.optimization_barrier((e2, e1_z_in, a_z_in))
+    e2, a_z = lax.optimization_barrier((e2, a_z))
+    a_z_in = swap(a_z, 1)
 
     def third(side, e_halo, a_halo):
         return call(
@@ -510,10 +513,11 @@
             [face, face, half],
         )(wave, e_halo, a_halo, e2, a1, seen, sigma_h, sigma_v)
 
+    e2_p, a1_p, a1_p_out = third(0, e1_p_in, a_p_in)
+    a1_p_in = swap(a1_p_out, 0)
+    a1_p, a_z_in = lax.optimization_barrier((a1_p, a_z_in))
     e2_z, a1_z, a1_z_out = third(1, e1_z_in, a_z_in)
     a1_z_in = swap(a1_z_out, 1)
-    e2_p, a1_p, a1_p_out = third(0, e1_p_in, a_p_in)
-    a1_p_in = swap(a1_p_out, 0)
     inner_blocks = (freqs, 2, layers - 2, share, size_z)
     blocks = (freqs, 2, layers, share, size_z)
     final, faces, inner = call(
@@ -523,7 +527,7 @@
         [(2, 3, layers) + plane, (2,) + face, inner_blocks],
         [more, more],
     )(wave, e2, e2_p, e2_z, a1_body, a1_p, a1_z, seen, sigma_h, sigma_v)
-    faces, a1_z_in = lax.optimization_barrier((faces, a1_z_in))
+    faces, a1_p_in = lax.optimization_barrier((faces, a1_p_in))
     (terms,) = call(gradient_kernel, "gradient", [VMEM] * 9, [blocks])(
         wave, a1_p_in, a1_z_in, e2_p, e2_z, faces, inner, sigma_h, sigma_v
     )

time: 80.6 us -> 75.4 us (0.935)
  the two profiles are of different devices: /device:TPU:96 before, /device:TPU:384 now
where the time goes in v8:
time: 75.4 us; the launch traced here: 74.9 us
  starting transfers between devices  25.8 us (34%)
  blocking collectives  18.9 us (25%)
  waiting for transfers between devices  14.3 us (19%)
  Pallas kernels  10.7 us (14%)
  local copies, waits for them, and re-layouts  2.34 us (3%)
  between operations  2.17 us (3%)
    ppermute x8, starting transfers between devices, swap(): return lax.ppermute(values, 'gx', swaps[side])  25.8 us
    all_to_all x1, blocking collectives, on_device(): gathered = lax.all_to_all(terms, 'freq', 0, 0)  18.9 us
    ppermute x8, waiting for transfers between devices, swap(): return lax.ppermute(values, 'gx', swaps[side])  14.3 us
    pallas_call x1, Pallas kernels, on_device(): call(last_sweep_kernel, 'last_sweep', [VMEM] * 10, [(2, 3, layers) + plan...  3.1 us
    unnamed x16, local copies, waits for them, and re-layouts  2.34 us
    pallas_call x1, Pallas kernels, on_device(): call(second_sweep_kernel, 'second_sweep', [VMEM] * 9, [body, body], [more...  1.97 us
    pallas_call x1, Pallas kernels, on_device(): call(first_sweep_kernel, 'first_sweep', [VMEM] * 5, [body], [more, more])  1.65 us
    pallas_call x1, Pallas kernels, on_device(): call(first_adjoint_kernel, 'first_adjoint', [VMEM] * 4, [body], [more, mo...  1.63 us
  transfers between devices with their start and end apart: 8, of which 4 were waited for; matrix products, arithmetic and copies ran while one was open for 0% of the time, Pallas kernels for 13%

profile of v8, /device:TPU:384, one launch (start us, length us, event | category | flops | bytes accessed | tf_op | source)
XLA Modules:
  0.0 74.9 jit_solution(600247202702401116)
XLA Ops:
  0.6 0.0 copy-start.1
  0.6 0.0 copy-start
  0.6 0.0 copy-start.5
  0.7 1.2 %copy-done.5 = bf16[1,2,3,4,64,256]{5,4,3,2,1,0:T(8,128)(2,1)S(1)} copy-done((bf16[1,2,3,4,64,256]{5,4,3,2,1,0:T(8,128)(2,1)S(1)}, bf16[1,2,3,4,64,256]{5,4,3,2,1,0:T(8,128)(2,1)}, u32[]{:S(2)}) %copy-start.5) | copy-done | bytes 786456
  1.8 0.0 copy-start.7
  1.8 0.2 first_faces.1
  2.0 3.4 %collective-permute-start = (f32[2,2,64,256]{3,2,1,0:T(8,128)S(1)}, f32[2,2,64,256]{3,2,1,0:T(8,128)S(1)}, u32[]{:S(2)}, u32[]{:S(2)}) collective-permute-start(f32[2,2,64,256]{3,2,1,0:T(8,128)S(1)} %get-tuple-element.46), channel_id=1, source_target_pairs={{0,1},{2,3},{4,5},{6,7},{8,9},{10,11},{12,13},{14,15},{16,17},{18,... | collective-permute-start | bytes 786440 | tf_op jit(solution)/shard_map/ppermute | solution.py:462
  6.7 0.0 copy-start.3
  6.7 1.1 %copy-done.3 = bf16[1,2,3,4,64,256]{5,4,3,2,1,0:T(8,128)(2,1)S(1)} copy-done((bf16[1,2,3,4,64,256]{5,4,3,2,1,0:T(8,128)(2,1)S(1)}, bf16[1,2,3,4,64,256]{5,4,3,2,1,0:T(8,128)(2,1)}, u32[]{:S(2)}) %copy-start.3) | copy-done | bytes 786456
  7.9 0.0 copy-start.6
  7.9 0.2 adjoint_faces.1
  8.1 0.0 copy-done.7
  8.1 0.2 source.1.src
  8.3 4.1 %collective-permute-start.1 = (f32[2,2,64,256]{3,2,1,0:T(8,128)S(1)}, f32[2,2,64,256]{3,2,1,0:T(8,128)S(1)}, u32[]{:S(2)}, u32[]{:S(2)}) collective-permute-start(f32[2,2,64,256]{3,2,1,0:T(8,128)S(1)} %get-tuple-element.50), channel_id=1, source_target_pairs={{1,2},{3,4},{5,6},{7,8},{9,10},{11,12},{13,14},{15,16},{17,18},{19... | collective-permute-start | bytes 786440 | tf_op jit(solution)/shard_map/ppermute | solution.py:462
  12.4 0.0 copy-done.1
  12.4 0.0 copy-done
  12.4 0.0 copy-done.6
  12.4 1.6 %first_sweep.1.refs_2_.e_body = f32[4,2,3,64,256]{4,3,2,1,0:T(8,128)S(1)} custom-call(f32[1,1]{1,0:T(1,128)} %bitcast.8.wave_ref, f32[4,64,256]{2,1,0:T(8,128)S(1)} %source.1.src, bf16[2,3,4,64,256]{4,3,2,1,0:T(8,128)(2,1)S(1)} %bitcast.25, f32[4,64,256]{2,1,0:T(8,128)S(1)} %copy-done, f32[4,64,256]{2,1,0:T(8,128)S(1)} %copy-done.1), custom_call_target="tpu_custom_call" | custom-call | tf_op jit(solution)/shard_map/first_sweep/pallas_call | solution.py:478
  14.1 0.0 copy-start.4
  14.1 0.0 collective-permute-done.refs_1_
  14.1 0.3 second_faces_0.1
  14.4 2.2 %collective-permute-start.3 = (f32[2,2,64,256]{3,2,1,0:T(8,128)S(1)}, f32[2,2,64,256]{3,2,1,0:T(8,128)S(1)}, u32[]{:S(2)}, u32[]{:S(2)}) collective-permute-start(f32[2,2,64,256]{3,2,1,0:T(8,128)S(1)} %get-tuple-element.56), channel_id=1, source_target_pairs={{0,1},{2,3},{4,5},{6,7},{8,9},{10,11},{12,13},{14,15},{16,17},{18,... | collective-permute-start | bytes 786440 | tf_op jit(solution)/shard_map/ppermute | solution.py:462
  16.6 0.0 copy-done.4
  16.6 1.6 %first_adjoint.1.a_part.refs_4_ = f32[4,2,3,64,256]{4,3,2,1,0:T(8,128)S(1)} custom-call(f32[1,1]{1,0:T(1,128)} %bitcast.10.wave_ref, bf16[2,3,4,64,256]{4,3,2,1,0:T(8,128)(2,1)S(1)} %bitcast.23, f32[4,64,256]{2,1,0:T(8,128)S(1)} %copy-done, f32[4,64,256]{2,1,0:T(8,128)S(1)} %copy-done.1), custom_call_target="tpu_custom_call" | custom-call | tf_op jit(solution)/shard_map/first_adjoint/pallas_call | solution.py:493
  18.2 0.0 copy-start.2
  18.2 1.9 %collective-permute-done.1.refs_1_ = f32[2,2,64,256]{3,2,1,0:T(8,128)S(1)} collective-permute-done((f32[2,2,64,256]{3,2,1,0:T(8,128)S(1)}, f32[2,2,64,256]{3,2,1,0:T(8,128)S(1)}, u32[]{:S(2)}, u32[]{:S(2)}) %collective-permute-start.1) | collective-permute-done | bytes 262176 | tf_op jit(solution)/shard_map/ppermute | solution.py:462
  20.2 0.3 second_faces_1.1
  20.4 4.1 %collective-permute-start.2 = (f32[2,2,64,256]{3,2,1,0:T(8,128)S(1)}, f32[2,2,64,256]{3,2,1,0:T(8,128)S(1)}, u32[]{:S(2)}, u32[]{:S(2)}) collective-permute-start(f32[2,2,64,256]{3,2,1,0:T(8,128)S(1)} %get-tuple-element.55), channel_id=1, source_target_pairs={{1,2},{3,4},{5,6},{7,8},{9,10},{11,12},{13,14},{15,16},{17,18},{19... | collective-permute-start | bytes 786440 | tf_op jit(solution)/shard_map/ppermute | solution.py:462
  24.5 1.9 %collective-permute-start.4 = (f32[2,2,64,256]{3,2,1,0:T(8,128)S(1)}, f32[2,2,64,256]{3,2,1,0:T(8,128)S(1)}, u32[]{:S(2)}, u32[]{:S(2)}) collective-permute-start(f32[2,2,64,256]{3,2,1,0:T(8,128)S(1)} %get-tuple-element.63), channel_id=1, source_target_pairs={{0,1},{2,3},{4,5},{6,7},{8,9},{10,11},{12,13},{14,15},{16,17},{18,... | collective-permute-start | bytes 786440 | tf_op jit(solution)/shard_map/ppermute | solution.py:462
  26.5 4.8 %collective-permute-done.3.refs_1_ = f32[2,2,64,256]{3,2,1,0:T(8,128)S(1)} collective-permute-done((f32[2,2,64,256]{3,2,1,0:T(8,128)S(1)}, f32[2,2,64,256]{3,2,1,0:T(8,128)S(1)}, u32[]{:S(2)}, u32[]{:S(2)}) %collective-permute-start.3) | collective-permute-done | bytes 262176 | tf_op jit(solution)/shard_map/ppermute | solution.py:462
  31.3 0.0 collective-permute-done.2.refs_1_
  31.3 0.0 copy-done.2
  31.3 2.0 %second_sweep.1 = (f32[4,2,3,64,256]{4,3,2,1,0:T(8,128)S(1)}, f32[4,2,3,64,256]{4,3,2,1,0:T(8,128)S(1)}) custom-call(f32[1,1]{1,0:T(1,128)} %bitcast.12.wave_ref, f32[4,2,3,64,256]{4,3,2,1,0:T(8,128)S(1)} %first_sweep.1.refs_2_.e_body, f32[2,3,64,256]{3,2,1,0:T(8,128)S(1)} %get-tuple-element.48.e_p, f32[2,3,64,256]{3,2,1,0:T(8,128)S(1)} %get-tuple-element.57.e_z, ...), custom_call_target="tpu_custom_call" | custom-call | tf_op jit(solution)/shard_map/second_sweep/pallas_call | solution.py:502
  33.3 4.1 %collective-permute-start.5 = (f32[2,2,64,256]{3,2,1,0:T(8,128)S(1)}, f32[2,2,64,256]{3,2,1,0:T(8,128)S(1)}, u32[]{:S(2)}, u32[]{:S(2)}) collective-permute-start(f32[2,2,64,256]{3,2,1,0:T(8,128)S(1)} %get-tuple-element.67), channel_id=1, source_target_pairs={{1,2},{3,4},{5,6},{7,8},{9,10},{11,12},{13,14},{15,16},{17,18},{19... | collective-permute-start | bytes 786440 | tf_op jit(solution)/shard_map/ppermute | solution.py:462
  37.4 0.0 collective-permute-done.4.refs_2_
  37.4 0.4 third_faces_0.1
  37.8 1.9 %collective-permute-start.6 = (f32[2,2,64,256]{3,2,1,0:T(8,128)S(1)}, f32[2,2,64,256]{3,2,1,0:T(8,128)S(1)}, u32[]{:S(2)}, u32[]{:S(2)}) collective-permute-start(f32[2,2,64,256]{3,2,1,0:T(8,128)S(1)} %get-tuple-element.74), channel_id=1, source_target_pairs={{0,1},{2,3},{4,5},{6,7},{8,9},{10,11},{12,13},{14,15},{16,17},{18,... | collective-permute-start | bytes 786440 | tf_op jit(solution)/shard_map/ppermute | solution.py:462
  39.8 4.0 %collective-permute-done.5.refs_2_ = f32[2,2,64,256]{3,2,1,0:T(8,128)S(1)} collective-permute-done((f32[2,2,64,256]{3,2,1,0:T(8,128)S(1)}, f32[2,2,64,256]{3,2,1,0:T(8,128)S(1)}, u32[]{:S(2)}, u32[]{:S(2)}) %collective-permute-start.5) | collective-permute-done | bytes 262176 | tf_op jit(solution)/shard_map/ppermute | solution.py:462
  43.8 0.4 third_faces_1.1
  44.2 4.1 %collective-permute-start.7 = (f32[2,2,64,256]{3,2,1,0:T(8,128)S(1)}, f32[2,2,64,256]{3,2,1,0:T(8,128)S(1)}, u32[]{:S(2)}, u32[]{:S(2)}) collective-permute-start(f32[2,2,64,256]{3,2,1,0:T(8,128)S(1)} %get-tuple-element.76), channel_id=1, source_target_pairs={{1,2},{3,4},{5,6},{7,8},{9,10},{11,12},{13,14},{15,16},{17,18},{19... | collective-permute-start | bytes 786440 | tf_op jit(solution)/shard_map/ppermute | solution.py:462
  48.3 3.1 %last_sweep.1 = (f32[2,3,4,64,256]{4,3,2,1,0:T(8,128)}, f32[2,2,3,64,256]{4,3,2,1,0:T(8,128)S(1)}, f32[16,2,2,4,256]{4,3,2,1,0:T(4,128)S(1)}) custom-call(f32[1,1]{1,0:T(1,128)} %bitcast.15.wave_ref, f32[4,2,3,64,256]{4,3,2,1,0:T(8,128)S(1)} %get-tuple-element.61.refs_3_.e_body, f32[2,3,64,256]{3,2,1,0:T(8,128)S(1)} %get-tuple-element.64.e_p, ...), custom_call_target="tpu_custom_call" | custom-call | tf_op jit(solution)/shard_map/last_sweep/pallas_call | solution.py:523
  51.4 3.5 %collective-permute-done.6.halo_p = f32[2,2,64,256]{3,2,1,0:T(8,128)S(1)} collective-permute-done((f32[2,2,64,256]{3,2,1,0:T(8,128)S(1)}, f32[2,2,64,256]{3,2,1,0:T(8,128)S(1)}, u32[]{:S(2)}, u32[]{:S(2)}) %collective-permute-start.6) | collective-permute-done | bytes 262176 | tf_op jit(solution)/shard_map/ppermute | solution.py:462
  54.9 0.0 collective-permute-done.7.halo_z
  54.9 0.4 gradient.1
  55.3 18.9 %all_to_all.5 = f32[16,2,4,4,256]{4,3,2,1,0:T(4,128)S(1)} all-to-all(f32[16,2,4,4,256]{4,3,2,1,0:T(4,128)S(1)} %gradient.1), channel_id=1, replica_groups=mesh['freq'=16,'gx'=32] {'freq'}, dimensions={0} | all-to-all | bytes 1048576 | tf_op jit(solution)/shard_map/all_to_all | solution.py:534
  74.2 0.7 reduce_sum.9
Async XLA Ops:
  0.6 11.8 %copy-start.1 = (f32[4,64,256]{2,1,0:T(8,128)S(1)}, f32[4,64,256]{2,1,0:T(8,128)}, u32[]{:S(2)}) copy-start(f32[4,64,256]{2,1,0:T(8,128)} %sigma_v.9) | copy-start | bytes 786436
  0.6 11.8 %copy-start = (f32[4,64,256]{2,1,0:T(8,128)S(1)}, f32[4,64,256]{2,1,0:T(8,128)}, u32[]{:S(2)}) copy-start(f32[4,64,256]{2,1,0:T(8,128)} %sigma_h.9) | copy-start | bytes 786436
  0.6 1.2 %copy-start.5 = (bf16[1,2,3,4,64,256]{5,4,3,2,1,0:T(8,128)(2,1)S(1)}, bf16[1,2,3,4,64,256]{5,4,3,2,1,0:T(8,128)(2,1)}, u32[]{:S(2)}) copy-start(bf16[1,2,3,4,64,256]{5,4,3,2,1,0:T(8,128)(2,1)} %param.11) | copy-start | bytes 2359300
  1.8 6.2 %copy-start.7 = (s32[64]{0:T(128)S(1)}, s32[64]{0:T(128)}, u32[]{:S(2)}) copy-start(s32[64]{0:T(128)} %param.15) | copy-start | bytes 772
  2.0 12.1 %collective-permute-start = (f32[2,2,64,256]{3,2,1,0:T(8,128)S(1)}, f32[2,2,64,256]{3,2,1,0:T(8,128)S(1)}, u32[]{:S(2)}, u32[]{:S(2)}) collective-permute-start(f32[2,2,64,256]{3,2,1,0:T(8,128)S(1)} %get-tuple-element.46), channel_id=1, source_target_pairs={{0,1},{2,3},{4,5},{6,7},{8,9},{10,11},{12,13},{14,15},{16,17},{18,... | collective-permute-start | bytes 786440 | tf_op jit(solution)/shard_map/ppermute | solution.py:462
  6.7 1.1 %copy-start.3 = (bf16[1,2,3,4,64,256]{5,4,3,2,1,0:T(8,128)(2,1)S(1)}, bf16[1,2,3,4,64,256]{5,4,3,2,1,0:T(8,128)(2,1)}, u32[]{:S(2)}) copy-start(bf16[1,2,3,4,64,256]{5,4,3,2,1,0:T(8,128)(2,1)} %param.12) | copy-start | bytes 2359300
  7.9 4.6 %copy-start.6 = (bf16[1,2,3,4,64,256]{5,4,3,2,1,0:T(8,128)(2,1)S(1)}, bf16[1,2,3,4,64,256]{5,4,3,2,1,0:T(8,128)(2,1)}, u32[]{:S(2)}) copy-start(bf16[1,2,3,4,64,256]{5,4,3,2,1,0:T(8,128)(2,1)} %param.11) | copy-start | bytes 2359300
  8.3 11.9 %collective-permute-start.1 = (f32[2,2,64,256]{3,2,1,0:T(8,128)S(1)}, f32[2,2,64,256]{3,2,1,0:T(8,128)S(1)}, u32[]{:S(2)}, u32[]{:S(2)}) collective-permute-start(f32[2,2,64,256]{3,2,1,0:T(8,128)S(1)} %get-tuple-element.50), channel_id=1, source_target_pairs={{1,2},{3,4},{5,6},{7,8},{9,10},{11,12},{13,14},{15,16},{17,18},{19... | collective-permute-start | bytes 786440 | tf_op jit(solution)/shard_map/ppermute | solution.py:462
  14.1 2.5 %copy-start.4 = (bf16[1,2,3,4,64,256]{5,4,3,2,1,0:T(8,128)(2,1)S(1)}, bf16[1,2,3,4,64,256]{5,4,3,2,1,0:T(8,128)(2,1)}, u32[]{:S(2)}) copy-start(bf16[1,2,3,4,64,256]{5,4,3,2,1,0:T(8,128)(2,1)} %param.12) | copy-start | bytes 2359300
  14.4 16.9 %collective-permute-start.3 = (f32[2,2,64,256]{3,2,1,0:T(8,128)S(1)}, f32[2,2,64,256]{3,2,1,0:T(8,128)S(1)}, u32[]{:S(2)}, u32[]{:S(2)}) collective-permute-start(f32[2,2,64,256]{3,2,1,0:T(8,128)S(1)} %get-tuple-element.56), channel_id=1, source_target_pairs={{0,1},{2,3},{4,5},{6,7},{8,9},{10,11},{12,13},{14,15},{16,17},{18,... | collective-permute-start | bytes 786440 | tf_op jit(solution)/shard_map/ppermute | solution.py:462
  18.2 13.1 %copy-start.2 = (bf16[1,2,3,4,64,256]{5,4,3,2,1,0:T(8,128)(2,1)S(1)}, bf16[1,2,3,4,64,256]{5,4,3,2,1,0:T(8,128)(2,1)}, u32[]{:S(2)}) copy-start(bf16[1,2,3,4,64,256]{5,4,3,2,1,0:T(8,128)(2,1)} %param.13) | copy-start | bytes 2359300
  20.4 10.9 %collective-permute-start.2 = (f32[2,2,64,256]{3,2,1,0:T(8,128)S(1)}, f32[2,2,64,256]{3,2,1,0:T(8,128)S(1)}, u32[]{:S(2)}, u32[]{:S(2)}) collective-permute-start(f32[2,2,64,256]{3,2,1,0:T(8,128)S(1)} %get-tuple-element.55), channel_id=1, source_target_pairs={{1,2},{3,4},{5,6},{7,8},{9,10},{11,12},{13,14},{15,16},{17,18},{19... | collective-permute-start | bytes 786440 | tf_op jit(solution)/shard_map/ppermute | solution.py:462
  24.5 12.9 %collective-permute-start.4 = (f32[2,2,64,256]{3,2,1,0:T(8,128)S(1)}, f32[2,2,64,256]{3,2,1,0:T(8,128)S(1)}, u32[]{:S(2)}, u32[]{:S(2)}) collective-permute-start(f32[2,2,64,256]{3,2,1,0:T(8,128)S(1)} %get-tuple-element.63), channel_id=1, source_target_pairs={{0,1},{2,3},{4,5},{6,7},{8,9},{10,11},{12,13},{14,15},{16,17},{18,... | collective-permute-start | bytes 786440 | tf_op jit(solution)/shard_map/ppermute | solution.py:462
  33.3 10.5 %collective-permute-start.5 = (f32[2,2,64,256]{3,2,1,0:T(8,128)S(1)}, f32[2,2,64,256]{3,2,1,0:T(8,128)S(1)}, u32[]{:S(2)}, u32[]{:S(2)}) collective-permute-start(f32[2,2,64,256]{3,2,1,0:T(8,128)S(1)} %get-tuple-element.67), channel_id=1, source_target_pairs={{1,2},{3,4},{5,6},{7,8},{9,10},{11,12},{13,14},{15,16},{17,18},{19... | collective-permute-start | bytes 786440 | tf_op jit(solution)/shard_map/ppermute | solution.py:462
  37.8 17.1 %collective-permute-start.6 = (f32[2,2,64,256]{3,2,1,0:T(8,128)S(1)}, f32[2,2,64,256]{3,2,1,0:T(8,128)S(1)}, u32[]{:S(2)}, u32[]{:S(2)}) collective-permute-start(f32[2,2,64,256]{3,2,1,0:T(8,128)S(1)} %get-tuple-element.74), channel_id=1, source_target_pairs={{0,1},{2,3},{4,5},{6,7},{8,9},{10,11},{12,13},{14,15},{16,17},{18,... | collective-permute-start | bytes 786440 | tf_op jit(solution)/shard_map/ppermute | solution.py:462
  44.2 10.7 %collective-permute-start.7 = (f32[2,2,64,256]{3,2,1,0:T(8,128)S(1)}, f32[2,2,64,256]{3,2,1,0:T(8,128)S(1)}, u32[]{:S(2)}, u32[]{:S(2)}) collective-permute-start(f32[2,2,64,256]{3,2,1,0:T(8,128)S(1)} %get-tuple-element.76), channel_id=1, source_target_pairs={{1,2},{3,4},{5,6},{7,8},{9,10},{11,12},{13,14},{15,16},{17,18},{19... | collective-permute-start | bytes 786440 | tf_op jit(solution)/shard_map/ppermute | solution.py:462

commit v9 on v8

--- a/solution.py
+++ b/solution.py
@@ -356,18 +356,22 @@
     return wave * (terms[0] + terms[1]), wave * terms[2]
 
 
-def put_rows(out, place, y, pair, share):
+def put_rows(halves, place, y, pair, share, core):
     for which in range(2):
         for k in range(ROWS // share):
-            out[y // share + k, which, place] = pair[which][k * share : (k + 1) * share]
+            block = y // share + k
+            half = core if block % 2 == 0 else 1 - core
+            halves[half, block // 2, which, place] = pair[which][k * share : (k + 1) * share]
 
 
 def last_sweep_kernel(
-    wave_ref, e_body, e_p, e_z, a_body, a_p, a_z, observed, sigma_h, sigma_v, final, faces, grad, field, twist
+    wave_ref, e_body, e_p, e_z, a_body, a_p, a_z, observed, sigma_h, sigma_v,
+    final, faces, keep, send, field, twist, halves,
 ):
     index, even = position("gx")
     layers, size_y, _ = sigma_h.shape
-    share = grad.shape[3]
+    share = keep.shape[3]
+    core = lax.rem(lax.axis_index("freq"), 2)
     wave = wave_ref[...]
     edge = jnp.where(index > 0, 1.0, 0.0)
     sides = [side_layer(side, even, layers - 1)[0] for side in range(2)]
@@ -393,10 +397,12 @@
     def inner(layer, carry):
         for y in range(0, size_y, ROWS):
             now, new = sweep(layer, y)
-            put_rows(grad, layer - 1, y, grad_rows(wave, now, new), share)
+            put_rows(halves, layer - 1, y, grad_rows(wave, now, new), share, core)
         return carry
 
     lax.fori_loop(1, layers - 1, inner, 0)
+    keep[...] = halves[0]
+    send[...] = halves[1]
 
     def outer(side, carry):
         layer = jnp.where(side == 0, sides[0], sides[1])
@@ -410,22 +416,32 @@
     lax.fori_loop(0, 2, outer, 0)
 
 
-def gradient_kernel(wave_ref, halo_p, halo_z, e_p, e_z, faces, inner, sigma_h, sigma_v, grad):
+def gradient_kernel(wave_ref, halo_p, halo_z, e_p, e_z, faces, sigma_h, sigma_v, keep, send, halves):
     _, even = position("gx")
     layers, size_y, _ = sigma_h.shape
-    share = grad.shape[3]
+    share = keep.shape[3]
+    core = lax.rem(lax.axis_index("freq"), 2)
     wave = wave_ref[...]
-    for layer in range(1, layers - 1):
-        for which in range(2):
-            grad[:, which, layer] = inner[:, which, layer - 1]
     for side, (halo, now) in enumerate(((halo_p, e_p), (halo_z, e_z))):
         layer, right = side_layer(side, even, layers - 1)
+        place = right.astype(jnp.int32)
         for y in range(0, size_y, ROWS):
             rows = slice(y, y + ROWS)
             add = fix(halo, y, right, wave, sigma_h[layer, rows], sigma_v[layer, rows], size_y)
             new = [[faces[side, part, comp, rows] + add[part][comp] for comp in range(3)] for part in range(2)]
             old = [[now[part, comp, rows] for comp in range(3)] for part in range(2)]
-            put_rows(grad, layer, y, grad_rows(wave, old, new), share)
+            put_rows(halves, place, y, grad_rows(wave, old, new), share, core)
+    keep[...] = halves[0]
+    send[...] = halves[1]
+
+
+def pair_sum_kernel(inner, inner_other, outer, outer_other, terms):
+    between = inner.shape[2]
+    for which in range(2):
+        for k in range(between):
+            terms[:, which, k + 1] = inner[:, which, k] + inner_other[:, which, k]
+        for k, layer in ((0, 0), (1, between + 1)):
+            terms[:, which, layer] = outer[:, which, k] + outer_other[:, which, k]
 
 
 def call(kernel, name, specs, outs, scratch=()):
@@ -518,20 +534,26 @@
     a1_p, a_z_in = lax.optimization_barrier((a1_p, a_z_in))
     e2_z, a1_z, a1_z_out = third(1, e1_z_in, a_z_in)
     a1_z_in = swap(a1_z_out, 1)
-    inner_blocks = (freqs, 2, layers - 2, share, size_z)
-    blocks = (freqs, 2, layers, share, size_z)
-    final, faces, inner = call(
+    half_blocks = (freqs // 2, 2, 2, share, size_z)
+    blocks = (freqs // 2, 2, layers, share, size_z)
+    cores = [(i, i ^ 1) for i in range(freqs)]
+    final, faces, inner, inner_out = call(
         last_sweep_kernel,
         "last_sweep",
         [VMEM] * 10,
-        [(2, 3, layers) + plane, (2,) + face, inner_blocks],
-        [more, more],
+        [(2, 3, layers) + plane, (2,) + face, half_blocks, half_blocks],
+        [more, more, (2,) + half_blocks],
     )(wave, e2, e2_p, e2_z, a1_body, a1_p, a1_z, seen, sigma_h, sigma_v)
     faces, a1_p_in = lax.optimization_barrier((faces, a1_p_in))
-    (terms,) = call(gradient_kernel, "gradient", [VMEM] * 9, [blocks])(
-        wave, a1_p_in, a1_z_in, e2_p, e2_z, faces, inner, sigma_h, sigma_v
-    )
-    gathered = lax.all_to_all(terms, "freq", 0, 0)
+    inner_in = lax.ppermute(inner_out, "freq", cores)
+    a1_z_in, inner_in = lax.optimization_barrier((a1_z_in, inner_in))
+    outer, outer_out = call(
+        gradient_kernel, "gradient", [VMEM] * 8, [half_blocks] * 2, [(2,) + half_blocks]
+    )(wave, a1_p_in, a1_z_in, e2_p, e2_z, faces, sigma_h, sigma_v)
+    outer_in = lax.ppermute(outer_out, "freq", cores)
+    (terms,) = call(pair_sum_kernel, "pair_sum", [VMEM] * 4, [blocks])(inner, inner_in, outer, outer_in)
+    groups = [list(range(core, freqs, 2)) for core in range(2)]
+    gathered = lax.all_to_all(terms, "freq", 0, 0, axis_index_groups=groups)
     return (jnp.sum(gathered, axis=0), final[None])
 
 

time: 75.4 us -> 75.4 us (level)
  the two profiles are of different devices: /device:TPU:384 before, /device:TPU:226 now
where the time goes in v9:
time: 75.4 us; the launch traced here: 74.9 us
  starting transfers between devices  36.3 us (48%)
  blocking collectives  15 us (20%)
  Pallas kernels  10.7 us (14%)
  waiting for transfers between devices  7.7 us (10%)
  local copies, waits for them, and re-layouts  2.34 us (3%)
  between operations  2.2 us (3%)
    ppermute x8, starting transfers between devices, swap(): return lax.ppermute(values, 'gx', swaps[side])  32.3 us
    all_to_all x1, blocking collectives, on_device(): gathered = lax.all_to_all(terms, 'freq', 0, 0, axis_index_groups=groups)  15 us
    ppermute x8, waiting for transfers between devices, swap(): return lax.ppermute(values, 'gx', swaps[side])  5.34 us
    pallas_call x1, Pallas kernels, on_device(): call(last_sweep_kernel, 'last_sweep', [VMEM] * 10, [(2, 3, layers) + plan...  3.11 us
    unnamed x16, local copies, waits for them, and re-layouts  2.34 us
    ppermute x1, starting transfers between devices, on_device(): outer_in = lax.ppermute(outer_out, 'freq', cores)  2.06 us
    pallas_call x1, Pallas kernels, on_device(): call(second_sweep_kernel, 'second_sweep', [VMEM] * 9, [body, body], [more...  1.97 us
    ppermute x1, starting transfers between devices, on_device(): inner_in = lax.ppermute(inner_out, 'freq', cores)  1.91 us
  transfers between devices with their start and end apart: 10, of which 6 were waited for; matrix products, arithmetic and copies ran while one was open for 0% of the time, Pallas kernels for 14%

profile of v9, /device:TPU:226, one launch (start us, length us, event | category | flops | bytes accessed | tf_op | source)
XLA Modules:
  0.0 74.9 jit_solution(10899238605567464147)
XLA Ops:
  0.6 0.0 copy-start.1
  0.6 0.0 copy-start
  0.6 0.0 copy-start.5
  0.7 1.2 %copy-done.5 = bf16[1,2,3,4,64,256]{5,4,3,2,1,0:T(8,128)(2,1)S(1)} copy-done((bf16[1,2,3,4,64,256]{5,4,3,2,1,0:T(8,128)(2,1)S(1)}, bf16[1,2,3,4,64,256]{5,4,3,2,1,0:T(8,128)(2,1)}, u32[]{:S(2)}) %copy-start.5) | copy-done | bytes 786456
  1.8 0.2 first_faces.1
  2.0 2.4 %collective-permute-start = (f32[2,2,64,256]{3,2,1,0:T(8,128)S(1)}, f32[2,2,64,256]{3,2,1,0:T(8,128)S(1)}, u32[]{:S(2)}, u32[]{:S(2)}) collective-permute-start(f32[2,2,64,256]{3,2,1,0:T(8,128)S(1)} %get-tuple-element.51), channel_id=1, source_target_pairs={{0,1},{2,3},{4,5},{6,7},{8,9},{10,11},{12,13},{14,15},{16,17},{18,... | collective-permute-start | bytes 786440 | tf_op jit(solution)/shard_map/ppermute | solution.py:478
  5.8 0.0 copy-start.3
  5.8 1.1 %copy-done.3 = bf16[1,2,3,4,64,256]{5,4,3,2,1,0:T(8,128)(2,1)S(1)} copy-done((bf16[1,2,3,4,64,256]{5,4,3,2,1,0:T(8,128)(2,1)S(1)}, bf16[1,2,3,4,64,256]{5,4,3,2,1,0:T(8,128)(2,1)}, u32[]{:S(2)}) %copy-start.3) | copy-done | bytes 786456
  6.9 0.2 adjoint_faces.1
  7.1 0.0 copy-done.7
  7.1 0.2 source.1.src
  7.3 6.0 %collective-permute-start.1 = (f32[2,2,64,256]{3,2,1,0:T(8,128)S(1)}, f32[2,2,64,256]{3,2,1,0:T(8,128)S(1)}, u32[]{:S(2)}, u32[]{:S(2)}) collective-permute-start(f32[2,2,64,256]{3,2,1,0:T(8,128)S(1)} %get-tuple-element.55), channel_id=1, source_target_pairs={{1,2},{3,4},{5,6},{7,8},{9,10},{11,12},{13,14},{15,16},{17,18},{19... | collective-permute-start | bytes 786440 | tf_op jit(solution)/shard_map/ppermute | solution.py:478
  13.3 0.0 copy-done.1
  13.3 0.0 copy-done
  13.3 0.0 copy-done.6
  13.4 1.6 %first_sweep.1.refs_2_.e_body = f32[4,2,3,64,256]{4,3,2,1,0:T(8,128)S(1)} custom-call(f32[1,1]{1,0:T(1,128)} %bitcast.8.wave_ref, f32[4,64,256]{2,1,0:T(8,128)S(1)} %source.1.src, bf16[2,3,4,64,256]{4,3,2,1,0:T(8,128)(2,1)S(1)} %bitcast.25, f32[4,64,256]{2,1,0:T(8,128)S(1)} %copy-done, f32[4,64,256]{2,1,0:T(8,128)S(1)} %copy-done.1), custom_call_target="tpu_custom_call" | custom-call | tf_op jit(solution)/shard_map/first_sweep/pallas_call | solution.py:494
  15.0 0.0 copy-start.4
  15.0 0.0 collective-permute-done.refs_1_
  15.0 0.3 second_faces_0.1
  15.3 1.9 %collective-permute-start.3 = (f32[2,2,64,256]{3,2,1,0:T(8,128)S(1)}, f32[2,2,64,256]{3,2,1,0:T(8,128)S(1)}, u32[]{:S(2)}, u32[]{:S(2)}) collective-permute-start(f32[2,2,64,256]{3,2,1,0:T(8,128)S(1)} %get-tuple-element.61), channel_id=1, source_target_pairs={{0,1},{2,3},{4,5},{6,7},{8,9},{10,11},{12,13},{14,15},{16,17},{18,... | collective-permute-start | bytes 786440 | tf_op jit(solution)/shard_map/ppermute | solution.py:478
  17.2 0.0 copy-done.4
  17.2 1.6 %first_adjoint.1.a_part.refs_4_ = f32[4,2,3,64,256]{4,3,2,1,0:T(8,128)S(1)} custom-call(f32[1,1]{1,0:T(1,128)} %bitcast.10.wave_ref, bf16[2,3,4,64,256]{4,3,2,1,0:T(8,128)(2,1)S(1)} %bitcast.23, f32[4,64,256]{2,1,0:T(8,128)S(1)} %copy-done, f32[4,64,256]{2,1,0:T(8,128)S(1)} %copy-done.1), custom_call_target="tpu_custom_call" | custom-call | tf_op jit(solution)/shard_map/first_adjoint/pallas_call | solution.py:509
  18.9 0.0 copy-start.2
  18.9 0.5 collective-permute-done.1.refs_1_
  19.4 0.3 second_faces_1.1
  19.6 5.8 %collective-permute-start.2 = (f32[2,2,64,256]{3,2,1,0:T(8,128)S(1)}, f32[2,2,64,256]{3,2,1,0:T(8,128)S(1)}, u32[]{:S(2)}, u32[]{:S(2)}) collective-permute-start(f32[2,2,64,256]{3,2,1,0:T(8,128)S(1)} %get-tuple-element.60), channel_id=1, source_target_pairs={{1,2},{3,4},{5,6},{7,8},{9,10},{11,12},{13,14},{15,16},{17,18},{19... | collective-permute-start | bytes 786440 | tf_op jit(solution)/shard_map/ppermute | solution.py:478
  25.5 1.9 %collective-permute-start.4 = (f32[2,2,64,256]{3,2,1,0:T(8,128)S(1)}, f32[2,2,64,256]{3,2,1,0:T(8,128)S(1)}, u32[]{:S(2)}, u32[]{:S(2)}) collective-permute-start(f32[2,2,64,256]{3,2,1,0:T(8,128)S(1)} %get-tuple-element.68), channel_id=1, source_target_pairs={{0,1},{2,3},{4,5},{6,7},{8,9},{10,11},{12,13},{14,15},{16,17},{18,... | collective-permute-start | bytes 786440 | tf_op jit(solution)/shard_map/ppermute | solution.py:478
  27.4 0.0 collective-permute-done.3.refs_1_
  27.4 3.4 %collective-permute-done.2.refs_1_ = f32[2,2,64,256]{3,2,1,0:T(8,128)S(1)} collective-permute-done((f32[2,2,64,256]{3,2,1,0:T(8,128)S(1)}, f32[2,2,64,256]{3,2,1,0:T(8,128)S(1)}, u32[]{:S(2)}, u32[]{:S(2)}) %collective-permute-start.2) | collective-permute-done | bytes 262176 | tf_op jit(solution)/shard_map/ppermute | solution.py:478
  30.8 0.0 copy-done.2
  30.8 2.0 %second_sweep.1 = (f32[4,2,3,64,256]{4,3,2,1,0:T(8,128)S(1)}, f32[4,2,3,64,256]{4,3,2,1,0:T(8,128)S(1)}) custom-call(f32[1,1]{1,0:T(1,128)} %bitcast.12.wave_ref, f32[4,2,3,64,256]{4,3,2,1,0:T(8,128)S(1)} %first_sweep.1.refs_2_.e_body, f32[2,3,64,256]{3,2,1,0:T(8,128)S(1)} %get-tuple-element.53.e_p, f32[2,3,64,256]{3,2,1,0:T(8,128)S(1)} %get-tuple-element.62.e_z, ...), custom_call_target="tpu_custom_call" | custom-call | tf_op jit(solution)/shard_map/second_sweep/pallas_call | solution.py:518
  32.8 5.5 %collective-permute-start.5 = (f32[2,2,64,256]{3,2,1,0:T(8,128)S(1)}, f32[2,2,64,256]{3,2,1,0:T(8,128)S(1)}, u32[]{:S(2)}, u32[]{:S(2)}) collective-permute-start(f32[2,2,64,256]{3,2,1,0:T(8,128)S(1)} %get-tuple-element.72), channel_id=1, source_target_pairs={{1,2},{3,4},{5,6},{7,8},{9,10},{11,12},{13,14},{15,16},{17,18},{19... | collective-permute-start | bytes 786440 | tf_op jit(solution)/shard_map/ppermute | solution.py:478
  38.3 0.0 collective-permute-done.4.refs_2_
  38.3 0.4 third_faces_0.1
  38.8 3.2 %collective-permute-start.8 = (f32[2,2,64,256]{3,2,1,0:T(8,128)S(1)}, f32[2,2,64,256]{3,2,1,0:T(8,128)S(1)}, u32[]{:S(2)}, u32[]{:S(2)}) collective-permute-start(f32[2,2,64,256]{3,2,1,0:T(8,128)S(1)} %get-tuple-element.83), channel_id=1, source_target_pairs={{0,1},{2,3},{4,5},{6,7},{8,9},{10,11},{12,13},{14,15},{16,17},{18,... | collective-permute-start | bytes 786440 | tf_op jit(solution)/shard_map/ppermute | solution.py:478
  41.9 1.3 %collective-permute-done.5.refs_2_ = f32[2,2,64,256]{3,2,1,0:T(8,128)S(1)} collective-permute-done((f32[2,2,64,256]{3,2,1,0:T(8,128)S(1)}, f32[2,2,64,256]{3,2,1,0:T(8,128)S(1)}, u32[]{:S(2)}, u32[]{:S(2)}) %collective-permute-start.5) | collective-permute-done | bytes 262176 | tf_op jit(solution)/shard_map/ppermute | solution.py:478
  43.3 0.4 third_faces_1.1
  43.7 5.5 %collective-permute-start.6 = (f32[2,2,64,256]{3,2,1,0:T(8,128)S(1)}, f32[2,2,64,256]{3,2,1,0:T(8,128)S(1)}, u32[]{:S(2)}, u32[]{:S(2)}) collective-permute-start(f32[2,2,64,256]{3,2,1,0:T(8,128)S(1)} %get-tuple-element.79), channel_id=1, source_target_pairs={{1,2},{3,4},{5,6},{7,8},{9,10},{11,12},{13,14},{15,16},{17,18},{19... | collective-permute-start | bytes 786440 | tf_op jit(solution)/shard_map/ppermute | solution.py:478
  49.2 3.1 %last_sweep.1 = (f32[2,3,4,64,256]{4,3,2,1,0:T(8,128)}, f32[2,2,3,64,256]{4,3,2,1,0:T(8,128)S(1)}, f32[8,2,2,4,256]{4,3,2,1,0:T(4,128)S(1)}, f32[8,2,2,4,256]{4,3,2,1,0:T(4,128)S(1)}) custom-call(f32[1,1]{1,0:T(1,128)} %bitcast.15.wave_ref, f32[4,2,3,64,256]{4,3,2,1,0:T(8,128)S(1)} %get-tuple-element.66.refs_3_.e_body, ...), custom_call_target="tpu_custom_call" | custom-call | tf_op jit(solution)/shard_map/last_sweep/pallas_call | solution.py:540
  52.3 1.9 %collective-permute-start.7 = (f32[8,2,2,4,256]{4,3,2,1,0:T(4,128)S(1)}, f32[8,2,2,4,256]{4,3,2,1,0:T(4,128)S(1)}, u32[]{:S(2)}, u32[]{:S(2)}) collective-permute-start(f32[8,2,2,4,256]{4,3,2,1,0:T(4,128)S(1)} %get-tuple-element.80), channel_id=1, source_target_pairs={{0,32},{32,0},{64,96},{96,64},{128,160},{160,128},{192,224},{224,1... | collective-permute-start | bytes 393224 | tf_op jit(solution)/shard_map/ppermute | solution.py:548
  54.3 0.1 collective-permute-done.8.halo_p
  54.4 1.2 %collective-permute-done.7.inner_other = f32[8,2,2,4,256]{4,3,2,1,0:T(4,128)S(1)} collective-permute-done((f32[8,2,2,4,256]{4,3,2,1,0:T(4,128)S(1)}, f32[8,2,2,4,256]{4,3,2,1,0:T(4,128)S(1)}, u32[]{:S(2)}, u32[]{:S(2)}) %collective-permute-start.7) | collective-permute-done | bytes 131104 | tf_op jit(solution)/shard_map/ppermute | solution.py:548
  55.6 0.0 collective-permute-done.6.halo_z
  55.6 0.4 gradient.1
  56.0 2.1 %collective-permute-start.9 = (f32[8,2,2,4,256]{4,3,2,1,0:T(4,128)S(1)}, f32[8,2,2,4,256]{4,3,2,1,0:T(4,128)S(1)}, u32[]{:S(2)}, u32[]{:S(2)}) collective-permute-start(f32[8,2,2,4,256]{4,3,2,1,0:T(4,128)S(1)} %get-tuple-element.88), channel_id=1, source_target_pairs={{0,32},{32,0},{64,96},{96,64},{128,160},{160,128},{192,224},{224,1... | collective-permute-start | bytes 393224 | tf_op jit(solution)/shard_map/ppermute | solution.py:553
  58.0 1.2 %collective-permute-done.9.outer_other = f32[8,2,2,4,256]{4,3,2,1,0:T(4,128)S(1)} collective-permute-done((f32[8,2,2,4,256]{4,3,2,1,0:T(4,128)S(1)}, f32[8,2,2,4,256]{4,3,2,1,0:T(4,128)S(1)}, u32[]{:S(2)}, u32[]{:S(2)}) %collective-permute-start.9) | collective-permute-done | bytes 131104 | tf_op jit(solution)/shard_map/ppermute | solution.py:553
  59.2 15.0 %all_to_all.5 = f32[8,2,4,4,256]{4,3,2,1,0:T(4,128)S(1)} all-to-all(f32[8,2,4,4,256]{4,3,2,1,0:T(4,128)S(1)} %pair_sum.1), channel_id=1, replica_groups={{0,64,128,192,256,320,384,448},{32,96,160,224,288,352,416,480},{1,65,12..., dimensions={0} | all-to-all | bytes 524288 | tf_op jit(solution)/shard_map/all_to_all | solution.py:556
  74.3 0.7 reduce_sum.9
  (3 shorter events, 0.0 us)
Async XLA Ops:
  0.6 12.7 %copy-start.1 = (f32[4,64,256]{2,1,0:T(8,128)S(1)}, f32[4,64,256]{2,1,0:T(8,128)}, u32[]{:S(2)}) copy-start(f32[4,64,256]{2,1,0:T(8,128)} %sigma_v.9) | copy-start | bytes 786436
  0.6 12.7 %copy-start = (f32[4,64,256]{2,1,0:T(8,128)S(1)}, f32[4,64,256]{2,1,0:T(8,128)}, u32[]{:S(2)}) copy-start(f32[4,64,256]{2,1,0:T(8,128)} %sigma_h.9) | copy-start | bytes 786436
  0.6 1.2 %copy-start.5 = (bf16[1,2,3,4,64,256]{5,4,3,2,1,0:T(8,128)(2,1)S(1)}, bf16[1,2,3,4,64,256]{5,4,3,2,1,0:T(8,128)(2,1)}, u32[]{:S(2)}) copy-start(bf16[1,2,3,4,64,256]{5,4,3,2,1,0:T(8,128)(2,1)} %param.11) | copy-start | bytes 2359300
  1.8 5.3 %copy-start.7 = (s32[64]{0:T(128)S(1)}, s32[64]{0:T(128)}, u32[]{:S(2)}) copy-start(s32[64]{0:T(128)} %param.15) | copy-start | bytes 772
  2.0 13.0 %collective-permute-start = (f32[2,2,64,256]{3,2,1,0:T(8,128)S(1)}, f32[2,2,64,256]{3,2,1,0:T(8,128)S(1)}, u32[]{:S(2)}, u32[]{:S(2)}) collective-permute-start(f32[2,2,64,256]{3,2,1,0:T(8,128)S(1)} %get-tuple-element.51), channel_id=1, source_target_pairs={{0,1},{2,3},{4,5},{6,7},{8,9},{10,11},{12,13},{14,15},{16,17},{18,... | collective-permute-start | bytes 786440 | tf_op jit(solution)/shard_map/ppermute | solution.py:478
  5.8 1.1 %copy-start.3 = (bf16[1,2,3,4,64,256]{5,4,3,2,1,0:T(8,128)(2,1)S(1)}, bf16[1,2,3,4,64,256]{5,4,3,2,1,0:T(8,128)(2,1)}, u32[]{:S(2)}) copy-start(bf16[1,2,3,4,64,256]{5,4,3,2,1,0:T(8,128)(2,1)} %param.12) | copy-start | bytes 2359300
  6.9 6.4 %copy-start.6 = (bf16[1,2,3,4,64,256]{5,4,3,2,1,0:T(8,128)(2,1)S(1)}, bf16[1,2,3,4,64,256]{5,4,3,2,1,0:T(8,128)(2,1)}, u32[]{:S(2)}) copy-start(bf16[1,2,3,4,64,256]{5,4,3,2,1,0:T(8,128)(2,1)} %param.11) | copy-start | bytes 2359300
  7.3 12.0 %collective-permute-start.1 = (f32[2,2,64,256]{3,2,1,0:T(8,128)S(1)}, f32[2,2,64,256]{3,2,1,0:T(8,128)S(1)}, u32[]{:S(2)}, u32[]{:S(2)}) collective-permute-start(f32[2,2,64,256]{3,2,1,0:T(8,128)S(1)} %get-tuple-element.55), channel_id=1, source_target_pairs={{1,2},{3,4},{5,6},{7,8},{9,10},{11,12},{13,14},{15,16},{17,18},{19... | collective-permute-start | bytes 786440 | tf_op jit(solution)/shard_map/ppermute | solution.py:478
  15.0 2.2 %copy-start.4 = (bf16[1,2,3,4,64,256]{5,4,3,2,1,0:T(8,128)(2,1)S(1)}, bf16[1,2,3,4,64,256]{5,4,3,2,1,0:T(8,128)(2,1)}, u32[]{:S(2)}) copy-start(bf16[1,2,3,4,64,256]{5,4,3,2,1,0:T(8,128)(2,1)} %param.12) | copy-start | bytes 2359300
  15.3 12.1 %collective-permute-start.3 = (f32[2,2,64,256]{3,2,1,0:T(8,128)S(1)}, f32[2,2,64,256]{3,2,1,0:T(8,128)S(1)}, u32[]{:S(2)}, u32[]{:S(2)}) collective-permute-start(f32[2,2,64,256]{3,2,1,0:T(8,128)S(1)} %get-tuple-element.61), channel_id=1, source_target_pairs={{0,1},{2,3},{4,5},{6,7},{8,9},{10,11},{12,13},{14,15},{16,17},{18,... | collective-permute-start | bytes 786440 | tf_op jit(solution)/shard_map/ppermute | solution.py:478
  18.9 11.9 %copy-start.2 = (bf16[1,2,3,4,64,256]{5,4,3,2,1,0:T(8,128)(2,1)S(1)}, bf16[1,2,3,4,64,256]{5,4,3,2,1,0:T(8,128)(2,1)}, u32[]{:S(2)}) copy-start(bf16[1,2,3,4,64,256]{5,4,3,2,1,0:T(8,128)(2,1)} %param.13) | copy-start | bytes 2359300
  19.6 11.2 %collective-permute-start.2 = (f32[2,2,64,256]{3,2,1,0:T(8,128)S(1)}, f32[2,2,64,256]{3,2,1,0:T(8,128)S(1)}, u32[]{:S(2)}, u32[]{:S(2)}) collective-permute-start(f32[2,2,64,256]{3,2,1,0:T(8,128)S(1)} %get-tuple-element.60), channel_id=1, source_target_pairs={{1,2},{3,4},{5,6},{7,8},{9,10},{11,12},{13,14},{15,16},{17,18},{19... | collective-permute-start | bytes 786440 | tf_op jit(solution)/shard_map/ppermute | solution.py:478
  25.5 12.9 %collective-permute-start.4 = (f32[2,2,64,256]{3,2,1,0:T(8,128)S(1)}, f32[2,2,64,256]{3,2,1,0:T(8,128)S(1)}, u32[]{:S(2)}, u32[]{:S(2)}) collective-permute-start(f32[2,2,64,256]{3,2,1,0:T(8,128)S(1)} %get-tuple-element.68), channel_id=1, source_target_pairs={{0,1},{2,3},{4,5},{6,7},{8,9},{10,11},{12,13},{14,15},{16,17},{18,... | collective-permute-start | bytes 786440 | tf_op jit(solution)/shard_map/ppermute | solution.py:478
  32.8 10.5 %collective-permute-start.5 = (f32[2,2,64,256]{3,2,1,0:T(8,128)S(1)}, f32[2,2,64,256]{3,2,1,0:T(8,128)S(1)}, u32[]{:S(2)}, u32[]{:S(2)}) collective-permute-start(f32[2,2,64,256]{3,2,1,0:T(8,128)S(1)} %get-tuple-element.72), channel_id=1, source_target_pairs={{1,2},{3,4},{5,6},{7,8},{9,10},{11,12},{13,14},{15,16},{17,18},{19... | collective-permute-start | bytes 786440 | tf_op jit(solution)/shard_map/ppermute | solution.py:478
  38.8 15.6 %collective-permute-start.8 = (f32[2,2,64,256]{3,2,1,0:T(8,128)S(1)}, f32[2,2,64,256]{3,2,1,0:T(8,128)S(1)}, u32[]{:S(2)}, u32[]{:S(2)}) collective-permute-start(f32[2,2,64,256]{3,2,1,0:T(8,128)S(1)} %get-tuple-element.83), channel_id=1, source_target_pairs={{0,1},{2,3},{4,5},{6,7},{8,9},{10,11},{12,13},{14,15},{16,17},{18,... | collective-permute-start | bytes 786440 | tf_op jit(solution)/shard_map/ppermute | solution.py:478
  43.7 11.9 %collective-permute-start.6 = (f32[2,2,64,256]{3,2,1,0:T(8,128)S(1)}, f32[2,2,64,256]{3,2,1,0:T(8,128)S(1)}, u32[]{:S(2)}, u32[]{:S(2)}) collective-permute-start(f32[2,2,64,256]{3,2,1,0:T(8,128)S(1)} %get-tuple-element.79), channel_id=1, source_target_pairs={{1,2},{3,4},{5,6},{7,8},{9,10},{11,12},{13,14},{15,16},{17,18},{19... | collective-permute-start | bytes 786440 | tf_op jit(solution)/shard_map/ppermute | solution.py:478
  52.3 3.2 %collective-permute-start.7 = (f32[8,2,2,4,256]{4,3,2,1,0:T(4,128)S(1)}, f32[8,2,2,4,256]{4,3,2,1,0:T(4,128)S(1)}, u32[]{:S(2)}, u32[]{:S(2)}) collective-permute-start(f32[8,2,2,4,256]{4,3,2,1,0:T(4,128)S(1)} %get-tuple-element.80), channel_id=1, source_target_pairs={{0,32},{32,0},{64,96},{96,64},{128,160},{160,128},{192,224},{224,1... | collective-permute-start | bytes 393224 | tf_op jit(solution)/shard_map/ppermute | solution.py:548
  56.0 3.2 %collective-permute-start.9 = (f32[8,2,2,4,256]{4,3,2,1,0:T(4,128)S(1)}, f32[8,2,2,4,256]{4,3,2,1,0:T(4,128)S(1)}, u32[]{:S(2)}, u32[]{:S(2)}) collective-permute-start(f32[8,2,2,4,256]{4,3,2,1,0:T(4,128)S(1)} %get-tuple-element.88), channel_id=1, source_target_pairs={{0,32},{32,0},{64,96},{96,64},{128,160},{160,128},{192,224},{224,1... | collective-permute-start | bytes 393224 | tf_op jit(solution)/shard_map/ppermute | solution.py:553

commit v10 on v8

--- a/solution.py
+++ b/solution.py
@@ -498,11 +498,10 @@
     a_p, e1_z_out = lax.optimization_barrier((a_p, e1_z_out))
     e1_z_in = swap(e1_z_out, 1)
     a_p_in = swap(a_p, 0)
-    e1_z, e1_z_in, e1_p_in = lax.optimization_barrier((e1_z, e1_z_in, e1_p_in))
     e2, a1_body = call(
         second_sweep_kernel, "second_sweep", [VMEM] * 9, [body, body], [more, more]
     )(wave, e1, e1_p, e1_z, a1, src, seen, sigma_h, sigma_v)
-    e2, a_z = lax.optimization_barrier((e2, a_z))
+    e2, a_z, e1_p_in, e1_z_in = lax.optimization_barrier((e2, a_z, e1_p_in, e1_z_in))
     a_z_in = swap(a_z, 1)
 
     def third(side, e_halo, a_halo):

time: 75.4 us -> 79.2 us (1.050)
  waiting for transfers between devices: 14.3 us -> 17.8 us
    ppermute x8, waiting for transfers between devices: 14.3 us -> 17.8 us  [swap(): return lax.ppermute(values, 'gx', swaps[side])]
where the time goes in v10:
time: 79.2 us; the launch traced here: 78.7 us
  starting transfers between devices  26.1 us (33%)
  blocking collectives  18.9 us (24%)
  waiting for transfers between devices  17.8 us (22%)
  Pallas kernels  10.7 us (14%)
  local copies, waits for them, and re-layouts  2.34 us (3%)
  between operations  2.18 us (3%)
    ppermute x8, starting transfers between devices, swap(): return lax.ppermute(values, 'gx', swaps[side])  26.1 us
    all_to_all x1, blocking collectives, on_device(): gathered = lax.all_to_all(terms, 'freq', 0, 0)  18.9 us
    ppermute x8, waiting for transfers between devices, swap(): return lax.ppermute(values, 'gx', swaps[side])  17.8 us
    pallas_call x1, Pallas kernels, on_device(): call(last_sweep_kernel, 'last_sweep', [VMEM] * 10, [(2, 3, layers) + plan...  3.1 us
    unnamed x16, local copies, waits for them, and re-layouts  2.34 us
    pallas_call x1, Pallas kernels, on_device(): call(second_sweep_kernel, 'second_sweep', [VMEM] * 9, [body, body], [more...  1.98 us
    pallas_call x1, Pallas kernels, on_device(): call(first_sweep_kernel, 'first_sweep', [VMEM] * 5, [body], [more, more])  1.65 us
    pallas_call x1, Pallas kernels, on_device(): call(first_adjoint_kernel, 'first_adjoint', [VMEM] * 4, [body], [more, mo...  1.63 us
  transfers between devices with their start and end apart: 8, of which 4 were waited for; matrix products, arithmetic and copies ran while one was open for 0% of the time, Pallas kernels for 13%

profile of v10, /device:TPU:384, one launch (start us, length us, event | category | flops | bytes accessed | tf_op | source)
XLA Modules:
  0.0 78.7 jit_solution(3776141835985519688)
XLA Ops:
  0.6 0.0 copy-start.1
  0.6 0.0 copy-start
  0.6 0.0 copy-start.5
  0.7 1.2 %copy-done.5 = bf16[1,2,3,4,64,256]{5,4,3,2,1,0:T(8,128)(2,1)S(1)} copy-done((bf16[1,2,3,4,64,256]{5,4,3,2,1,0:T(8,128)(2,1)S(1)}, bf16[1,2,3,4,64,256]{5,4,3,2,1,0:T(8,128)(2,1)}, u32[]{:S(2)}) %copy-start.5) | copy-done | bytes 786456
  1.8 0.0 copy-start.7
  1.8 0.2 first_faces.1
  2.0 3.4 %collective-permute-start = (f32[2,2,64,256]{3,2,1,0:T(8,128)S(1)}, f32[2,2,64,256]{3,2,1,0:T(8,128)S(1)}, u32[]{:S(2)}, u32[]{:S(2)}) collective-permute-start(f32[2,2,64,256]{3,2,1,0:T(8,128)S(1)} %get-tuple-element.45), channel_id=1, source_target_pairs={{0,1},{2,3},{4,5},{6,7},{8,9},{10,11},{12,13},{14,15},{16,17},{18,... | collective-permute-start | bytes 786440 | tf_op jit(solution)/shard_map/ppermute | solution.py:462
  6.7 0.0 copy-start.3
  6.7 1.1 %copy-done.3 = bf16[1,2,3,4,64,256]{5,4,3,2,1,0:T(8,128)(2,1)S(1)} copy-done((bf16[1,2,3,4,64,256]{5,4,3,2,1,0:T(8,128)(2,1)S(1)}, bf16[1,2,3,4,64,256]{5,4,3,2,1,0:T(8,128)(2,1)}, u32[]{:S(2)}) %copy-start.3) | copy-done | bytes 786456
  7.9 0.0 copy-start.6
  7.9 0.2 adjoint_faces.1
  8.1 0.0 copy-done.7
  8.1 0.2 source.1.src
  8.3 4.1 %collective-permute-start.1 = (f32[2,2,64,256]{3,2,1,0:T(8,128)S(1)}, f32[2,2,64,256]{3,2,1,0:T(8,128)S(1)}, u32[]{:S(2)}, u32[]{:S(2)}) collective-permute-start(f32[2,2,64,256]{3,2,1,0:T(8,128)S(1)} %get-tuple-element.49), channel_id=1, source_target_pairs={{1,2},{3,4},{5,6},{7,8},{9,10},{11,12},{13,14},{15,16},{17,18},{19... | collective-permute-start | bytes 786440 | tf_op jit(solution)/shard_map/ppermute | solution.py:462
  12.4 0.0 copy-done.1
  12.4 0.0 copy-done
  12.4 0.0 copy-done.6
  12.4 1.6 %first_sweep.1.refs_2_.e_body = f32[4,2,3,64,256]{4,3,2,1,0:T(8,128)S(1)} custom-call(f32[1,1]{1,0:T(1,128)} %bitcast.8.wave_ref, f32[4,64,256]{2,1,0:T(8,128)S(1)} %source.1.src, bf16[2,3,4,64,256]{4,3,2,1,0:T(8,128)(2,1)S(1)} %bitcast.25, f32[4,64,256]{2,1,0:T(8,128)S(1)} %copy-done, f32[4,64,256]{2,1,0:T(8,128)S(1)} %copy-done.1), custom_call_target="tpu_custom_call" | custom-call | tf_op jit(solution)/shard_map/first_sweep/pallas_call | solution.py:478
  14.1 0.0 copy-start.4
  14.1 0.0 collective-permute-done.refs_1_
  14.1 0.3 second_faces_0.1
  14.4 2.2 %collective-permute-start.2 = (f32[2,2,64,256]{3,2,1,0:T(8,128)S(1)}, f32[2,2,64,256]{3,2,1,0:T(8,128)S(1)}, u32[]{:S(2)}, u32[]{:S(2)}) collective-permute-start(f32[2,2,64,256]{3,2,1,0:T(8,128)S(1)} %get-tuple-element.55), channel_id=1, source_target_pairs={{0,1},{2,3},{4,5},{6,7},{8,9},{10,11},{12,13},{14,15},{16,17},{18,... | collective-permute-start | bytes 786440 | tf_op jit(solution)/shard_map/ppermute | solution.py:462
  16.6 0.0 copy-done.4
  16.6 1.6 %first_adjoint.1.a_part.refs_4_ = f32[4,2,3,64,256]{4,3,2,1,0:T(8,128)S(1)} custom-call(f32[1,1]{1,0:T(1,128)} %bitcast.10.wave_ref, bf16[2,3,4,64,256]{4,3,2,1,0:T(8,128)(2,1)S(1)} %bitcast.23, f32[4,64,256]{2,1,0:T(8,128)S(1)} %copy-done, f32[4,64,256]{2,1,0:T(8,128)S(1)} %copy-done.1), custom_call_target="tpu_custom_call" | custom-call | tf_op jit(solution)/shard_map/first_adjoint/pallas_call | solution.py:493
  18.2 0.0 copy-start.2
  18.2 1.9 %collective-permute-done.1.refs_1_ = f32[2,2,64,256]{3,2,1,0:T(8,128)S(1)} collective-permute-done((f32[2,2,64,256]{3,2,1,0:T(8,128)S(1)}, f32[2,2,64,256]{3,2,1,0:T(8,128)S(1)}, u32[]{:S(2)}, u32[]{:S(2)}) %collective-permute-start.1) | collective-permute-done | bytes 262176 | tf_op jit(solution)/shard_map/ppermute | solution.py:462
  20.2 0.3 second_faces_1.1
  20.4 4.1 %collective-permute-start.3 = (f32[2,2,64,256]{3,2,1,0:T(8,128)S(1)}, f32[2,2,64,256]{3,2,1,0:T(8,128)S(1)}, u32[]{:S(2)}, u32[]{:S(2)}) collective-permute-start(f32[2,2,64,256]{3,2,1,0:T(8,128)S(1)} %get-tuple-element.58), channel_id=1, source_target_pairs={{1,2},{3,4},{5,6},{7,8},{9,10},{11,12},{13,14},{15,16},{17,18},{19... | collective-permute-start | bytes 786440 | tf_op jit(solution)/shard_map/ppermute | solution.py:462
  24.5 1.9 %collective-permute-start.4 = (f32[2,2,64,256]{3,2,1,0:T(8,128)S(1)}, f32[2,2,64,256]{3,2,1,0:T(8,128)S(1)}, u32[]{:S(2)}, u32[]{:S(2)}) collective-permute-start(f32[2,2,64,256]{3,2,1,0:T(8,128)S(1)} %get-tuple-element.61), channel_id=1, source_target_pairs={{0,1},{2,3},{4,5},{6,7},{8,9},{10,11},{12,13},{14,15},{16,17},{18,... | collective-permute-start | bytes 786440 | tf_op jit(solution)/shard_map/ppermute | solution.py:462
  26.5 0.0 copy-done.2
  26.5 2.0 %second_sweep.1 = (f32[4,2,3,64,256]{4,3,2,1,0:T(8,128)S(1)}, f32[4,2,3,64,256]{4,3,2,1,0:T(8,128)S(1)}) custom-call(f32[1,1]{1,0:T(1,128)} %bitcast.12.wave_ref, f32[4,2,3,64,256]{4,3,2,1,0:T(8,128)S(1)} %first_sweep.1.refs_2_.e_body, f32[2,3,64,256]{3,2,1,0:T(8,128)S(1)} %get-tuple-element.47.e_p, f32[2,3,64,256]{3,2,1,0:T(8,128)S(1)} %get-tuple-element.51.e_z, ...), custom_call_target="tpu_custom_call" | custom-call | tf_op jit(solution)/shard_map/second_sweep/pallas_call | solution.py:501
  28.5 2.8 %collective-permute-done.2.refs_1_ = f32[2,2,64,256]{3,2,1,0:T(8,128)S(1)} collective-permute-done((f32[2,2,64,256]{3,2,1,0:T(8,128)S(1)}, f32[2,2,64,256]{3,2,1,0:T(8,128)S(1)}, u32[]{:S(2)}, u32[]{:S(2)}) %collective-permute-start.2) | collective-permute-done | bytes 262176 | tf_op jit(solution)/shard_map/ppermute | solution.py:462
  31.3 0.0 collective-permute-done.3.refs_1_
  31.3 4.1 %collective-permute-start.5 = (f32[2,2,64,256]{3,2,1,0:T(8,128)S(1)}, f32[2,2,64,256]{3,2,1,0:T(8,128)S(1)}, u32[]{:S(2)}, u32[]{:S(2)}) collective-permute-start(f32[2,2,64,256]{3,2,1,0:T(8,128)S(1)} %get-tuple-element.65), channel_id=1, source_target_pairs={{1,2},{3,4},{5,6},{7,8},{9,10},{11,12},{13,14},{15,16},{17,18},{19... | collective-permute-start | bytes 786440 | tf_op jit(solution)/shard_map/ppermute | solution.py:462
  35.4 7.1 %collective-permute-done.4.refs_2_ = f32[2,2,64,256]{3,2,1,0:T(8,128)S(1)} collective-permute-done((f32[2,2,64,256]{3,2,1,0:T(8,128)S(1)}, f32[2,2,64,256]{3,2,1,0:T(8,128)S(1)}, u32[]{:S(2)}, u32[]{:S(2)}) %collective-permute-start.4) | collective-permute-done | bytes 262176 | tf_op jit(solution)/shard_map/ppermute | solution.py:462
  42.5 0.4 third_faces_0.1
  42.9 1.9 %collective-permute-start.6 = (f32[2,2,64,256]{3,2,1,0:T(8,128)S(1)}, f32[2,2,64,256]{3,2,1,0:T(8,128)S(1)}, u32[]{:S(2)}, u32[]{:S(2)}) collective-permute-start(f32[2,2,64,256]{3,2,1,0:T(8,128)S(1)} %get-tuple-element.72), channel_id=1, source_target_pairs={{0,1},{2,3},{4,5},{6,7},{8,9},{10,11},{12,13},{14,15},{16,17},{18,... | collective-permute-start | bytes 786440 | tf_op jit(solution)/shard_map/ppermute | solution.py:462
  44.8 0.0 collective-permute-done.5.refs_2_
  44.9 0.4 third_faces_1.1
  45.3 4.4 %collective-permute-start.7 = (f32[2,2,64,256]{3,2,1,0:T(8,128)S(1)}, f32[2,2,64,256]{3,2,1,0:T(8,128)S(1)}, u32[]{:S(2)}, u32[]{:S(2)}) collective-permute-start(f32[2,2,64,256]{3,2,1,0:T(8,128)S(1)} %get-tuple-element.74), channel_id=1, source_target_pairs={{1,2},{3,4},{5,6},{7,8},{9,10},{11,12},{13,14},{15,16},{17,18},{19... | collective-permute-start | bytes 786440 | tf_op jit(solution)/shard_map/ppermute | solution.py:462
  49.7 3.1 %last_sweep.1 = (f32[2,3,4,64,256]{4,3,2,1,0:T(8,128)}, f32[2,2,3,64,256]{4,3,2,1,0:T(8,128)S(1)}, f32[16,2,2,4,256]{4,3,2,1,0:T(4,128)S(1)}) custom-call(f32[1,1]{1,0:T(1,128)} %bitcast.15.wave_ref, f32[4,2,3,64,256]{4,3,2,1,0:T(8,128)S(1)} %get-tuple-element.59.refs_3_.e_body, f32[2,3,64,256]{3,2,1,0:T(8,128)S(1)} %get-tuple-element.62.e_p, ...), custom_call_target="tpu_custom_call" | custom-call | tf_op jit(solution)/shard_map/last_sweep/pallas_call | solution.py:522
  52.8 5.9 %collective-permute-done.6.halo_p = f32[2,2,64,256]{3,2,1,0:T(8,128)S(1)} collective-permute-done((f32[2,2,64,256]{3,2,1,0:T(8,128)S(1)}, f32[2,2,64,256]{3,2,1,0:T(8,128)S(1)}, u32[]{:S(2)}, u32[]{:S(2)}) %collective-permute-start.6) | collective-permute-done | bytes 262176 | tf_op jit(solution)/shard_map/ppermute | solution.py:462
  58.8 0.0 collective-permute-done.7.halo_z
  58.8 0.4 gradient.1
  59.1 18.9 %all_to_all.5 = f32[16,2,4,4,256]{4,3,2,1,0:T(4,128)S(1)} all-to-all(f32[16,2,4,4,256]{4,3,2,1,0:T(4,128)S(1)} %gradient.1), channel_id=1, replica_groups=mesh['freq'=16,'gx'=32] {'freq'}, dimensions={0} | all-to-all | bytes 1048576 | tf_op jit(solution)/shard_map/all_to_all | solution.py:533
  78.0 0.7 reduce_sum.9
Async XLA Ops:
  0.6 11.8 %copy-start.1 = (f32[4,64,256]{2,1,0:T(8,128)S(1)}, f32[4,64,256]{2,1,0:T(8,128)}, u32[]{:S(2)}) copy-start(f32[4,64,256]{2,1,0:T(8,128)} %sigma_v.9) | copy-start | bytes 786436
  0.6 11.8 %copy-start = (f32[4,64,256]{2,1,0:T(8,128)S(1)}, f32[4,64,256]{2,1,0:T(8,128)}, u32[]{:S(2)}) copy-start(f32[4,64,256]{2,1,0:T(8,128)} %sigma_h.9) | copy-start | bytes 786436
  0.6 1.2 %copy-start.5 = (bf16[1,2,3,4,64,256]{5,4,3,2,1,0:T(8,128)(2,1)S(1)}, bf16[1,2,3,4,64,256]{5,4,3,2,1,0:T(8,128)(2,1)}, u32[]{:S(2)}) copy-start(bf16[1,2,3,4,64,256]{5,4,3,2,1,0:T(8,128)(2,1)} %param.11) | copy-start | bytes 2359300
  1.8 6.2 %copy-start.7 = (s32[64]{0:T(128)S(1)}, s32[64]{0:T(128)}, u32[]{:S(2)}) copy-start(s32[64]{0:T(128)} %param.15) | copy-start | bytes 772
  2.0 12.1 %collective-permute-start = (f32[2,2,64,256]{3,2,1,0:T(8,128)S(1)}, f32[2,2,64,256]{3,2,1,0:T(8,128)S(1)}, u32[]{:S(2)}, u32[]{:S(2)}) collective-permute-start(f32[2,2,64,256]{3,2,1,0:T(8,128)S(1)} %get-tuple-element.45), channel_id=1, source_target_pairs={{0,1},{2,3},{4,5},{6,7},{8,9},{10,11},{12,13},{14,15},{16,17},{18,... | collective-permute-start | bytes 786440 | tf_op jit(solution)/shard_map/ppermute | solution.py:462
  6.7 1.1 %copy-start.3 = (bf16[1,2,3,4,64,256]{5,4,3,2,1,0:T(8,128)(2,1)S(1)}, bf16[1,2,3,4,64,256]{5,4,3,2,1,0:T(8,128)(2,1)}, u32[]{:S(2)}) copy-start(bf16[1,2,3,4,64,256]{5,4,3,2,1,0:T(8,128)(2,1)} %param.12) | copy-start | bytes 2359300
  7.9 4.6 %copy-start.6 = (bf16[1,2,3,4,64,256]{5,4,3,2,1,0:T(8,128)(2,1)S(1)}, bf16[1,2,3,4,64,256]{5,4,3,2,1,0:T(8,128)(2,1)}, u32[]{:S(2)}) copy-start(bf16[1,2,3,4,64,256]{5,4,3,2,1,0:T(8,128)(2,1)} %param.11) | copy-start | bytes 2359300
  8.3 11.9 %collective-permute-start.1 = (f32[2,2,64,256]{3,2,1,0:T(8,128)S(1)}, f32[2,2,64,256]{3,2,1,0:T(8,128)S(1)}, u32[]{:S(2)}, u32[]{:S(2)}) collective-permute-start(f32[2,2,64,256]{3,2,1,0:T(8,128)S(1)} %get-tuple-element.49), channel_id=1, source_target_pairs={{1,2},{3,4},{5,6},{7,8},{9,10},{11,12},{13,14},{15,16},{17,18},{19... | collective-permute-start | bytes 786440 | tf_op jit(solution)/shard_map/ppermute | solution.py:462
  14.1 2.5 %copy-start.4 = (bf16[1,2,3,4,64,256]{5,4,3,2,1,0:T(8,128)(2,1)S(1)}, bf16[1,2,3,4,64,256]{5,4,3,2,1,0:T(8,128)(2,1)}, u32[]{:S(2)}) copy-start(bf16[1,2,3,4,64,256]{5,4,3,2,1,0:T(8,128)(2,1)} %param.12) | copy-start | bytes 2359300
  14.4 16.9 %collective-permute-start.2 = (f32[2,2,64,256]{3,2,1,0:T(8,128)S(1)}, f32[2,2,64,256]{3,2,1,0:T(8,128)S(1)}, u32[]{:S(2)}, u32[]{:S(2)}) collective-permute-start(f32[2,2,64,256]{3,2,1,0:T(8,128)S(1)} %get-tuple-element.55), channel_id=1, source_target_pairs={{0,1},{2,3},{4,5},{6,7},{8,9},{10,11},{12,13},{14,15},{16,17},{18,... | collective-permute-start | bytes 786440 | tf_op jit(solution)/shard_map/ppermute | solution.py:462
  18.2 8.2 %copy-start.2 = (bf16[1,2,3,4,64,256]{5,4,3,2,1,0:T(8,128)(2,1)S(1)}, bf16[1,2,3,4,64,256]{5,4,3,2,1,0:T(8,128)(2,1)}, u32[]{:S(2)}) copy-start(bf16[1,2,3,4,64,256]{5,4,3,2,1,0:T(8,128)(2,1)} %param.13) | copy-start | bytes 2359300
  20.4 10.9 %collective-permute-start.3 = (f32[2,2,64,256]{3,2,1,0:T(8,128)S(1)}, f32[2,2,64,256]{3,2,1,0:T(8,128)S(1)}, u32[]{:S(2)}, u32[]{:S(2)}) collective-permute-start(f32[2,2,64,256]{3,2,1,0:T(8,128)S(1)} %get-tuple-element.58), channel_id=1, source_target_pairs={{1,2},{3,4},{5,6},{7,8},{9,10},{11,12},{13,14},{15,16},{17,18},{19... | collective-permute-start | bytes 786440 | tf_op jit(solution)/shard_map/ppermute | solution.py:462
  24.5 17.9 %collective-permute-start.4 = (f32[2,2,64,256]{3,2,1,0:T(8,128)S(1)}, f32[2,2,64,256]{3,2,1,0:T(8,128)S(1)}, u32[]{:S(2)}, u32[]{:S(2)}) collective-permute-start(f32[2,2,64,256]{3,2,1,0:T(8,128)S(1)} %get-tuple-element.61), channel_id=1, source_target_pairs={{0,1},{2,3},{4,5},{6,7},{8,9},{10,11},{12,13},{14,15},{16,17},{18,... | collective-permute-start | bytes 786440 | tf_op jit(solution)/shard_map/ppermute | solution.py:462
  31.3 13.5 %collective-permute-start.5 = (f32[2,2,64,256]{3,2,1,0:T(8,128)S(1)}, f32[2,2,64,256]{3,2,1,0:T(8,128)S(1)}, u32[]{:S(2)}, u32[]{:S(2)}) collective-permute-start(f32[2,2,64,256]{3,2,1,0:T(8,128)S(1)} %get-tuple-element.65), channel_id=1, source_target_pairs={{1,2},{3,4},{5,6},{7,8},{9,10},{11,12},{13,14},{15,16},{17,18},{19... | collective-permute-start | bytes 786440 | tf_op jit(solution)/shard_map/ppermute | solution.py:462
  42.9 15.8 %collective-permute-start.6 = (f32[2,2,64,256]{3,2,1,0:T(8,128)S(1)}, f32[2,2,64,256]{3,2,1,0:T(8,128)S(1)}, u32[]{:S(2)}, u32[]{:S(2)}) collective-permute-start(f32[2,2,64,256]{3,2,1,0:T(8,128)S(1)} %get-tuple-element.72), channel_id=1, source_target_pairs={{0,1},{2,3},{4,5},{6,7},{8,9},{10,11},{12,13},{14,15},{16,17},{18,... | collective-permute-start | bytes 786440 | tf_op jit(solution)/shard_map/ppermute | solution.py:462
  45.3 13.5 %collective-permute-start.7 = (f32[2,2,64,256]{3,2,1,0:T(8,128)S(1)}, f32[2,2,64,256]{3,2,1,0:T(8,128)S(1)}, u32[]{:S(2)}, u32[]{:S(2)}) collective-permute-start(f32[2,2,64,256]{3,2,1,0:T(8,128)S(1)} %get-tuple-element.74), channel_id=1, source_target_pairs={{1,2},{3,4},{5,6},{7,8},{9,10},{11,12},{13,14},{15,16},{17,18},{19... | collective-permute-start | bytes 786440 | tf_op jit(solution)/shard_map/ppermute | solution.py:462
